TPU v7x, 256 devices: a whole 4x4x8 slice. The times are simulated.
256 devices in a mesh: dp: 32 (over x, y, core), tensor: 8 (over z).
Axes of the slice: x: 4, y: 4, z: 8, core: 2. Of those that a mesh axis runs over, the one named last changes fastest.
Arguments:
- output_gradient: bfloat16 [8192, 8192], P('dp', 'tensor'), may hold values from -96 to 96
- hidden: bfloat16 [8192, 28672], P('dp', 'tensor'), may hold values from -3 to 3
- adapter_down: bfloat16 [64, 16, 28672], P('dp', None, 'tensor'), may hold values from -0.03125 to 0.03125
- adapter_up: bfloat16 [64, 16, 8192], P('dp', None, 'tensor'), may hold values from -0.0625 to 0.0625
- counts: int32 [64], replicated, may hold values from 32 to 288, as said below
- offsets: int32 [64], replicated, may hold values from 0 to 8160, as said below
- adapter_slot: int32 [64], replicated, may hold values from 0 to 63, as said below
Outputs:
- adapter_hidden_gradient: bfloat16 [8192, 28672], P('dp', 'tensor')
- adapter_down_gradient: float32 [64, 16, 28672], P('dp', None, 'tensor')
- adapter_up_gradient: float32 [64, 16, 8192], P('dp', None, 'tensor')
Inputs may be any that keep to these rules, and one draw needn't show every extreme that they name: counts sum to 8192; the last adapter has exactly 32 tokens; exactly one adapter has 288 tokens, every other fewer. Tokens are grouped by adapter in increasing order: offsets[a] is the sum of counts of the adapters before a. `adapter_slot`: every slot holds exactly one adapter; slot k lies on dp index k // 2, and any 64 // 2 adapters in a row lie on distinct dp indices.
All inputs are finite; a program needn't handle non-finite values.
Results may differ from a plain program's by a relative error of at most 0.0075.
Values may be sent and summed in bfloat16 or wider, within the bound.
No kernel may reach another device: no remote copies, remote signals or barrier semaphores. Data moves between devices by JAX's collectives and lax.ppermute only.
A program may use at most 64 MiB of HBM per device.

v0:
```python
import jax
import jax.numpy as jnp
from jax import lax
from jax.sharding import PartitionSpec as P

adapter_factor = 2.0


def selected_rows(value_entries, shard_portion, member_rows):
    shard_count = shard_portion.shape[0]
    adapter_rank = shard_portion.shape[1]
    flattened_rows = shard_portion.reshape(shard_count * adapter_rank, shard_portion.shape[2])
    rank_scores = lax.dot_general(
        value_entries, flattened_rows, (((1,), (1,)), ((), ())), preferred_element_type=jnp.float32
    )
    selected_entries = member_rows.astype(jnp.float32)
    return jnp.sum(
        rank_scores.reshape(value_entries.shape[0], shard_count, adapter_rank)
        * selected_entries[:, :, None],
        axis=1,
    )


def on_device(output_gradient, hidden, adapter_down, adapter_up, counts, offsets, adapter_slot):
    total_rows = output_gradient.shape[0]
    slots_per_worker = adapter_down.shape[0]
    adapter_rank = adapter_down.shape[1]
    hidden_size_count = hidden.shape[1]
    dp_count = lax.axis_size("dp")
    adapter_list = slots_per_worker * dp_count
    first_token = lax.axis_index("dp") * total_rows
    positions = first_token + lax.broadcasted_iota(jnp.int32, (total_rows, 1), 0)
    inside = (positions >= offsets[None, :]) & (positions < (offsets + counts)[None, :])
    slot_of_row = jnp.sum(jnp.where(inside, adapter_slot[None, :], 0), axis=1)
    columns = lax.broadcasted_iota(jnp.int32, (1, adapter_list), 1)
    member_rows = (slot_of_row[:, None] == columns).astype(jnp.bfloat16)
    up_portion = selected_rows(
        output_gradient, lax.all_gather(adapter_up, "dp", axis=0, tiled=True), member_rows
    )
    up_incoming = lax.psum(up_portion, "tensor").astype(jnp.bfloat16)
    broadcast_up = member_rows[:, :, None] * up_incoming[:, None, :]
    shard_portion = lax.all_gather(adapter_down, "dp", axis=0, tiled=True)
    shard_count = shard_portion.shape[0]
    flattened_rows = shard_portion.reshape(shard_count * adapter_rank, hidden_size_count)
    down_partial = selected_rows(hidden, shard_portion, member_rows)
    broadcast_portion = broadcast_up
    broadcast_portion = broadcast_portion.reshape(total_rows, shard_count * adapter_rank)
    gradient_running = jnp.dot(
        broadcast_portion, flattened_rows, preferred_element_type=jnp.float32
    )
    down_partial, gradient_running = (down_partial, gradient_running)
    down_incoming = lax.psum(down_partial, "tensor").astype(jnp.bfloat16)
    adapter_hidden_gradient = (adapter_factor * gradient_running).astype(jnp.bfloat16)
    broadcast_down = member_rows[:, :, None] * down_incoming[:, None, :]

    def slot_term(spread, value_entries, shard_count):
        broadcast_portion = spread
        broadcast_portion = broadcast_portion.reshape(total_rows, shard_count * adapter_rank)
        matrix_product = lax.dot_general(
            broadcast_portion,
            value_entries,
            (((0,), (0,)), ((), ())),
            preferred_element_type=jnp.float32,
        )
        return matrix_product.reshape(shard_count, adapter_rank, value_entries.shape[1])

    down_reduced = lax.psum_scatter(
        slot_term(broadcast_up, hidden, slots_per_worker * lax.axis_size("dp")).astype(
            jnp.bfloat16
        ),
        "dp",
        scatter_dimension=0,
        tiled=True,
    ).astype(jnp.float32)
    up_reduced = lax.psum_scatter(
        slot_term(broadcast_down, output_gradient, slots_per_worker * lax.axis_size("dp")).astype(
            jnp.bfloat16
        ),
        "dp",
        scatter_dimension=0,
        tiled=True,
    ).astype(jnp.float32)
    slot_grid = adapter_slot[:, None] == columns
    total_slots = jnp.sum(jnp.where(slot_grid, counts[:, None], 0), axis=0)
    scale_entries = adapter_factor / total_slots.astype(jnp.float32)
    owner_scale = lax.dynamic_slice_in_dim(
        scale_entries, lax.axis_index("dp") * slots_per_worker, slots_per_worker, 0
    )
    adapter_down_gradient = down_reduced * owner_scale[:, None, None]
    adapter_up_gradient = up_reduced * owner_scale[:, None, None]
    return (adapter_hidden_gradient, adapter_down_gradient, adapter_up_gradient)


def solution(mesh):
    placed = (
        P("dp", "tensor"),
        P("dp", "tensor"),
        P("dp", None, "tensor"),
        P("dp", None, "tensor"),
        P(),
        P(),
        P(),
    )
    return jax.shard_map(
        on_device,
        mesh=mesh,
        in_specs=placed,
        out_specs=(P("dp", "tensor"), P("dp", None, "tensor"), P("dp", None, "tensor")),
        check_vma=False,
    )
```

profile of v0, /device:TPU:1, one launch (start us, length us, event | category | flops | bytes accessed | tf_op | source)
XLA Modules:
  0.0 353.3 jit_solution(15384436137109650157)
XLA Ops:
  7.2 0.0 copy-start
  7.2 0.0 all-gather.3.cloned.1.call-start
  7.2 0.7 all-gather.3.cloned.1.call-update
  7.9 0.0 all-gather.5.cloned.1.call-start
  8.0 0.7 all-gather.5.cloned.1.call-update
  8.7 0.0 reduce-scatter.5.cloned.1.call-start
  8.7 0.7 add.27
  9.4 0.8 select_reduce_fusion
  10.2 53.1 %all-gather.3.cloned.1.call-done = bf16[64,16,1024]{2,1,0:T(8,128)(2,1)} async-done(((bf16[2,16,1024]{2,1,0:T(8,128)(2,1)}), bf16[64,16,1024]{2,1,0:T(8,128)(2,1)}) %all-gather.3.cloned.1.call-update) | async-done | bytes 2097168 | tf_op jit(solution)/shard_map/all_gather | solution.py:38
  63.3 4.2 %fusion.16 = f32[256,16]{0,1:T(8,128)S(1)} fusion(bf16[64,16,1024]{2,1,0:T(8,128)(2,1)} %all-gather.3.cloned.1.call-done, bf16[256,1024]{1,0:T(8,128)(2,1)} %param.7, f32[256,64]{0,1:T(8,128)S(1)} %get-tuple-element.6), kind=kOutput, calls=%fused_computation.13 | convolution fusion | flops 537391104 | bytes 2703360 | tf_op jit(solution)/shard_map/dot_general | solution.py:13
  67.6 0.0 copy-start.1
  67.6 53.5 %all-gather.5.cloned.1.call-done = bf16[64,16,3584]{2,1,0:T(8,128)(2,1)} async-done(((bf16[2,16,3584]{2,1,0:T(8,128)(2,1)}), bf16[64,16,3584]{2,1,0:T(8,128)(2,1)}) %all-gather.5.cloned.1.call-update) | async-done | bytes 7340048 | tf_op jit(solution)/shard_map/all_gather | solution.py:42
  121.1 0.0 copy-done
  121.1 11.0 %fusion.19 = f32[256,16]{0,1:T(8,128)S(1)} fusion(bf16[64,16,3584]{2,1,0:T(8,128)(2,1)} %all-gather.5.cloned.1.call-done, bf16[256,3584]{1,0:T(8,128)(2,1)S(1)} %copy-done, f32[256,64]{0,1:T(8,128)S(1)} %get-tuple-element.6), kind=kOutput, calls=%fused_computation.14 | convolution fusion | flops 1879568384 | bytes 9256960 | tf_op jit(solution)/shard_map/dot_general | solution.py:13
  132.0 23.2 %all-reduce = (bf16[256,16]{0,1:T(8,128)(2,1)S(1)}, bf16[256,16]{0,1:T(8,128)(2,1)S(1)}) all-reduce(f32[256,16]{0,1:T(8,128)S(1)} %fusion.16, f32[256,16]{0,1:T(8,128)S(1)} %fusion.19), channel_id=1, replica_groups=mesh['dp'=32,'tensor'=8] {'tensor'}, use_global_device_ids=true, to_apply=%region_2.3 | all-reduce | flops 8192 | bytes 49152 | tf_op jit(solution)/shard_map/psum | solution.py:40
  155.3 0.0 copy-done.1
  155.3 2.0 convolution_convert_fusion.1
  157.3 0.0 reduce-scatter.5.cloned.1.call-update
  157.3 0.0 reduce-scatter.3.cloned.1.call-start
  157.4 5.1 %convolution_convert_fusion = bf16[64,16,3584]{2,1,0:T(8,128)(2,1)} fusion(bf16[256,3584]{1,0:T(8,128)(2,1)S(1)} %copy-done, bf16[256,16]{0,1:T(8,128)(2,1)S(1)} %get-tuple-element.3, bf16[256,64]{0,1:T(8,128)(2,1)S(1)} %get-tuple-element.5), kind=kOutput, calls=%fused_computation | convolution fusion | flops 1882980352 | bytes 9216000 | tf_op jit(solution)/shard_map/dot_general | solution.py:59
  162.5 0.0 copy-start.2
  162.5 0.0 copy-start.3
  162.5 0.0 reduce-scatter.3.cloned.1.call-update
  162.5 0.6 copy-done.2
  163.2 0.0 copy-done.3
  163.2 0.1 select_reduce_fusion.1
  163.3 0.1 dynamic_slice.3
  163.4 6.4 %fusion.3 = bf16[256,3584]{1,0:T(8,128)(2,1)} fusion(bf16[64,16,3584]{2,1,0:T(8,128)(2,1)} %all-gather.5.cloned.1.call-done, bf16[256,16]{0,1:T(8,128)(2,1)S(1)} %get-tuple-element.3, bf16[256,64]{0,1:T(8,128)(2,1)S(1)} %get-tuple-element.5), kind=kOutput, calls=%fused_computation.5 | convolution fusion | flops 1881145344 | bytes 9216000 | tf_op jit(solution)/shard_map/dot_general | solution.py:48
  169.8 75.8 %reduce-scatter.5.cloned.1.call-done = bf16[2,16,1024]{2,1,0:T(8,128)(2,1)} async-done(((bf16[64,16,1024]{2,1,0:T(8,128)(2,1)}), bf16[2,16,1024]{2,1,0:T(8,128)(2,1)}) %reduce-scatter.5.cloned.1.call-update) | async-done | bytes 65552 | tf_op jit(solution)/shard_map/reduce_scatter | solution.py:75
  245.6 1.6 convert_multiply_fusion.1
  247.2 97.8 %reduce-scatter.3.cloned.1.call-done = bf16[2,16,3584]{2,1,0:T(8,128)(2,1)} async-done(((bf16[64,16,3584]{2,1,0:T(8,128)(2,1)}), bf16[2,16,3584]{2,1,0:T(8,128)(2,1)}) %reduce-scatter.3.cloned.1.call-update) | async-done | bytes 229392 | tf_op jit(solution)/shard_map/reduce_scatter | solution.py:67
  345.0 1.8 convert_multiply_fusion
  (3 shorter events, 0.0 us)
Async XLA Ops:
  7.2 113.9 %copy-start = (bf16[256,3584]{1,0:T(8,128)(2,1)S(1)}, bf16[256,3584]{1,0:T(8,128)(2,1)}, u32[]{:S(2)}) copy-start(bf16[256,3584]{1,0:T(8,128)(2,1)} %param.8) | copy-start | bytes 5505028
  7.2 56.2 %all-gather.3.cloned.1.call-start = ((), (), s32[]{:S(2)}) async-start(), calls=%async_computation.2 | async-start | bytes 2162688 | tf_op jit(solution)/shard_map/all_gather | solution.py:38
  7.9 113.1 %all-gather.5.cloned.1.call-start = ((), (), s32[]{:S(2)}) async-start(), calls=%async_computation.3 | async-start | bytes 7569408 | tf_op jit(solution)/shard_map/all_gather | solution.py:42
  8.7 236.9 %reduce-scatter.5.cloned.1.call-start = ((), (), s32[]{:S(2)}) async-start(), calls=%async_computation.5 | async-start | bytes 2162688 | tf_op jit(solution)/shard_map/reduce_scatter | solution.py:75
  67.6 87.7 %copy-start.1 = (bf16[256,1024]{1,0:T(8,128)(2,1)S(1)}, bf16[256,1024]{1,0:T(8,128)(2,1)}, u32[]{:S(2)}) copy-start(bf16[256,1024]{1,0:T(8,128)(2,1)} %param.7) | copy-start | bytes 1572868
  157.3 187.7 %reduce-scatter.3.cloned.1.call-start = ((), (), s32[]{:S(2)}) async-start(), calls=%async_computation.4 | async-start | bytes 7569408 | tf_op jit(solution)/shard_map/reduce_scatter | solution.py:67
  162.5 0.7 copy-start.2
  162.5 0.7 copy-start.3
Sparse Core Ops, SparseCore 0:
  10.5 52.7 all-gather.2
  65.9 55.1 all-gather.4
  157.5 88.0 reduce-scatter.4
  249.5 95.4 reduce-scatter.2
where the time goes:
time: 354 us; the launch traced here: 353 us
  waiting for transfers between devices  282 us (80%)
  matrix products  28.8 us (8%)
  blocking collectives  23.2 us (7%)
  between operations  13.8 us (4%)
  other arithmetic  4.95 us (1%)
    reduce_scatter x1, waiting for transfers between devices, on_device(): lax.psum_scatter(slot_term(broadcast_up, hidden, slots_per_worker * lax.a...  97.8 us
    reduce_scatter x1, waiting for transfers between devices, on_device(): lax.psum_scatter(slot_term(broadcast_down, output_gradient, slots_per_wor...  75.8 us
    all_gather x1, waiting for transfers between devices, on_device(): shard_portion = lax.all_gather(adapter_down, 'dp', axis=0, tiled=True)  53.5 us
    all_gather x1, waiting for transfers between devices, on_device(): lax.all_gather(adapter_up, 'dp', axis=0, tiled=True)  53.1 us
    psum x1, blocking collectives, on_device(): up_incoming = lax.psum(up_portion, 'tensor').astype(jnp.bfloat16)  23.2 us
    dot_general x2, matrix products, selected_rows(): lax.dot_general(value_entries, flattened_rows, (((1,), (1,)), ((), ())),...  15.2 us
    dot_general x2, matrix products, slot_term(): lax.dot_general(broadcast_portion, value_entries, (((0,), (0,)), ((), ())...  7.15 us
  transfers between devices with their start and end apart: 4, of which 4 were waited for; matrix products, arithmetic and copies ran while one was open for 5% of the time, Pallas kernels for 0%

commit v1 on v0

v1 whole, which is shorter than its diff:
```python
import jax
import jax.numpy as jnp
from jax import lax
from jax.experimental import pallas as pl
from jax.experimental.pallas import tpu as pltpu
from jax.sharding import PartitionSpec as P

adapter_factor = 2.0
BF = jnp.bfloat16
F32 = jnp.float32
I32 = jnp.int32
DP = 32
TP = 8
SLOTS = 64
RANK = 16
TOK = 256
HID = 3584
FEA = 1024
QH = HID // 4
QF = FEA // 4
ROW = QH + QF
LO = 640
HI = ROW - LO
NINE = 256
WIDE = ROW + NINE
LIMIT = 48 * 1024 * 1024


def iota(shape, axis):
    return lax.broadcasted_iota(I32, shape, axis)


def one_hot(condition):
    return jnp.where(condition, 1.0, 0.0).astype(BF)


def dot(a, b, ca=1, cb=0):
    return lax.dot_general(a, b, (((ca,), (cb,)), ((), ())), preferred_element_type=F32)


def tables_kernel(dp_ref, off_ref, cnt_ref, slot_ref, tab_ref, mine_ref, scale_ref):
    dp = dp_ref[0]
    i = iota((8, 640), 1)
    main = i < 512
    d = jnp.where(main, i >> 4, i & 31)
    k = jnp.where(main, (i >> 1) & 7, 8)
    first = d * TOK

    def count_before(a, low):
        return low + jnp.where(off_ref[a] + cnt_ref[a] <= first, 1, 0)

    wanted = lax.fori_loop(0, SLOTS, count_before, jnp.zeros((8, 640), I32), unroll=8) + k

    p = iota((8, TOK), 1)
    start = dp * TOK

    def collect(a, carry):
        tab, mine, c0, c1 = carry
        off = off_ref[a]
        slot = slot_ref[a]
        hit = (wanted == a) & (off < first + TOK)
        tab = jnp.where(hit, slot, tab)
        mine = mine + jnp.where((off > start) & (off <= start + p), 1, 0)
        c0 = jnp.where(slot == 2 * dp, cnt_ref[a], c0)
        c1 = jnp.where(slot == 2 * dp + 1, cnt_ref[a], c1)
        return tab, mine, c0, c1

    init = (jnp.full((8, 640), -1, I32), jnp.zeros((8, TOK), I32), jnp.int32(1), jnp.int32(1))
    tab, mine, c0, c1 = lax.fori_loop(0, SLOTS, collect, init, unroll=8)
    tab_ref[...] = tab
    mine_ref[...] = mine
    rows = iota((32, 128), 0)
    scale_ref[...] = adapter_factor / jnp.where(rows < 16, c0, c1).astype(F32)


def travel_order():
    i = iota((256, 256), 0)
    j = iota((256, 256), 1)
    rp, q, s, r, h = i >> 5, (i >> 3) & 3, (i >> 2) & 1, (i >> 1) & 1, i & 1
    return one_hot(j == q * 64 + h * 32 + s * 16 + rp * 2 + r)


def cut_kernel(down_ref, up_ref, out_ref):
    parts = []
    for q in range(4):
        parts.append(down_ref[:, q * QH : q * QH + LO])
        parts.append(
            jnp.concatenate(
                [
                    down_ref[:, q * QH + LO : (q + 1) * QH],
                    up_ref[:, q * QF : (q + 1) * QF],
                    jnp.zeros((32, LO - HI), BF),
                ],
                axis=1,
            )
        )
    out_ref[...] = dot(travel_order(), jnp.concatenate(parts, axis=0)).astype(BF)


def slot_hits(tab_row, part):
    n = tab_row.shape[1]
    i = iota((256, n), 0)
    c = iota((256, n), 1)
    r = c & 1 if n == 512 else c >> 5
    return one_hot(((i >> 2) == tab_row) & (((i >> 1) & 1) == r) & ((i & 1) == part))


def load_nine(ref, nine):
    nine[:512, :] = ref[:, ROW : ROW + 128].astype(F32)
    nine[512:, :] = ref[:, ROW + 128 :].astype(F32)


def store_nine(nine, ref):
    ref[:, ROW : ROW + 128] = nine[:512, :].astype(BF)
    ref[:, ROW + 128 :] = nine[512:, :].astype(BF)


def pick_kernel(tab_ref, in_ref, out_ref, nine):
    low = in_ref[...]
    high = in_ref[:, :HI]
    main = tab_ref[0:1, 0:512]
    last = tab_ref[0:1, 512:576]
    out_ref[:, :LO] = dot(slot_hits(main, 0), low, 0, 0).astype(BF)
    out_ref[:, LO:ROW] = dot(slot_hits(main, 1), high, 0, 0).astype(BF)
    x = jnp.concatenate(
        [dot(slot_hits(last, 0), low, 0, 0), dot(slot_hits(last, 1), high, 0, 0)], axis=1
    )
    nine[...] = jnp.zeros_like(nine)
    for r in range(2):
        for t in range(9):
            lane, row = divmod(r * 9 + t, 16)
            nine[pl.ds(lane * 512 + row, 32, stride=16), :] = x[
                r * 32 : (r + 1) * 32, t * 128 : (t + 1) * 128
            ]
    store_nine(nine, out_ref)


def unpack_maps(in_ref, nine, maps):
    load_nine(in_ref, nine)
    for q in range(4):
        for rp in range(8):
            at = rp * 64 + q * 16
            maps[q, rp * 16 : rp * 16 + 16, :] = in_ref[at : at + 16, :ROW]
        for t in range(9):
            both = []
            for r in range(2):
                lane, row = divmod(r * 9 + t, 16)
                both.append(nine[pl.ds(lane * 512 + q * 16 + row, 8, stride=64), :])
            maps[q, 128:144, t * 128 : (t + 1) * 128] = jnp.concatenate(both, axis=0).astype(BF)


def row_members(mine):
    i = iota((144, TOK), 0)
    k = jnp.where(i < 128, (i >> 1) & 7, 8)
    return k == mine


def rank_rows():
    o = iota((RANK, 144), 0)
    i = iota((RANK, 144), 1)
    return jnp.where(i < 128, (i & 1) * 8 + (i >> 4), i - 128) == o


def score_kernel(in_ref, hid_ref, grad_ref, mine_ref, out_ref, nine, maps):
    unpack_maps(in_ref, nine, maps)
    up = jnp.zeros((144, TOK), F32)
    down = jnp.zeros((144, TOK), F32)
    for q in range(4):
        down += dot(maps[q, :, :QH], hid_ref[:, q * QH : (q + 1) * QH], 1, 1)
        up += dot(maps[q, :, QH:], grad_ref[:, q * QF : (q + 1) * QF], 1, 1)
    member = row_members(mine_ref[0:1, :])
    fold = jnp.where(rank_rows(), 1.0, 0.0)
    both = [
        lax.dot_general(
            fold,
            jnp.where(member, part, 0.0),
            (((1,), (0,)), ((), ())),
            preferred_element_type=F32,
            precision=lax.Precision.HIGHEST,
        )
        for part in (up, down)
    ]
    block = jnp.concatenate(both, axis=0).astype(BF)
    for z in range(TP):
        out_ref[z * 32 : (z + 1) * 32, :] = block


def gradient_kernel(sig_ref, in_ref, hid_ref, grad_ref, mine_ref, hidden_out, out_ref, nine, maps):
    unpack_maps(in_ref, nine, maps)
    total = sig_ref[0:32, :].astype(F32)
    for z in range(1, TP):
        total += sig_ref[z * 32 : (z + 1) * 32, :].astype(F32)
    signal = total.astype(BF)
    member = row_members(mine_ref[0:1, :])
    fold = one_hot(rank_rows())
    up = jnp.where(member, dot(fold, signal[:RANK], 0, 0), 0.0).astype(BF)
    down = jnp.where(member, dot(fold, signal[RANK:], 0, 0), 0.0).astype(BF)
    nine[...] = jnp.zeros_like(nine)
    for q in range(4):
        hid = hid_ref[:, q * QH : (q + 1) * QH]
        hidden_out[:, q * QH : (q + 1) * QH] = (
            adapter_factor * dot(up, maps[q, :, :QH], 0, 0)
        ).astype(BF)
        sums = jnp.concatenate([dot(up, hid), dot(down, grad_ref[:, q * QF : (q + 1) * QF])], axis=1)
        for rp in range(8):
            at = rp * 64 + q * 16
            out_ref[at : at + 16, :ROW] = sums[rp * 16 : rp * 16 + 16, :].astype(BF)
        for r in range(2):
            for t in range(9):
                lane, row = divmod(r * 9 + t, 16)
                nine[pl.ds(lane * 512 + q * 16 + row, 8, stride=64), :] = sums[
                    128 + r * 8 : 136 + r * 8, t * 128 : (t + 1) * 128
                ]
    store_nine(nine, out_ref)


def reduce_kernel(tab_ref, in_ref, out_ref, nine):
    load_nine(in_ref, nine)
    rows = []
    for r in range(2):
        tiles = []
        for t in range(9):
            lane, row = divmod(r * 9 + t, 16)
            tiles.append(nine[pl.ds(lane * 512 + row, 32, stride=16), :])
        rows.append(jnp.concatenate(tiles, axis=1))
    last = jnp.concatenate(rows, axis=0).astype(BF)
    tab = tab_ref[0:1, 0:512]
    tab9 = tab_ref[0:1, 512:576]
    low = dot(slot_hits(tab, 0), in_ref[:, :LO]) + dot(slot_hits(tab9, 0), last[:, :LO])
    high = dot(slot_hits(tab, 1), in_ref[:, LO:ROW]) + dot(slot_hits(tab9, 1), last[:, LO:])
    out_ref[:, :HI] = (low[:, :HI] + high).astype(BF)
    out_ref[:, HI:] = low[:, HI:].astype(BF)


def join_kernel(scale_ref, in_ref, down_ref, up_ref):
    rows = dot(travel_order(), in_ref[...], 0, 0)
    scale = scale_ref[:, 0:1]
    for q in range(4):
        low = rows[q * 64 : q * 64 + 32, :] * scale
        high = rows[q * 64 + 32 : q * 64 + 64, :] * scale
        down_ref[:, q * QH : q * QH + LO] = low
        down_ref[:, q * QH + LO : (q + 1) * QH] = high[:, : QH - LO]
        up_ref[:, q * QF : (q + 1) * QF] = high[:, QH - LO : HI]


def call(kernel, name, outs, scratch, *args, smem=0):
    vmem = pl.BlockSpec(memory_space=pltpu.VMEM)
    scalar = pl.BlockSpec(memory_space=pltpu.SMEM)
    return pl.pallas_call(
        kernel,
        name=name,
        out_shape=[jax.ShapeDtypeStruct(s, t) for s, t in outs],
        in_specs=[scalar] * smem + [vmem] * (len(args) - smem),
        out_specs=[vmem] * len(outs),
        scratch_shapes=[pltpu.VMEM(s, t) for s, t in scratch],
        compiler_params=pltpu.CompilerParams(vmem_limit_bytes=LIMIT),
    )(*args)


def exchange(x, axis, parts):
    block = x.reshape(parts, x.shape[0] // parts, x.shape[1])
    return lax.all_to_all(block, axis, 0, 0, tiled=True).reshape(x.shape)


def on_device(output_gradient, hidden, adapter_down, adapter_up, counts, offsets, adapter_slot):
    dp = lax.axis_index("dp").astype(I32).reshape(1)
    down = adapter_down.reshape(2 * RANK, HID)
    up = adapter_up.reshape(2 * RANK, FEA)
    (cut,) = call(cut_kernel, "cut", [((256, LO), BF)], [], down, up)
    pieces = exchange(cut, "dp", DP)
    tab, mine, scale = call(
        tables_kernel,
        "tables",
        [((8, 640), I32), ((8, TOK), I32), ((32, 128), F32)],
        [],
        dp,
        offsets,
        counts,
        adapter_slot,
        smem=4,
    )
    nine = ((2 * 512, 128), F32)
    maps = ((4, 144, ROW), BF)
    (picked,) = call(pick_kernel, "pick", [((512, WIDE), BF)], [nine], tab, pieces)
    local = exchange(picked, "dp", DP)
    (partial,) = call(
        score_kernel,
        "score",
        [((TP * 32, TOK), BF)],
        [nine, maps],
        local,
        hidden,
        output_gradient,
        mine,
    )
    signals = exchange(partial, "tensor", TP)
    hidden_gradient, sums = call(
        gradient_kernel,
        "gradient",
        [((TOK, HID), BF), ((512, WIDE), BF)],
        [nine, maps],
        signals,
        local,
        hidden,
        output_gradient,
        mine,
    )
    gathered = exchange(sums, "dp", DP)
    (slot_sums,) = call(reduce_kernel, "reduce", [((256, LO), BF)], [nine], tab, gathered)
    owned = exchange(slot_sums, "dp", DP)
    down_gradient, up_gradient = call(
        join_kernel, "join", [((32, HID), F32), ((32, FEA), F32)], [], scale, owned
    )
    return (
        hidden_gradient,
        down_gradient.reshape(2, RANK, HID),
        up_gradient.reshape(2, RANK, FEA),
    )


def solution(mesh):
    placed = (
        P("dp", "tensor"),
        P("dp", "tensor"),
        P("dp", None, "tensor"),
        P("dp", None, "tensor"),
        P(),
        P(),
        P(),
    )
    return jax.shard_map(
        on_device,
        mesh=mesh,
        in_specs=placed,
        out_specs=(P("dp", "tensor"), P("dp", None, "tensor"), P("dp", None, "tensor")),
        check_vma=False,
    )
```

time: 354 us -> 109 us (0.31)
  waiting for transfers between devices: 282 us -> 6.58 us
  blocking collectives: 23.2 us -> 80.6 us
  matrix products: 28.8 us -> 0 us
  between operations: 13.8 us -> 0.71 us
  Pallas kernels: 0 us -> 8.62 us
  starting transfers between devices: 0.16 us -> 8.59 us
  other arithmetic: 4.95 us -> 0 us
    reduce_scatter x2 -> x0, waiting for transfers between devices: 174 us -> none  [the longest x1 97.8 us: on_device(): lax.psum_scatter(slot_term(broadcast_up, hidden, slots_per_worker * lax.a...]
    all_gather x2 -> x0, waiting for transfers between devices: 107 us -> none  [the longest x1 53.5 us: on_device(): shard_portion = lax.all_gather(adapter_down, 'dp', axis=0, tiled=True)]
    all_to_all x0 -> x4, blocking collectives: none -> 80.6 us  [exchange(): return lax.all_to_all(block, axis, 0, 0, tiled=True).reshape(x.shape)]
    dot_general x5 -> x0, matrix products: 28.8 us -> none  [the longest x2 15.2 us: selected_rows(): lax.dot_general(value_entries, flattened_rows, (((1,), (1,)), ((), ())),...]
    psum x1 -> x0, blocking collectives: 23.2 us -> none  [on_device(): up_incoming = lax.psum(up_portion, 'tensor').astype(jnp.bfloat16)]
    pallas_call x0 -> x7, Pallas kernels: none -> 8.62 us  [call(): pl.pallas_call(kernel, name=name, out_shape=[jax.ShapeDtypeStruct(s, t) f...]
    all_to_all x0 -> x1, starting transfers between devices: none -> 8.59 us  [exchange(): return lax.all_to_all(block, axis, 0, 0, tiled=True).reshape(x.shape)]
    all_to_all x0 -> x1, waiting for transfers between devices: none -> 6.58 us  [exchange(): return lax.all_to_all(block, axis, 0, 0, tiled=True).reshape(x.shape)]
  transfers between devices with their start and end apart: 4 -> 1, of which waited for: 4 -> 1; matrix products, arithmetic and copies ran while one was open for 5% -> 0% of each run, Pallas kernels for 0% -> 1%
where the time goes in v1:
time: 109 us
  blocking collectives  80.6 us (74%)
  Pallas kernels  8.62 us (8%)
  starting transfers between devices  8.59 us (8%)
  waiting for transfers between devices  6.58 us (6%)
  local copies, waits for them, and re-layouts  3.74 us (3%)
    all_to_all x4, blocking collectives, exchange(): return lax.all_to_all(block, axis, 0, 0, tiled=True).reshape(x.shape)  80.6 us
    pallas_call x7, Pallas kernels, call(): pl.pallas_call(kernel, name=name, out_shape=[jax.ShapeDtypeStruct(s, t) f...  8.62 us
    all_to_all x1, starting transfers between devices, exchange(): return lax.all_to_all(block, axis, 0, 0, tiled=True).reshape(x.shape)  8.59 us
    all_to_all x1, waiting for transfers between devices, exchange(): return lax.all_to_all(block, axis, 0, 0, tiled=True).reshape(x.shape)  6.58 us
    unnamed x14, local copies, waits for them, and re-layouts  3.74 us
  transfers between devices with their start and end apart: 1, of which 1 were waited for; matrix products, arithmetic and copies ran while one was open for 0% of the time, Pallas kernels for 1%

profile of v1, /device:TPU:1, one launch (start us, length us, event | category | flops | bytes accessed | tf_op | source)
XLA Modules:
  0.0 108.9 jit_solution(16989844630939781729)
XLA Ops:
  0.6 0.0 copy-start.2
  0.6 0.9 copy-done.2
  1.6 0.0 copy-start.3
  1.6 0.8 copy-done.3
  2.4 1.0 cut.1
  3.4 8.6 %all-to-all-start = ((bf16[32,8,640]{2,1,0:T(8,128)(2,1)}), bf16[32,8,640]{2,1,0:T(8,128)(2,1)S(1)}, u32[]{:S(2)}, u32[]{:S(2)}) async-start(bf16[32,8,640]{2,1,0:T(8,128)(2,1)} %bitcast.3), calls=%async_computation | async-start | bytes 655360 | tf_op jit(solution)/shard_map/all_to_all | solution.py:262
  12.0 0.0 copy-start.4
  12.0 0.6 copy-done.4
  12.7 0.0 copy-start.5
  12.7 0.7 copy-done.5
  13.3 0.0 copy-start.6
  13.3 0.7 copy-done.6
  14.0 1.1 tables.1
  15.1 6.6 %all-to-all-done = bf16[32,8,640]{2,1,0:T(8,128)(2,1)S(1)} async-done(((bf16[32,8,640]{2,1,0:T(8,128)(2,1)}), bf16[32,8,640]{2,1,0:T(8,128)(2,1)S(1)}, u32[]{:S(2)}, u32[]{:S(2)}) %all-to-all-start) | async-done | bytes 327712 | tf_op jit(solution)/shard_map/all_to_all | solution.py:262
  21.6 0.8 pick.1
  22.4 0.0 copy-start
  22.4 0.0 copy-start.1
  22.4 25.0 %all_to_all.25 = bf16[32,16,1408]{2,1,0:T(8,128)(2,1)S(1)} all-to-all(bf16[32,16,1408]{2,1,0:T(8,128)(2,1)S(1)} %bitcast.18), channel_id=1, replica_groups=mesh['dp'=32,'tensor'=8] {'dp'}, dimensions={0} | all-to-all | bytes 2883584 | tf_op jit(solution)/shard_map/all_to_all | solution.py:262
  47.5 0.0 copy-done
  47.5 0.0 copy-done.1
  47.5 1.3 %score.1 = bf16[256,256]{1,0:T(8,128)(2,1)S(1)} custom-call(bf16[512,1408]{1,0:T(8,128)(2,1)S(1)} %bitcast.15, bf16[256,3584]{1,0:T(8,128)(2,1)S(1)} %copy-done, bf16[256,1024]{1,0:T(8,128)(2,1)S(1)} %copy-done.1, s32[8,256]{1,0:T(8,128)S(1)} %get-tuple-element.11.mine_ref), custom_call_target="tpu_custom_call" | custom-call | tf_op jit(solution)/shard_map/score/pallas_call | solution.py:249
  48.8 16.6 %all_to_all.26 = bf16[8,32,256]{2,1,0:T(8,128)(2,1)S(1)} all-to-all(bf16[8,32,256]{2,1,0:T(8,128)(2,1)S(1)} %bitcast.24), channel_id=1, replica_groups=mesh['dp'=32,'tensor'=8] {'tensor'}, dimensions={0} | all-to-all | bytes 262144 | tf_op jit(solution)/shard_map/all_to_all | solution.py:262
  65.3 2.7 %gradient.1 = (bf16[256,3584]{1,0:T(8,128)(2,1)}, bf16[512,1408]{1,0:T(8,128)(2,1)S(1)}) custom-call(bf16[256,256]{1,0:T(8,128)(2,1)S(1)} %bitcast.23, bf16[512,1408]{1,0:T(8,128)(2,1)S(1)} %bitcast.16, bf16[256,3584]{1,0:T(8,128)(2,1)S(1)} %copy-done, bf16[256,1024]{1,0:T(8,128)(2,1)S(1)} %copy-done.1, s32[8,256]{1,0:T(8,128)S(1)} %get-tuple-element.11.mine_ref), custom_call_target="tpu_custom_call" | custom-call | tf_op jit(solution)/shard_map/gradient/pallas_call | solution.py:249
  68.0 26.1 %all_to_all.27 = bf16[32,16,1408]{2,1,0:T(8,128)(2,1)S(1)} all-to-all(bf16[32,16,1408]{2,1,0:T(8,128)(2,1)S(1)} %bitcast.19), channel_id=1, replica_groups=mesh['dp'=32,'tensor'=8] {'dp'}, dimensions={0} | all-to-all | bytes 2883584 | tf_op jit(solution)/shard_map/all_to_all | solution.py:262
  94.0 0.7 reduce.1
  94.8 13.0 %all_to_all.28 = bf16[32,8,640]{2,1,0:T(8,128)(2,1)S(1)} all-to-all(bf16[32,8,640]{2,1,0:T(8,128)(2,1)S(1)} %bitcast.21), channel_id=1, replica_groups=mesh['dp'=32,'tensor'=8] {'dp'}, dimensions={0} | all-to-all | bytes 655360 | tf_op jit(solution)/shard_map/all_to_all | solution.py:262
  107.7 1.2 %join.1 = (f32[32,3584]{1,0:T(8,128)}, f32[32,1024]{1,0:T(8,128)}) custom-call(f32[32,128]{1,0:T(8,128)S(1)} %get-tuple-element.13.scale_ref, bf16[256,640]{1,0:T(8,128)(2,1)S(1)} %bitcast.22), custom_call_target="tpu_custom_call" | custom-call | tf_op jit(solution)/shard_map/join/pallas_call | solution.py:249
Async XLA Ops:
  0.6 0.9 copy-start.2
  1.6 0.8 copy-start.3
  3.4 18.2 %all-to-all-start = ((bf16[32,8,640]{2,1,0:T(8,128)(2,1)}), bf16[32,8,640]{2,1,0:T(8,128)(2,1)S(1)}, u32[]{:S(2)}, u32[]{:S(2)}) async-start(bf16[32,8,640]{2,1,0:T(8,128)(2,1)} %bitcast.3), calls=%async_computation | async-start | bytes 655360 | tf_op jit(solution)/shard_map/all_to_all | solution.py:262
  12.0 0.7 copy-start.4
  12.7 0.7 copy-start.5
  13.3 0.7 copy-start.6
  22.4 25.1 %copy-start = (bf16[256,3584]{1,0:T(8,128)(2,1)S(1)}, bf16[256,3584]{1,0:T(8,128)(2,1)}, u32[]{:S(2)}) copy-start(bf16[256,3584]{1,0:T(8,128)(2,1)} %hid_ref.3) | copy-start | bytes 5505028
  22.4 25.1 %copy-start.1 = (bf16[256,1024]{1,0:T(8,128)(2,1)S(1)}, bf16[256,1024]{1,0:T(8,128)(2,1)}, u32[]{:S(2)}) copy-start(bf16[256,1024]{1,0:T(8,128)(2,1)} %grad_ref.3) | copy-start | bytes 1572868

commit v2 on v1

v2 whole, which is shorter than its diff:
```python
import jax
import jax.numpy as jnp
from jax import lax
from jax.experimental import pallas as pl
from jax.experimental.pallas import tpu as pltpu
from jax.sharding import PartitionSpec as P

adapter_factor = 2.0
BF = jnp.bfloat16
F32 = jnp.float32
I32 = jnp.int32
DP = 32
TP = 8
SLOTS = 64
RANK = 16
TOK = 256
HID = 3584
FEA = 1024
QH = HID // 4
QF = FEA // 4
ROW = QH + QF
LO = 640
HI = ROW - LO
BLOCK = 168
LIMIT = 48 * 1024 * 1024


def iota(shape, axis):
    return lax.broadcasted_iota(I32, shape, axis)


def one_hot(condition):
    return jnp.where(condition, 1.0, 0.0).astype(BF)


def dot(a, b, ca=1, cb=0):
    return lax.dot_general(a, b, (((ca,), (cb,)), ((), ())), preferred_element_type=F32)


def tables_kernel(dp_ref, off_ref, cnt_ref, slot_ref, tab_ref, mine_ref, scale_ref):
    dp = dp_ref[0]
    i = iota((8, 640), 1)
    main = i < 512
    d = jnp.where(main, i >> 4, i & 31)
    k = jnp.where(main, (i >> 1) & 7, 8)
    first = d * TOK

    def count_before(a, low):
        return low + jnp.where(off_ref[a] + cnt_ref[a] <= first, 1, 0)

    wanted = lax.fori_loop(0, SLOTS, count_before, jnp.zeros((8, 640), I32), unroll=8) + k

    p = iota((8, TOK), 1)
    start = dp * TOK

    def collect(a, carry):
        tab, mine, c0, c1 = carry
        off = off_ref[a]
        slot = slot_ref[a]
        hit = (wanted == a) & (off < first + TOK)
        tab = jnp.where(hit, slot, tab)
        mine = mine + jnp.where((off > start) & (off <= start + p), 1, 0)
        c0 = jnp.where(slot == 2 * dp, cnt_ref[a], c0)
        c1 = jnp.where(slot == 2 * dp + 1, cnt_ref[a], c1)
        return tab, mine, c0, c1

    init = (jnp.full((8, 640), -1, I32), jnp.zeros((8, TOK), I32), jnp.int32(1), jnp.int32(1))
    tab, mine, c0, c1 = lax.fori_loop(0, SLOTS, collect, init, unroll=8)
    tab_ref[...] = tab
    mine_ref[...] = mine
    rows = iota((32, 128), 0)
    scale_ref[...] = adapter_factor / jnp.where(rows < 16, c0, c1).astype(F32)


def travel_order(first, count):
    i = iota((256, count), 0)
    j = iota((256, count), 1) + first
    rp, q, s, r, h = i >> 5, (i >> 3) & 3, (i >> 2) & 1, (i >> 1) & 1, i & 1
    return one_hot(j == q * 64 + h * 32 + s * 16 + rp * 2 + r)


def cut_kernel(down_hbm, up_hbm, out_ref, down_ref, up_ref, sems):
    copies = [
        pltpu.make_async_copy(down_hbm, down_ref, sems.at[0]),
        pltpu.make_async_copy(up_hbm, up_ref, sems.at[1]),
    ]
    for copy in copies:
        copy.start()
    order = travel_order(0, 256)
    for copy in copies:
        copy.wait()
    parts = []
    for q in range(4):
        parts.append(down_ref[:, q * QH : q * QH + LO])
        parts.append(
            jnp.concatenate(
                [
                    down_ref[:, q * QH + LO : (q + 1) * QH],
                    up_ref[:, q * QF : (q + 1) * QF],
                    jnp.zeros((32, LO - HI), BF),
                ],
                axis=1,
            )
        )
    out_ref[...] = dot(order, jnp.concatenate(parts, axis=0)).astype(BF)


def slot_hits(tab_row, part):
    n = tab_row.shape[1]
    i = iota((256, n), 0)
    c = iota((256, n), 1)
    r = c & 1 if n == 512 else c >> 5
    return one_hot(((i >> 2) == tab_row) & (((i >> 1) & 1) == r) & ((i & 1) == part))


def tile_at(block, t):
    return pl.ds(block * BLOCK + t * 16, 16)


def load_nine(ref, nine):
    for b in range(DP):
        nine[b * 24 : b * 24 + 24, :] = ref[b * BLOCK + 144 : (b + 1) * BLOCK, :].astype(F32)


def store_nine(nine, ref):
    for b in range(DP):
        ref[b * BLOCK + 144 : (b + 1) * BLOCK, :] = nine[b * 24 : b * 24 + 24, :].astype(BF)


def pick_kernel(tab_ref, in_ref, out_ref, nine):
    low = in_ref[...]
    high = in_ref[:, :HI]
    main = tab_ref[0:1, 0:512]
    last = tab_ref[0:1, 512:576]
    for part, first, source in ((0, 0, low), (1, LO // 128, high)):
        rows = dot(slot_hits(main, part), source, 0, 0).astype(BF)
        ninth = dot(slot_hits(last, part), source, 0, 0)
        for t in range(source.shape[1] // 128):
            lanes = slice(t * 128, (t + 1) * 128)
            for b in range(DP):
                out_ref[tile_at(b, first + t), :] = rows[b * 16 : b * 16 + 16, lanes]
            for r in range(2):
                nine[pl.ds(r * 9 + first + t, DP, stride=24), :] = ninth[r * 32 : r * 32 + 32, lanes]
    for row in range(18, 24):
        nine[pl.ds(row, DP, stride=24), :] = jnp.zeros((DP, 128), F32)
    store_nine(nine, out_ref)


def unpack_maps(in_ref, nine, maps):
    load_nine(in_ref, nine)
    for q in range(4):
        for t in range(9):
            lanes = slice(t * 128, (t + 1) * 128)
            for rp in range(8):
                maps[q, rp * 16 : rp * 16 + 16, lanes] = in_ref[tile_at(rp * 4 + q, t), :]
            both = [nine[pl.ds(q * 24 + r * 9 + t, 8, stride=96), :] for r in range(2)]
            maps[q, 128:144, lanes] = jnp.concatenate(both, axis=0).astype(BF)


def row_members(mine):
    i = iota((144, TOK), 0)
    k = jnp.where(i < 128, (i >> 1) & 7, 8)
    return k == mine


def rank_rows():
    o = iota((RANK, 144), 0)
    i = iota((RANK, 144), 1)
    return jnp.where(i < 128, (i & 1) * 8 + (i >> 4), i - 128) == o


def score_kernel(in_ref, hid_ref, grad_ref, mine_ref, out_ref, nine, maps):
    unpack_maps(in_ref, nine, maps)
    up = jnp.zeros((144, TOK), F32)
    down = jnp.zeros((144, TOK), F32)
    for q in range(4):
        down += dot(maps[q, :, :QH], hid_ref[:, q * QH : (q + 1) * QH], 1, 1)
        up += dot(maps[q, :, QH:], grad_ref[:, q * QF : (q + 1) * QF], 1, 1)
    member = row_members(mine_ref[0:1, :])
    fold = jnp.where(rank_rows(), 1.0, 0.0)
    both = [
        lax.dot_general(
            fold,
            jnp.where(member, part, 0.0),
            (((1,), (0,)), ((), ())),
            preferred_element_type=F32,
            precision=lax.Precision.HIGHEST,
        )
        for part in (up, down)
    ]
    block = jnp.concatenate(both, axis=0).astype(BF)
    for z in range(TP):
        out_ref[z * 32 : (z + 1) * 32, :] = block


def spread_signal(sig_ref, mine_ref, first):
    total = sig_ref[first : first + RANK, :].astype(F32)
    for z in range(1, TP):
        total += sig_ref[z * 32 + first : z * 32 + first + RANK, :].astype(F32)
    rows = dot(one_hot(rank_rows()), total.astype(BF), 0, 0)
    return jnp.where(row_members(mine_ref[0:1, :]), rows, 0.0).astype(BF)


def sum_kernel(sig_ref, hid_ref, grad_ref, mine_ref, out_ref, nine):
    up = spread_signal(sig_ref, mine_ref, 0)
    down = spread_signal(sig_ref, mine_ref, RANK)
    for q in range(4):
        both = (
            (0, dot(up, hid_ref[:, q * QH : (q + 1) * QH])),
            (7, dot(down, grad_ref[:, q * QF : (q + 1) * QF])),
        )
        for first, sums in both:
            for t in range(sums.shape[1] // 128):
                tile = sums[:, t * 128 : (t + 1) * 128]
                for rp in range(8):
                    out_ref[tile_at(rp * 4 + q, first + t), :] = tile[
                        rp * 16 : rp * 16 + 16, :
                    ].astype(BF)
                for r in range(2):
                    nine[pl.ds(q * 24 + r * 9 + first + t, 8, stride=96), :] = tile[
                        128 + r * 8 : 136 + r * 8, :
                    ]
    for row in range(18, 24):
        nine[pl.ds(row, DP, stride=24), :] = jnp.zeros((DP, 128), F32)
    store_nine(nine, out_ref)


def hidden_kernel(sig_ref, in_ref, mine_ref, out_ref, nine, maps):
    unpack_maps(in_ref, nine, maps)
    up = spread_signal(sig_ref, mine_ref, 0)
    for q in range(4):
        out_ref[:, q * QH : (q + 1) * QH] = (
            adapter_factor * dot(up, maps[q, :, :QH], 0, 0)
        ).astype(BF)


def reduce_kernel(tab_ref, in_ref, out_ref, nine):
    load_nine(in_ref, nine)

    def columns(first, last):
        main, ninth = [], []
        for t in range(first, last):
            main.append(jnp.concatenate([in_ref[tile_at(b, t), :] for b in range(DP)], axis=0))
            rows = [nine[pl.ds(r * 9 + t, DP, stride=24), :] for r in range(2)]
            ninth.append(jnp.concatenate(rows, axis=0).astype(BF))
        return jnp.concatenate(main, axis=1), jnp.concatenate(ninth, axis=1)

    def summed(part, first, last):
        main, ninth = columns(first, last)
        return dot(slot_hits(tab_ref[0:1, 0:512], part), main) + dot(
            slot_hits(tab_ref[0:1, 512:576], part), ninth
        )

    low = summed(0, 0, LO // 128)
    high = summed(1, LO // 128, 9)
    out_ref[:, :HI] = (low[:, :HI] + high).astype(BF)
    out_ref[:, HI:] = low[:, HI:].astype(BF)


def join_kernel(scale_ref, in_ref, down_hbm, up_hbm, down_ref, up_ref, sems):
    scale = scale_ref[:, 0:1]
    pieces = in_ref[...]
    copies = []
    for q in range(4):
        rows = dot(travel_order(q * 64, 64), pieces, 0, 0)
        low = rows[:32, :] * scale
        high = rows[32:, :] * scale
        down_ref[:, q * QH : q * QH + LO] = low
        down_ref[:, q * QH + LO : (q + 1) * QH] = high[:, : QH - LO]
        up_ref[:, q * QF : (q + 1) * QF] = high[:, QH - LO : HI]
        lanes = pl.ds(q * QH, QH)
        copies.append(
            pltpu.make_async_copy(down_ref.at[:, lanes], down_hbm.at[:, lanes], sems.at[q])
        )
        lanes = pl.ds(q * QF, QF)
        copies.append(pltpu.make_async_copy(up_ref.at[:, lanes], up_hbm.at[:, lanes], sems.at[4 + q]))
        for copy in copies[-2:]:
            copy.start()
    for copy in copies:
        copy.wait()


def call(kernel, name, outs, scratch, *args, smem=0, hbm_in=0, hbm_out=False, limit=LIMIT):
    vmem = pl.BlockSpec(memory_space=pltpu.VMEM)
    scalar = pl.BlockSpec(memory_space=pltpu.SMEM)
    hbm = pl.BlockSpec(memory_space=pltpu.HBM)
    return pl.pallas_call(
        kernel,
        name=name,
        out_shape=[jax.ShapeDtypeStruct(s, t) for s, t in outs],
        in_specs=[scalar] * smem + [hbm] * hbm_in + [vmem] * (len(args) - smem - hbm_in),
        out_specs=[hbm if hbm_out else vmem] * len(outs),
        scratch_shapes=scratch,
        compiler_params=pltpu.CompilerParams(vmem_limit_bytes=limit),
    )(*args)


def exchange(x, axis, parts):
    block = x.reshape(parts, x.shape[0] // parts, x.shape[1])
    return lax.all_to_all(block, axis, 0, 0, tiled=True).reshape(x.shape)


def on_device(output_gradient, hidden, adapter_down, adapter_up, counts, offsets, adapter_slot):
    dp = lax.axis_index("dp").astype(I32).reshape(1)
    down = adapter_down.reshape(2 * RANK, HID)
    up = adapter_up.reshape(2 * RANK, FEA)
    (cut,) = call(
        cut_kernel,
        "cut",
        [((256, LO), BF)],
        [
            pltpu.VMEM((32, HID), BF),
            pltpu.VMEM((32, FEA), BF),
            pltpu.SemaphoreType.DMA((2,)),
        ],
        down,
        up,
        hbm_in=2,
        limit=63_400_000,
    )
    pieces = exchange(cut, "dp", DP)
    tab, mine, scale = call(
        tables_kernel,
        "tables",
        [((8, 640), I32), ((8, TOK), I32), ((32, 128), F32)],
        [],
        dp,
        offsets,
        counts,
        adapter_slot,
        smem=4,
    )
    nine = pltpu.VMEM((DP * 24, 128), F32)
    maps = pltpu.VMEM((4, 144, ROW), BF)
    block = ((DP * BLOCK, 128), BF)
    (picked,) = call(pick_kernel, "pick", [block], [nine], tab, pieces)
    local = exchange(picked, "dp", DP)
    (partial,) = call(
        score_kernel,
        "score",
        [((TP * 32, TOK), BF)],
        [nine, maps],
        local,
        hidden,
        output_gradient,
        mine,
    )
    signals = exchange(partial, "tensor", TP)
    (sums,) = call(sum_kernel, "sums", [block], [nine], signals, hidden, output_gradient, mine)
    gathered = exchange(sums, "dp", DP)
    (hidden_gradient,) = call(
        hidden_kernel, "hidden", [((TOK, HID), BF)], [nine, maps], signals, local, mine
    )
    (slot_sums,) = call(reduce_kernel, "reduce", [((256, LO), BF)], [nine], tab, gathered)
    owned = exchange(slot_sums, "dp", DP)
    down_gradient, up_gradient = call(
        join_kernel,
        "join",
        [((32, HID), F32), ((32, FEA), F32)],
        [
            pltpu.VMEM((32, HID), F32),
            pltpu.VMEM((32, FEA), F32),
            pltpu.SemaphoreType.DMA((8,)),
        ],
        scale,
        owned,
        hbm_out=True,
    )
    return (
        hidden_gradient,
        down_gradient.reshape(2, RANK, HID),
        up_gradient.reshape(2, RANK, FEA),
    )


def solution(mesh):
    placed = (
        P("dp", "tensor"),
        P("dp", "tensor"),
        P("dp", None, "tensor"),
        P("dp", None, "tensor"),
        P(),
        P(),
        P(),
    )
    return jax.shard_map(
        on_device,
        mesh=mesh,
        in_specs=placed,
        out_specs=(P("dp", "tensor"), P("dp", None, "tensor"), P("dp", None, "tensor")),
        check_vma=False,
    )
```

time: 109 us -> 106 us (0.972)
  blocking collectives: 80.6 us -> 66.3 us
  waiting for transfers between devices: 6.58 us -> 14.1 us
  starting transfers between devices: 8.59 us -> 12.3 us
  Pallas kernels: 8.62 us -> 10.6 us
  local copies, waits for them, and re-layouts: 3.74 us -> 1.97 us
    all_to_all x4 -> x3, blocking collectives: 80.6 us -> 66.3 us  [exchange(): return lax.all_to_all(block, axis, 0, 0, tiled=True).reshape(x.shape)]
    all_to_all x1 -> x2, waiting for transfers between devices: 6.58 us -> 14.1 us  [exchange(): return lax.all_to_all(block, axis, 0, 0, tiled=True).reshape(x.shape)]
    all_to_all x1 -> x2, starting transfers between devices: 8.59 us -> 12.3 us  [exchange(): return lax.all_to_all(block, axis, 0, 0, tiled=True).reshape(x.shape)]
    pallas_call x7 -> x8, Pallas kernels: 8.62 us -> 10.6 us  [call(): pl.pallas_call(kernel, name=name, out_shape=[jax.ShapeDtypeStruct(s, t) f...]
    unnamed x14 -> x10, local copies, waits for them, and re-layouts: 3.74 us -> 1.97 us
  transfers between devices with their start and end apart: 1 -> 2, of which waited for: 1 -> 2; matrix products, arithmetic and copies ran while one was open for 0% -> 0% of each run, Pallas kernels for 1% -> 3%
where the time goes in v2:
time: 106 us
  blocking collectives  66.3 us (63%)
  waiting for transfers between devices  14.1 us (13%)
  starting transfers between devices  12.3 us (12%)
  Pallas kernels  10.6 us (10%)
  local copies, waits for them, and re-layouts  1.97 us (2%)
    all_to_all x3, blocking collectives, exchange(): return lax.all_to_all(block, axis, 0, 0, tiled=True).reshape(x.shape)  66.3 us
    all_to_all x2, waiting for transfers between devices, exchange(): return lax.all_to_all(block, axis, 0, 0, tiled=True).reshape(x.shape)  14.1 us
    all_to_all x2, starting transfers between devices, exchange(): return lax.all_to_all(block, axis, 0, 0, tiled=True).reshape(x.shape)  12.3 us
    pallas_call x8, Pallas kernels, call(): pl.pallas_call(kernel, name=name, out_shape=[jax.ShapeDtypeStruct(s, t) f...  10.6 us
  transfers between devices with their start and end apart: 2, of which 2 were waited for; matrix products, arithmetic and copies ran while one was open for 0% of the time, Pallas kernels for 3%

profile of v2, /device:TPU:1, one launch (start us, length us, event | category | flops | bytes accessed | tf_op | source)
XLA Modules:
  0.0 106.0 jit_solution(16525317994241755409)
XLA Ops:
  0.6 2.0 %cut.1 = bf16[256,640]{1,0:T(8,128)(2,1)} custom-call(bf16[32,3584]{1,0:T(8,128)(2,1)} %bitcast.26, bf16[32,1024]{1,0:T(8,128)(2,1)} %bitcast.27), custom_call_target="tpu_custom_call" | custom-call | tf_op jit(solution)/shard_map/cut/pallas_call | solution.py:287
  2.6 8.6 %all-to-all-start = ((bf16[32,8,640]{2,1,0:T(8,128)(2,1)}), bf16[32,8,640]{2,1,0:T(8,128)(2,1)S(1)}, u32[]{:S(2)}, u32[]{:S(2)}) async-start(bf16[32,8,640]{2,1,0:T(8,128)(2,1)} %bitcast.25), calls=%async_computation | async-start | bytes 655360 | tf_op jit(solution)/shard_map/all_to_all | solution.py:300
  11.2 0.0 copy-start.2
  11.2 0.6 copy-done.2
  11.9 0.0 copy-start.3
  11.9 0.7 copy-done.3
  12.5 0.0 copy-start.4
  12.5 0.7 copy-done.4
  13.2 1.1 tables.1
  14.2 6.6 %all-to-all-done = bf16[32,8,640]{2,1,0:T(8,128)(2,1)S(1)} async-done(((bf16[32,8,640]{2,1,0:T(8,128)(2,1)}), bf16[32,8,640]{2,1,0:T(8,128)(2,1)S(1)}, u32[]{:S(2)}, u32[]{:S(2)}) %all-to-all-start) | async-done | bytes 327712 | tf_op jit(solution)/shard_map/all_to_all | solution.py:300
  20.8 0.7 pick.1
  21.6 0.0 copy-start
  21.6 0.0 copy-start.1
  21.6 24.4 %all_to_all.25 = bf16[32,168,128]{2,1,0:T(8,128)(2,1)S(1)} all-to-all(bf16[32,168,128]{2,1,0:T(8,128)(2,1)S(1)} %bitcast.18), channel_id=1, replica_groups=mesh['dp'=32,'tensor'=8] {'dp'}, dimensions={0} | all-to-all | bytes 2752512 | tf_op jit(solution)/shard_map/all_to_all | solution.py:300
  46.0 0.0 copy-done
  46.0 0.0 copy-done.1
  46.0 1.3 %score.1 = bf16[256,256]{1,0:T(8,128)(2,1)S(1)} custom-call(bf16[5376,128]{1,0:T(8,128)(2,1)S(1)} %bitcast.15, bf16[256,3584]{1,0:T(8,128)(2,1)S(1)} %copy-done, bf16[256,1024]{1,0:T(8,128)(2,1)S(1)} %copy-done.1, s32[8,256]{1,0:T(8,128)S(1)} %get-tuple-element.9.mine_ref), custom_call_target="tpu_custom_call" | custom-call | tf_op jit(solution)/shard_map/score/pallas_call | solution.py:287
  47.3 16.4 %all_to_all.26 = bf16[8,32,256]{2,1,0:T(8,128)(2,1)S(1)} all-to-all(bf16[8,32,256]{2,1,0:T(8,128)(2,1)S(1)} %bitcast.24), channel_id=1, replica_groups=mesh['dp'=32,'tensor'=8] {'tensor'}, dimensions={0} | all-to-all | bytes 262144 | tf_op jit(solution)/shard_map/all_to_all | solution.py:300
  63.6 0.8 sums.1
  64.5 25.6 %all_to_all.27 = bf16[32,168,128]{2,1,0:T(8,128)(2,1)S(1)} all-to-all(bf16[32,168,128]{2,1,0:T(8,128)(2,1)S(1)} %bitcast.19), channel_id=1, replica_groups=mesh['dp'=32,'tensor'=8] {'dp'}, dimensions={0} | all-to-all | bytes 2752512 | tf_op jit(solution)/shard_map/all_to_all | solution.py:300
  90.0 1.4 %reduce.1 = bf16[256,640]{1,0:T(8,128)(2,1)} custom-call(s32[8,640]{1,0:T(8,128)S(1)} %get-tuple-element.8.tab_ref, bf16[5376,128]{1,0:T(8,128)(2,1)S(1)} %bitcast.17), custom_call_target="tpu_custom_call" | custom-call | tf_op jit(solution)/shard_map/reduce/pallas_call | solution.py:287
  91.4 3.7 %all-to-all-start.4 = ((bf16[32,8,640]{2,1,0:T(8,128)(2,1)}), bf16[32,8,640]{2,1,0:T(8,128)(2,1)S(1)}, u32[]{:S(2)}, u32[]{:S(2)}) async-start(bf16[32,8,640]{2,1,0:T(8,128)(2,1)} %bitcast.11), calls=%async_computation.4 | async-start | bytes 655360 | tf_op jit(solution)/shard_map/all_to_all | solution.py:300
  95.1 2.2 %hidden.1 = bf16[256,3584]{1,0:T(8,128)(2,1)} custom-call(bf16[256,256]{1,0:T(8,128)(2,1)S(1)} %bitcast.23, bf16[5376,128]{1,0:T(8,128)(2,1)S(1)} %bitcast.16, s32[8,256]{1,0:T(8,128)S(1)} %get-tuple-element.9.mine_ref), custom_call_target="tpu_custom_call" | custom-call | tf_op jit(solution)/shard_map/hidden/pallas_call | solution.py:287
  97.3 7.5 %all-to-all-done.4 = bf16[32,8,640]{2,1,0:T(8,128)(2,1)S(1)} async-done(((bf16[32,8,640]{2,1,0:T(8,128)(2,1)}), bf16[32,8,640]{2,1,0:T(8,128)(2,1)S(1)}, u32[]{:S(2)}, u32[]{:S(2)}) %all-to-all-start.4) | async-done | bytes 327712 | tf_op jit(solution)/shard_map/all_to_all | solution.py:300
  104.8 1.2 %join.1 = (f32[32,3584]{1,0:T(8,128)}, f32[32,1024]{1,0:T(8,128)}) custom-call(f32[32,128]{1,0:T(8,128)S(1)} %get-tuple-element.10.scale_ref, bf16[256,640]{1,0:T(8,128)(2,1)S(1)} %bitcast.20), custom_call_target="tpu_custom_call" | custom-call | tf_op jit(solution)/shard_map/join/pallas_call | solution.py:287
Async XLA Ops:
  2.6 18.2 %all-to-all-start = ((bf16[32,8,640]{2,1,0:T(8,128)(2,1)}), bf16[32,8,640]{2,1,0:T(8,128)(2,1)S(1)}, u32[]{:S(2)}, u32[]{:S(2)}) async-start(bf16[32,8,640]{2,1,0:T(8,128)(2,1)} %bitcast.25), calls=%async_computation | async-start | bytes 655360 | tf_op jit(solution)/shard_map/all_to_all | solution.py:300
  11.2 0.7 copy-start.2
  11.9 0.7 copy-start.3
  12.5 0.7 copy-start.4
  21.6 24.4 %copy-start = (bf16[256,3584]{1,0:T(8,128)(2,1)S(1)}, bf16[256,3584]{1,0:T(8,128)(2,1)}, u32[]{:S(2)}) copy-start(bf16[256,3584]{1,0:T(8,128)(2,1)} %hid_ref.3) | copy-start | bytes 5505028
  21.6 24.4 %copy-start.1 = (bf16[256,1024]{1,0:T(8,128)(2,1)S(1)}, bf16[256,1024]{1,0:T(8,128)(2,1)}, u32[]{:S(2)}) copy-start(bf16[256,1024]{1,0:T(8,128)(2,1)} %grad_ref.3) | copy-start | bytes 1572868
  91.4 13.4 %all-to-all-start.4 = ((bf16[32,8,640]{2,1,0:T(8,128)(2,1)}), bf16[32,8,640]{2,1,0:T(8,128)(2,1)S(1)}, u32[]{:S(2)}, u32[]{:S(2)}) async-start(bf16[32,8,640]{2,1,0:T(8,128)(2,1)} %bitcast.11), calls=%async_computation.4 | async-start | bytes 655360 | tf_op jit(solution)/shard_map/all_to_all | solution.py:300

commit v3 on v2

v3 whole, which is shorter than its diff:
```python
import jax
import jax.numpy as jnp
from jax import lax
from jax.experimental import pallas as pl
from jax.experimental.pallas import tpu as pltpu
from jax.sharding import PartitionSpec as P

adapter_factor = 2.0
BF = jnp.bfloat16
F32 = jnp.float32
I32 = jnp.int32
DP = 32
TP = 8
SLOTS = 64
RANK = 16
TOK = 256
HID = 3584
FEA = 1024
QH = HID // 4
QF = FEA // 4
ROW = QH + QF
LO = 640
HI = ROW - LO
EXTRA = 32
SIG = 96
LIMIT = 16 * 1024 * 1024


def iota(shape, axis):
    return lax.broadcasted_iota(I32, shape, axis)


def one_hot(condition):
    return jnp.where(condition, 1.0, 0.0).astype(BF)


def dot(a, b, ca=1, cb=0):
    return lax.dot_general(a, b, (((ca,), (cb,)), ((), ())), preferred_element_type=F32)


def tables_kernel(dp_ref, off_ref, cnt_ref, slot_ref, tab_ref, mine_ref, scale_ref):
    dp = dp_ref[0]
    i = iota((8, 512), 1)
    first = (i >> 4) * TOK

    def count_before(a, low):
        return low + jnp.where(off_ref[a] + cnt_ref[a] <= first, 1, 0)

    wanted = lax.fori_loop(0, SLOTS, count_before, jnp.zeros((8, 512), I32), unroll=8)
    wanted += (i >> 1) & 7

    p = iota((8, 384), 1)
    own = p < TOK
    start = (dp - jnp.where(own, 0, 1)) * TOK
    at = start + jnp.where(own, p, p - EXTRA)

    def collect(a, carry):
        tab, mine, c0, c1 = carry
        off = off_ref[a]
        slot = slot_ref[a]
        hit = (wanted == a) & (off < first + TOK)
        tab = jnp.where(hit, slot, tab)
        mine = mine + jnp.where((off > start) & (off <= at), 1, 0)
        c0 = jnp.where(slot == 2 * dp, cnt_ref[a], c0)
        c1 = jnp.where(slot == 2 * dp + 1, cnt_ref[a], c1)
        return tab, mine, c0, c1

    init = (jnp.full((8, 512), -1, I32), jnp.zeros((8, 384), I32), jnp.int32(1), jnp.int32(1))
    tab, mine, c0, c1 = lax.fori_loop(0, SLOTS, collect, init, unroll=8)
    tab_ref[...] = tab
    extra = (p < TOK + EXTRA) & (mine == 8)
    mine_ref[...] = jnp.where(own, mine, jnp.where(extra, 0, -1))
    rows = iota((32, 128), 0)
    scale_ref[...] = adapter_factor / jnp.where(rows < 16, c0, c1).astype(F32)


def travel_order(first, count):
    i = iota((256, count), 0)
    j = iota((256, count), 1) + first
    rp, q, s, r, h = i >> 5, (i >> 3) & 3, (i >> 2) & 1, (i >> 1) & 1, i & 1
    return one_hot(j == q * 64 + h * 32 + s * 16 + rp * 2 + r)


def cut_kernel(down_hbm, up_hbm, out_ref, down_ref, up_ref, sems):
    copies = [
        pltpu.make_async_copy(down_hbm, down_ref, sems.at[0]),
        pltpu.make_async_copy(up_hbm, up_ref, sems.at[1]),
    ]
    for copy in copies:
        copy.start()
    order = travel_order(0, 256)
    for copy in copies:
        copy.wait()
    parts = []
    for q in range(4):
        parts.append(down_ref[:, q * QH : q * QH + LO])
        parts.append(
            jnp.concatenate(
                [
                    down_ref[:, q * QH + LO : (q + 1) * QH],
                    up_ref[:, q * QF : (q + 1) * QF],
                    jnp.zeros((32, LO - HI), BF),
                ],
                axis=1,
            )
        )
    out_ref[...] = dot(order, jnp.concatenate(parts, axis=0)).astype(BF)


def slot_hits(tab_ref, part):
    i = iota((256, 512), 0)
    r = iota((256, 512), 1) & 1
    return one_hot(((i >> 2) == tab_ref[0:1, :]) & (((i >> 1) & 1) == r) & ((i & 1) == part))


def pick_kernel(tab_ref, in_ref, after_ref, out_ref):
    out_ref[:, :LO] = dot(slot_hits(tab_ref, 0), in_ref[...], 0, 0).astype(BF)
    out_ref[:, LO:] = dot(slot_hits(tab_ref, 1), in_ref[:, :HI], 0, 0).astype(BF)


def quarter(ref, q, lanes):
    tiles = [ref[(rp * 4 + q) * 16 : (rp * 4 + q) * 16 + 16, lanes] for rp in range(8)]
    return jnp.concatenate(tiles, axis=0)


def members(mine_ref):
    k = (iota((128, TOK), 0) >> 1) & 7
    own = k == mine_ref[0:1, :TOK]
    k = (iota((128, EXTRA), 0) >> 1) & 7
    return own, k == mine_ref[0:1, TOK : TOK + EXTRA]


def rank_rows():
    o = iota((RANK, 128), 0)
    i = iota((RANK, 128), 1)
    return (i & 1) * 8 + (i >> 4) == o


def score_kernel(in_ref, hid_ref, grad_ref, extra_ref, mine_ref, out_ref):
    own_up = jnp.zeros((128, TOK), F32)
    own_down = jnp.zeros((128, TOK), F32)
    extra_up = jnp.zeros((128, EXTRA), F32)
    extra_down = jnp.zeros((128, EXTRA), F32)
    for q in range(4):
        lanes = slice(q * QH, (q + 1) * QH)
        part = quarter(in_ref, q, slice(0, QH))
        own_down += dot(part, hid_ref[:, lanes], 1, 1)
        extra_down += dot(part, extra_ref[:, lanes], 1, 1)
        lanes = slice(q * QF, (q + 1) * QF)
        part = quarter(in_ref, q, slice(QH, ROW))
        own_up += dot(part, grad_ref[:, lanes], 1, 1)
        extra_up += dot(part, extra_ref[:, HID + q * QF : HID + (q + 1) * QF], 1, 1)
    own, extra = members(mine_ref)
    fold = jnp.where(rank_rows(), 1.0, 0.0)

    def folded(member, up, down):
        return [
            lax.dot_general(
                fold,
                jnp.where(member, part, 0.0),
                (((1,), (0,)), ((), ())),
                preferred_element_type=F32,
                precision=lax.Precision.HIGHEST,
            )
            for part in (up, down)
        ]

    block = jnp.concatenate(folded(own, own_up, own_down), axis=0).astype(BF)
    tail = jnp.concatenate(folded(extra, extra_up, extra_down), axis=0).astype(BF)
    tail = jnp.concatenate([tail, jnp.zeros((32, 128 - EXTRA), BF)], axis=1)
    block = jnp.concatenate([block[:, :128], block[:, 128:], tail], axis=0)
    for z in range(TP):
        out_ref[z * SIG : (z + 1) * SIG, :] = block


def spread_signal(sig_ref, mine_ref, first):
    parts = []
    for base in (0, 32, 64):
        at = base + first
        total = sig_ref[at : at + RANK, :].astype(F32)
        for z in range(1, TP):
            total += sig_ref[z * SIG + at : z * SIG + at + RANK, :].astype(F32)
        parts.append(total.astype(BF))
    own, extra = members(mine_ref)
    fold = one_hot(rank_rows())
    rows = dot(fold, jnp.concatenate(parts[:2], axis=1), 0, 0)
    tail = dot(fold, parts[2], 0, 0)[:, :EXTRA]
    return jnp.where(own, rows, 0.0).astype(BF), jnp.where(extra, tail, 0.0).astype(BF)


def sum_kernel(sig_ref, hid_ref, grad_ref, extra_ref, mine_ref, out_ref):
    up, up_extra = spread_signal(sig_ref, mine_ref, 0)
    down, down_extra = spread_signal(sig_ref, mine_ref, RANK)
    for q in range(4):
        lanes = slice(q * QH, (q + 1) * QH)
        sums = dot(up, hid_ref[:, lanes]) + dot(up_extra, extra_ref[:, lanes])
        for rp in range(8):
            at = (rp * 4 + q) * 16
            out_ref[at : at + 16, :QH] = sums[rp * 16 : rp * 16 + 16, :].astype(BF)
        sums = dot(down, grad_ref[:, q * QF : (q + 1) * QF]) + dot(
            down_extra, extra_ref[:, HID + q * QF : HID + (q + 1) * QF]
        )
        for rp in range(8):
            at = (rp * 4 + q) * 16
            out_ref[at : at + 16, QH:] = sums[rp * 16 : rp * 16 + 16, :].astype(BF)


def extra_kernel(sig_ref, in_ref, mine_ref, out_ref):
    _, up = spread_signal(sig_ref, mine_ref, 0)
    for q in range(4):
        out_ref[:, q * QH : (q + 1) * QH] = (
            adapter_factor * dot(up, quarter(in_ref, q, slice(0, QH)), 0, 0)
        ).astype(BF)


def hidden_kernel(sig_ref, in_ref, mine_ref, back_ref, out_ref):
    up, _ = spread_signal(sig_ref, mine_ref, 0)
    cut = TOK - EXTRA
    for q in range(4):
        lanes = slice(q * QH, (q + 1) * QH)
        rows = adapter_factor * dot(up, quarter(in_ref, q, slice(0, QH)), 0, 0)
        out_ref[:cut, lanes] = rows[:cut, :].astype(BF)
        out_ref[cut:, lanes] = (rows[cut:, :] + back_ref[:, lanes].astype(F32)).astype(BF)


def reduce_kernel(tab_ref, in_ref, out_ref):
    low = dot(slot_hits(tab_ref, 0), in_ref[:, :LO])
    high = dot(slot_hits(tab_ref, 1), in_ref[:, LO:])
    out_ref[:, :HI] = (low[:, :HI] + high).astype(BF)
    out_ref[:, HI:] = low[:, HI:].astype(BF)


def join_kernel(scale_ref, in_ref, down_hbm, up_hbm, down_ref, up_ref, sems):
    scale = scale_ref[:, 0:1]
    pieces = in_ref[...]
    copies = []
    for q in range(4):
        rows = dot(travel_order(q * 64, 64), pieces, 0, 0)
        low = rows[:32, :] * scale
        high = rows[32:, :] * scale
        down_ref[:, q * QH : q * QH + LO] = low
        down_ref[:, q * QH + LO : (q + 1) * QH] = high[:, : QH - LO]
        up_ref[:, q * QF : (q + 1) * QF] = high[:, QH - LO : HI]
        lanes = pl.ds(q * QH, QH)
        copies.append(
            pltpu.make_async_copy(down_ref.at[:, lanes], down_hbm.at[:, lanes], sems.at[q])
        )
        lanes = pl.ds(q * QF, QF)
        copies.append(pltpu.make_async_copy(up_ref.at[:, lanes], up_hbm.at[:, lanes], sems.at[4 + q]))
        for copy in copies[-2:]:
            copy.start()
    for copy in copies:
        copy.wait()


def call(kernel, name, outs, scratch, *args, smem=0, hbm_in=0, any_in=0, hbm_out=False, limit=LIMIT):
    vmem = pl.BlockSpec(memory_space=pltpu.VMEM)
    scalar = pl.BlockSpec(memory_space=pltpu.SMEM)
    hbm = pl.BlockSpec(memory_space=pltpu.HBM)
    return pl.pallas_call(
        kernel,
        name=name,
        out_shape=[jax.ShapeDtypeStruct(s, t) for s, t in outs],
        in_specs=[scalar] * smem + [hbm] * hbm_in
        + [vmem] * (len(args) - smem - hbm_in - any_in)
        + [pl.BlockSpec(memory_space=pl.ANY)] * any_in,
        out_specs=[hbm if hbm_out else vmem] * len(outs),
        scratch_shapes=scratch,
        compiler_params=pltpu.CompilerParams(vmem_limit_bytes=limit),
    )(*args)


def exchange(x, axis, parts):
    block = x.reshape(parts, x.shape[0] // parts, x.shape[1])
    return lax.all_to_all(block, axis, 0, 0, tiled=True).reshape(x.shape)


def on_device(output_gradient, hidden, adapter_down, adapter_up, counts, offsets, adapter_slot):
    dp = lax.axis_index("dp").astype(I32).reshape(1)
    onward = [(i, i + 1) for i in range(DP - 1)]
    backward = [(i + 1, i) for i in range(DP - 1)]
    last = jnp.concatenate([hidden[TOK - EXTRA :], output_gradient[TOK - EXTRA :]], axis=1)
    extra = lax.ppermute(last, "dp", onward)
    down = adapter_down.reshape(2 * RANK, HID)
    up = adapter_up.reshape(2 * RANK, FEA)
    (cut,) = call(
        cut_kernel,
        "cut",
        [((256, LO), BF)],
        [
            pltpu.VMEM((32, HID), BF),
            pltpu.VMEM((32, FEA), BF),
            pltpu.SemaphoreType.DMA((2,)),
        ],
        down,
        up,
        hbm_in=2,
        limit=63_400_000,
    )
    pieces = exchange(cut, "dp", DP)
    tab, mine, scale = call(
        tables_kernel,
        "tables",
        [((8, 512), I32), ((8, 384), I32), ((32, 128), F32)],
        [],
        dp,
        offsets,
        counts,
        adapter_slot,
        smem=4,
    )
    block = ((512, ROW), BF)
    (picked,) = call(pick_kernel, "pick", [block], [], tab, pieces, extra, any_in=1)
    local = exchange(picked, "dp", DP)
    tokens = (hidden, output_gradient, extra, mine)
    (partial,) = call(score_kernel, "score", [((TP * SIG, 128), BF)], [], local, *tokens)
    signals = exchange(partial, "tensor", TP)
    (sums,) = call(sum_kernel, "sums", [block], [], signals, *tokens)
    gathered = exchange(sums, "dp", DP)
    (extra_gradient,) = call(
        extra_kernel, "extra", [((EXTRA, HID), BF)], [], signals, local, mine
    )
    back = lax.ppermute(extra_gradient, "dp", backward)
    (hidden_gradient,) = call(
        hidden_kernel, "hidden", [((TOK, HID), BF)], [], signals, local, mine, back
    )
    (slot_sums,) = call(reduce_kernel, "reduce", [((256, LO), BF)], [], tab, gathered)
    owned = exchange(slot_sums, "dp", DP)
    down_gradient, up_gradient = call(
        join_kernel,
        "join",
        [((32, HID), F32), ((32, FEA), F32)],
        [
            pltpu.VMEM((32, HID), F32),
            pltpu.VMEM((32, FEA), F32),
            pltpu.SemaphoreType.DMA((8,)),
        ],
        scale,
        owned,
        hbm_out=True,
    )
    return (
        hidden_gradient,
        down_gradient.reshape(2, RANK, HID),
        up_gradient.reshape(2, RANK, FEA),
    )


def solution(mesh):
    placed = (
        P("dp", "tensor"),
        P("dp", "tensor"),
        P("dp", None, "tensor"),
        P("dp", None, "tensor"),
        P(),
        P(),
        P(),
    )
    return jax.shard_map(
        on_device,
        mesh=mesh,
        in_specs=placed,
        out_specs=(P("dp", "tensor"), P("dp", None, "tensor"), P("dp", None, "tensor")),
        check_vma=False,
    )
```

time: 106 us -> 109 us (1.028)
  starting transfers between devices: 12.3 us -> 18.3 us
  waiting for transfers between devices: 14.1 us -> 11.7 us
  local copies, waits for them, and re-layouts: 1.97 us -> 0.04 us
    all_to_all x2, waiting for transfers between devices: 14.1 us -> 1.11 us  [exchange(): return lax.all_to_all(block, axis, 0, 0, tiled=True).reshape(x.shape)]
    ppermute x0 -> x2, waiting for transfers between devices: none -> 10.6 us  [the longest x1 6.71 us: on_device(): back = lax.ppermute(extra_gradient, 'dp', backward)]
    ppermute x0 -> x2, starting transfers between devices: none -> 5.8 us  [the longest x1 3.54 us: on_device(): extra = lax.ppermute(last, 'dp', onward)]
    unnamed x10, local copies, waits for them, and re-layouts: 1.97 us -> 0.03 us
    pallas_call x8 -> x9, Pallas kernels: 10.6 us -> 11.2 us  [call(): pl.pallas_call(kernel, name=name, out_shape=[jax.ShapeDtypeStruct(s, t) f...]
  transfers between devices with their start and end apart: 2 -> 4, of which waited for: 2 -> 3; matrix products, arithmetic and copies ran while one was open for 0% -> 0% of each run, Pallas kernels for 3% -> 3%
where the time goes in v3:
time: 109 us
  blocking collectives  66.5 us (61%)
  starting transfers between devices  18.3 us (17%)
  waiting for transfers between devices  11.7 us (11%)
  Pallas kernels  11.2 us (10%)
    all_to_all x3, blocking collectives, exchange(): return lax.all_to_all(block, axis, 0, 0, tiled=True).reshape(x.shape)  66.5 us
    all_to_all x2, starting transfers between devices, exchange(): return lax.all_to_all(block, axis, 0, 0, tiled=True).reshape(x.shape)  12.5 us
    pallas_call x9, Pallas kernels, call(): pl.pallas_call(kernel, name=name, out_shape=[jax.ShapeDtypeStruct(s, t) f...  11.2 us
    ppermute x1, waiting for transfers between devices, on_device(): back = lax.ppermute(extra_gradient, 'dp', backward)  6.71 us
    ppermute x1, waiting for transfers between devices, on_device(): extra = lax.ppermute(last, 'dp', onward)  3.85 us
    ppermute x1, starting transfers between devices, on_device(): extra = lax.ppermute(last, 'dp', onward)  3.54 us
    ppermute x1, starting transfers between devices, on_device(): back = lax.ppermute(extra_gradient, 'dp', backward)  2.26 us
  transfers between devices with their start and end apart: 4, of which 3 were waited for; matrix products, arithmetic and copies ran while one was open for 0% of the time, Pallas kernels for 3%

profile of v3, /device:TPU:1, one launch (start us, length us, event | category | flops | bytes accessed | tf_op | source)
XLA Modules:
  0.0 108.5 jit_solution(8021324509320136810)
XLA Ops:
  0.6 0.0 slice-start.1
  0.6 0.0 slice-start
  0.7 0.0 copy-start.2
  0.7 0.0 copy-start.3
  0.7 0.0 copy-start.4
  0.7 2.0 %cut.1 = bf16[256,640]{1,0:T(8,128)(2,1)} custom-call(bf16[32,3584]{1,0:T(8,128)(2,1)} %bitcast.28, bf16[32,1024]{1,0:T(8,128)(2,1)} %bitcast.29), custom_call_target="tpu_custom_call" | custom-call | tf_op jit(solution)/shard_map/cut/pallas_call | solution.py:260
  2.7 8.6 %all-to-all-start = ((bf16[32,8,640]{2,1,0:T(8,128)(2,1)}), bf16[32,8,640]{2,1,0:T(8,128)(2,1)S(1)}, u32[]{:S(2)}, u32[]{:S(2)}) async-start(bf16[32,8,640]{2,1,0:T(8,128)(2,1)} %bitcast.27), calls=%async_computation | async-start | bytes 655360 | tf_op jit(solution)/shard_map/all_to_all | solution.py:275
  11.3 0.0 slice-done.1
  11.3 0.0 slice-done
  11.4 3.5 %collective-permute-start = (bf16[32,4608]{1,0:T(8,128)(2,1)S(1)}, bf16[32,4608]{1,0:T(8,128)(2,1)S(1)}, u32[]{:S(2)}, u32[]{:S(2)}) collective-permute-start(bf16[32,4608]{1,0:T(8,128)(2,1)S(1)} %pad_maximum_fusion), channel_id=1, source_target_pairs={{0,8},{8,16},{16,24},{24,32},{32,40},{40,48},{48,56},{56,64},{64,7... | collective-permute-start | bytes 884744 | tf_op jit(solution)/shard_map/ppermute | solution.py:283
  14.9 0.0 copy-done.2
  14.9 0.0 copy-done.3
  15.0 1.0 tables.1
  16.0 3.8 %collective-permute-done.after_ref.extra_ref = bf16[32,4608]{1,0:T(8,128)(2,1)S(1)} collective-permute-done((bf16[32,4608]{1,0:T(8,128)(2,1)S(1)}, bf16[32,4608]{1,0:T(8,128)(2,1)S(1)}, u32[]{:S(2)}, u32[]{:S(2)}) %collective-permute-start) | collective-permute-done | bytes 294944 | tf_op jit(solution)/shard_map/ppermute | solution.py:283
  19.8 1.1 %all-to-all-done = bf16[32,8,640]{2,1,0:T(8,128)(2,1)S(1)} async-done(((bf16[32,8,640]{2,1,0:T(8,128)(2,1)}), bf16[32,8,640]{2,1,0:T(8,128)(2,1)S(1)}, u32[]{:S(2)}, u32[]{:S(2)}) %all-to-all-start) | async-done | bytes 327712 | tf_op jit(solution)/shard_map/all_to_all | solution.py:275
  20.9 0.6 pick.1
  21.6 0.0 copy-start
  21.6 0.0 copy-start.1
  21.6 25.1 %all_to_all.25 = bf16[32,16,1152]{2,1,0:T(8,128)(2,1)S(1)} all-to-all(bf16[32,16,1152]{2,1,0:T(8,128)(2,1)S(1)} %bitcast.20), channel_id=1, replica_groups=mesh['dp'=32,'tensor'=8] {'dp'}, dimensions={0} | all-to-all | bytes 2359296 | tf_op jit(solution)/shard_map/all_to_all | solution.py:275
  46.7 0.0 copy-done.1
  46.7 1.5 %score.1 = bf16[768,128]{1,0:T(8,128)(2,1)S(1)} custom-call(bf16[512,1152]{1,0:T(8,128)(2,1)S(1)} %bitcast.15, bf16[256,3584]{1,0:T(8,128)(2,1)S(1)} %copy-done, bf16[256,1024]{1,0:T(8,128)(2,1)S(1)} %copy-done.1, bf16[32,4608]{1,0:T(8,128)(2,1)S(1)} %collective-permute-done.after_ref.extra_ref, s32[8,384]{1,0:T(8,128)S(1)} %get-tuple-element.9.mine_ref), custom_call_target="tpu_custom_call" | custom-call | tf_op jit(solution)/shard_map/score/pallas_call | solution.py:260
  48.2 17.4 %all_to_all.26 = bf16[8,96,128]{2,1,0:T(8,128)(2,1)S(1)} all-to-all(bf16[8,96,128]{2,1,0:T(8,128)(2,1)S(1)} %bitcast.26), channel_id=1, replica_groups=mesh['dp'=32,'tensor'=8] {'tensor'}, dimensions={0} | all-to-all | bytes 393216 | tf_op jit(solution)/shard_map/all_to_all | solution.py:275
  65.6 1.1 %sums.1 = bf16[512,1152]{1,0:T(8,128)(2,1)S(1)} custom-call(bf16[768,128]{1,0:T(8,128)(2,1)S(1)} %bitcast.21, bf16[256,3584]{1,0:T(8,128)(2,1)S(1)} %copy-done, bf16[256,1024]{1,0:T(8,128)(2,1)S(1)} %copy-done.1, bf16[32,4608]{1,0:T(8,128)(2,1)S(1)} %collective-permute-done.after_ref.extra_ref, s32[8,384]{1,0:T(8,128)S(1)} %get-tuple-element.9.mine_ref), custom_call_target="tpu_custom_call" | custom-call | tf_op jit(solution)/shard_map/sums/pallas_call | solution.py:260
  66.7 23.9 %all_to_all.27 = bf16[32,16,1152]{2,1,0:T(8,128)(2,1)S(1)} all-to-all(bf16[32,16,1152]{2,1,0:T(8,128)(2,1)S(1)} %bitcast.18), channel_id=1, replica_groups=mesh['dp'=32,'tensor'=8] {'dp'}, dimensions={0} | all-to-all | bytes 2359296 | tf_op jit(solution)/shard_map/all_to_all | solution.py:275
  90.6 1.3 %reduce.1 = bf16[256,640]{1,0:T(8,128)(2,1)} custom-call(s32[8,512]{1,0:T(8,128)S(1)} %get-tuple-element.8.tab_ref, bf16[512,1152]{1,0:T(8,128)(2,1)S(1)} %bitcast.19), custom_call_target="tpu_custom_call" | custom-call | tf_op jit(solution)/shard_map/reduce/pallas_call | solution.py:260
  91.9 3.9 %all-to-all-start.4 = ((bf16[32,8,640]{2,1,0:T(8,128)(2,1)}), bf16[32,8,640]{2,1,0:T(8,128)(2,1)S(1)}, u32[]{:S(2)}, u32[]{:S(2)}) async-start(bf16[32,8,640]{2,1,0:T(8,128)(2,1)} %bitcast.11), calls=%async_computation.4 | async-start | bytes 655360 | tf_op jit(solution)/shard_map/all_to_all | solution.py:275
  95.8 0.5 extra.1
  96.3 2.3 %collective-permute-start.1 = (bf16[32,3584]{1,0:T(8,128)(2,1)S(1)}, bf16[32,3584]{1,0:T(8,128)(2,1)S(1)}, u32[]{:S(2)}, u32[]{:S(2)}) collective-permute-start(bf16[32,3584]{1,0:T(8,128)(2,1)S(1)} %extra.1), channel_id=1, source_target_pairs={{8,0},{16,8},{24,16},{32,24},{40,32},{48,40},{56,48},{64,56},{72,6... | collective-permute-start | bytes 688136 | tf_op jit(solution)/shard_map/ppermute | solution.py:323
  98.6 6.7 %collective-permute-done.1.back_ref = bf16[32,3584]{1,0:T(8,128)(2,1)S(1)} collective-permute-done((bf16[32,3584]{1,0:T(8,128)(2,1)S(1)}, bf16[32,3584]{1,0:T(8,128)(2,1)S(1)}, u32[]{:S(2)}, u32[]{:S(2)}) %collective-permute-start.1) | collective-permute-done | bytes 229408 | tf_op jit(solution)/shard_map/ppermute | solution.py:323
  105.3 2.1 %hidden.1 = bf16[256,3584]{1,0:T(8,128)(2,1)} custom-call(bf16[768,128]{1,0:T(8,128)(2,1)S(1)} %bitcast.23, bf16[512,1152]{1,0:T(8,128)(2,1)S(1)} %bitcast.17, s32[8,384]{1,0:T(8,128)S(1)} %get-tuple-element.9.mine_ref, bf16[32,3584]{1,0:T(8,128)(2,1)S(1)} %collective-permute-done.1.back_ref), custom_call_target="tpu_custom_call" | custom-call | tf_op jit(solution)/shard_map/hidden/pallas_call | solution.py:260
  107.4 0.0 all-to-all-done.4
  107.4 1.2 %join.1 = (f32[32,3584]{1,0:T(8,128)}, f32[32,1024]{1,0:T(8,128)}) custom-call(f32[32,128]{1,0:T(8,128)S(1)} %get-tuple-element.10.scale_ref, bf16[256,640]{1,0:T(8,128)(2,1)S(1)} %bitcast.25), custom_call_target="tpu_custom_call" | custom-call | tf_op jit(solution)/shard_map/join/pallas_call | solution.py:260
  (3 shorter events, 0.0 us)
Async XLA Ops:
  0.6 10.7 %slice-start.1 = ((bf16[256,1024]{1,0:T(8,128)(2,1)}), bf16[32,1024]{1,0:T(8,128)(2,1)S(1)}, s32[]{:S(2)}) async-start(bf16[256,1024]{1,0:T(8,128)(2,1)} %grad_ref.3), calls=%async_computation.6 | async-start | bytes 131072 | tf_op jit(solution)/shard_map/slice | solution.py:282
  0.6 10.7 %slice-start = ((bf16[256,3584]{1,0:T(8,128)(2,1)}), bf16[32,3584]{1,0:T(8,128)(2,1)S(1)}, s32[]{:S(2)}) async-start(bf16[256,3584]{1,0:T(8,128)(2,1)} %hid_ref.3), calls=%async_computation.5 | async-start | bytes 458752 | tf_op jit(solution)/shard_map/slice | solution.py:282
  0.7 14.3 %copy-start.2 = (s32[64]{0:T(128)S(1)}, s32[64]{0:T(128)}, u32[]{:S(2)}) copy-start(s32[64]{0:T(128)} %off_ref.1) | copy-start | bytes 772
  0.7 14.3 %copy-start.3 = (s32[64]{0:T(128)S(1)}, s32[64]{0:T(128)}, u32[]{:S(2)}) copy-start(s32[64]{0:T(128)} %cnt_ref.1) | copy-start | bytes 772
  0.7 14.3 %copy-start.4 = (s32[64]{0:T(128)S(1)}, s32[64]{0:T(128)}, u32[]{:S(2)}) copy-start(s32[64]{0:T(128)} %slot_ref.1) | copy-start | bytes 772
  2.7 18.2 %all-to-all-start = ((bf16[32,8,640]{2,1,0:T(8,128)(2,1)}), bf16[32,8,640]{2,1,0:T(8,128)(2,1)S(1)}, u32[]{:S(2)}, u32[]{:S(2)}) async-start(bf16[32,8,640]{2,1,0:T(8,128)(2,1)} %bitcast.27), calls=%async_computation | async-start | bytes 655360 | tf_op jit(solution)/shard_map/all_to_all | solution.py:275
  11.4 8.5 %collective-permute-start = (bf16[32,4608]{1,0:T(8,128)(2,1)S(1)}, bf16[32,4608]{1,0:T(8,128)(2,1)S(1)}, u32[]{:S(2)}, u32[]{:S(2)}) collective-permute-start(bf16[32,4608]{1,0:T(8,128)(2,1)S(1)} %pad_maximum_fusion), channel_id=1, source_target_pairs={{0,8},{8,16},{16,24},{24,32},{32,40},{40,48},{48,56},{56,64},{64,7... | collective-permute-start | bytes 884744 | tf_op jit(solution)/shard_map/ppermute | solution.py:283
  21.6 25.1 %copy-start = (bf16[256,3584]{1,0:T(8,128)(2,1)S(1)}, bf16[256,3584]{1,0:T(8,128)(2,1)}, u32[]{:S(2)}) copy-start(bf16[256,3584]{1,0:T(8,128)(2,1)} %hid_ref.3) | copy-start | bytes 5505028
  21.6 25.1 %copy-start.1 = (bf16[256,1024]{1,0:T(8,128)(2,1)S(1)}, bf16[256,1024]{1,0:T(8,128)(2,1)}, u32[]{:S(2)}) copy-start(bf16[256,1024]{1,0:T(8,128)(2,1)} %grad_ref.3) | copy-start | bytes 1572868
  91.9 15.5 %all-to-all-start.4 = ((bf16[32,8,640]{2,1,0:T(8,128)(2,1)}), bf16[32,8,640]{2,1,0:T(8,128)(2,1)S(1)}, u32[]{:S(2)}, u32[]{:S(2)}) async-start(bf16[32,8,640]{2,1,0:T(8,128)(2,1)} %bitcast.11), calls=%async_computation.4 | async-start | bytes 655360 | tf_op jit(solution)/shard_map/all_to_all | solution.py:275
  96.3 9.0 %collective-permute-start.1 = (bf16[32,3584]{1,0:T(8,128)(2,1)S(1)}, bf16[32,3584]{1,0:T(8,128)(2,1)S(1)}, u32[]{:S(2)}, u32[]{:S(2)}) collective-permute-start(bf16[32,3584]{1,0:T(8,128)(2,1)S(1)} %extra.1), channel_id=1, source_target_pairs={{8,0},{16,8},{24,16},{32,24},{40,32},{48,40},{56,48},{64,56},{72,6... | collective-permute-start | bytes 688136 | tf_op jit(solution)/shard_map/ppermute | solution.py:323

commit v4 on v3

--- a/solution.py
+++ b/solution.py
@@ -4,6 +4,7 @@
 from jax.experimental import pallas as pl
 from jax.experimental.pallas import tpu as pltpu
 from jax.sharding import PartitionSpec as P
+
 
 adapter_factor = 2.0
 BF = jnp.bfloat16
@@ -113,7 +114,7 @@
     return one_hot(((i >> 2) == tab_ref[0:1, :]) & (((i >> 1) & 1) == r) & ((i & 1) == part))
 
 
-def pick_kernel(tab_ref, in_ref, after_ref, out_ref):
+def pick_kernel(tab_ref, in_ref, out_ref):
     out_ref[:, :LO] = dot(slot_hits(tab_ref, 0), in_ref[...], 0, 0).astype(BF)
     out_ref[:, LO:] = dot(slot_hits(tab_ref, 1), in_ref[:, :HI], 0, 0).astype(BF)
 
@@ -134,6 +135,10 @@
     o = iota((RANK, 128), 0)
     i = iota((RANK, 128), 1)
     return (i & 1) * 8 + (i >> 4) == o
+
+
+def mark_kernel(in_hbm, mine_ref, out_ref):
+    out_ref[...] = mine_ref[...]
 
 
 def score_kernel(in_ref, hid_ref, grad_ref, extra_ref, mine_ref, out_ref):
@@ -213,14 +218,25 @@
         ).astype(BF)
 
 
-def hidden_kernel(sig_ref, in_ref, mine_ref, back_ref, out_ref):
+def hidden_kernel(sig_ref, in_ref, mine_ref, out_hbm, tail_ref, head_ref, sems):
     up, _ = spread_signal(sig_ref, mine_ref, 0)
     cut = TOK - EXTRA
+    copies = []
     for q in range(4):
         lanes = slice(q * QH, (q + 1) * QH)
         rows = adapter_factor * dot(up, quarter(in_ref, q, slice(0, QH)), 0, 0)
-        out_ref[:cut, lanes] = rows[:cut, :].astype(BF)
-        out_ref[cut:, lanes] = (rows[cut:, :] + back_ref[:, lanes].astype(F32)).astype(BF)
+        head_ref[:, lanes] = rows[:cut, :].astype(BF)
+        tail_ref[:, lanes] = rows[cut:, :].astype(BF)
+        copies.append(
+            pltpu.make_async_copy(
+                head_ref.at[:, pl.ds(q * QH, QH)],
+                out_hbm.at[pl.ds(0, cut), pl.ds(q * QH, QH)],
+                sems.at[q],
+            )
+        )
+        copies[-1].start()
+    for copy in copies:
+        copy.wait()
 
 
 def reduce_kernel(tab_ref, in_ref, out_ref):
@@ -230,10 +246,29 @@
     out_ref[:, HI:] = low[:, HI:].astype(BF)
 
 
-def join_kernel(scale_ref, in_ref, down_hbm, up_hbm, down_ref, up_ref, sems):
+def join_kernel(
+    head_hbm,
+    scale_ref,
+    in_ref,
+    tail_ref,
+    back_ref,
+    hidden_hbm,
+    down_hbm,
+    up_hbm,
+    down_ref,
+    up_ref,
+    rows_ref,
+    sems,
+):
+    rows_ref[...] = (tail_ref[...].astype(F32) + back_ref[...].astype(F32)).astype(BF)
+    copies = [
+        pltpu.make_async_copy(
+            rows_ref, hidden_hbm.at[pl.ds(TOK - EXTRA, EXTRA), :], sems.at[8]
+        )
+    ]
+    copies[0].start()
     scale = scale_ref[:, 0:1]
     pieces = in_ref[...]
-    copies = []
     for q in range(4):
         rows = dot(travel_order(q * 64, 64), pieces, 0, 0)
         low = rows[:32, :] * scale
@@ -253,19 +288,19 @@
         copy.wait()
 
 
-def call(kernel, name, outs, scratch, *args, smem=0, hbm_in=0, any_in=0, hbm_out=False, limit=LIMIT):
+def call(kernel, outs, scratch, *args, smem=0, any_in=0, hbm_in=0, hbm_out=0, alias=None, limit=LIMIT):
     vmem = pl.BlockSpec(memory_space=pltpu.VMEM)
     scalar = pl.BlockSpec(memory_space=pltpu.SMEM)
     hbm = pl.BlockSpec(memory_space=pltpu.HBM)
     return pl.pallas_call(
         kernel,
-        name=name,
         out_shape=[jax.ShapeDtypeStruct(s, t) for s, t in outs],
-        in_specs=[scalar] * smem + [hbm] * hbm_in
-        + [vmem] * (len(args) - smem - hbm_in - any_in)
-        + [pl.BlockSpec(memory_space=pl.ANY)] * any_in,
-        out_specs=[hbm if hbm_out else vmem] * len(outs),
+        in_specs=[scalar] * smem + [pl.BlockSpec(memory_space=pl.ANY)] * any_in
+        + [hbm] * hbm_in
+        + [vmem] * (len(args) - smem - any_in - hbm_in),
+        out_specs=[hbm] * hbm_out + [vmem] * (len(outs) - hbm_out),
         scratch_shapes=scratch,
+        input_output_aliases=alias or {},
         compiler_params=pltpu.CompilerParams(vmem_limit_bytes=limit),
     )(*args)
 
@@ -285,7 +320,6 @@
     up = adapter_up.reshape(2 * RANK, FEA)
     (cut,) = call(
         cut_kernel,
-        "cut",
         [((256, LO), BF)],
         [
             pltpu.VMEM((32, HID), BF),
@@ -300,7 +334,6 @@
     pieces = exchange(cut, "dp", DP)
     tab, mine, scale = call(
         tables_kernel,
-        "tables",
         [((8, 512), I32), ((8, 384), I32), ((32, 128), F32)],
         [],
         dp,
@@ -310,34 +343,44 @@
         smem=4,
     )
     block = ((512, ROW), BF)
-    (picked,) = call(pick_kernel, "pick", [block], [], tab, pieces, extra, any_in=1)
+    (picked,) = call(pick_kernel, [block], [], tab, pieces)
     local = exchange(picked, "dp", DP)
+    (mine,) = call(mark_kernel, [((8, 384), I32)], [], local, mine, any_in=1)
     tokens = (hidden, output_gradient, extra, mine)
-    (partial,) = call(score_kernel, "score", [((TP * SIG, 128), BF)], [], local, *tokens)
+    (partial,) = call(score_kernel, [((TP * SIG, 128), BF)], [], local, *tokens)
     signals = exchange(partial, "tensor", TP)
-    (sums,) = call(sum_kernel, "sums", [block], [], signals, *tokens)
+    (sums,) = call(sum_kernel, [block], [], signals, *tokens)
     gathered = exchange(sums, "dp", DP)
-    (extra_gradient,) = call(
-        extra_kernel, "extra", [((EXTRA, HID), BF)], [], signals, local, mine
-    )
+    (extra_gradient,) = call(extra_kernel, [((EXTRA, HID), BF)], [], signals, local, mine)
     back = lax.ppermute(extra_gradient, "dp", backward)
-    (hidden_gradient,) = call(
-        hidden_kernel, "hidden", [((TOK, HID), BF)], [], signals, local, mine, back
-    )
-    (slot_sums,) = call(reduce_kernel, "reduce", [((256, LO), BF)], [], tab, gathered)
+    head, tail = call(
+        hidden_kernel,
+        [((TOK, HID), BF), ((EXTRA, HID), BF)],
+        [pltpu.VMEM((TOK - EXTRA, HID), BF), pltpu.SemaphoreType.DMA((4,))],
+        signals,
+        local,
+        mine,
+        hbm_out=1,
+    )
+    (slot_sums,) = call(reduce_kernel, [((256, LO), BF)], [], tab, gathered)
     owned = exchange(slot_sums, "dp", DP)
-    down_gradient, up_gradient = call(
+    hidden_gradient, down_gradient, up_gradient = call(
         join_kernel,
-        "join",
-        [((32, HID), F32), ((32, FEA), F32)],
+        [((TOK, HID), BF), ((32, HID), F32), ((32, FEA), F32)],
         [
             pltpu.VMEM((32, HID), F32),
             pltpu.VMEM((32, FEA), F32),
-            pltpu.SemaphoreType.DMA((8,)),
+            pltpu.VMEM((EXTRA, HID), BF),
+            pltpu.SemaphoreType.DMA((9,)),
         ],
+        head,
         scale,
         owned,
-        hbm_out=True,
+        tail,
+        back,
+        hbm_in=1,
+        hbm_out=3,
+        alias={0: 0},
     )
     return (
         hidden_gradient,

time: 109 us -> 108 us (level)
  blocking collectives: 66.5 us -> 42.5 us
  waiting for transfers between devices: 11.7 us -> 26.8 us
  starting transfers between devices: 18.3 us -> 22.1 us
  local copies, waits for them, and re-layouts: 0.04 us -> 2.98 us
    all_to_all x3 -> x2, blocking collectives: 66.5 us -> 42.5 us  [exchange(): return lax.all_to_all(block, axis, 0, 0, tiled=True).reshape(x.shape)]
    all_to_all x2 -> x3, waiting for transfers between devices: 1.11 us -> 21.8 us  [exchange(): return lax.all_to_all(block, axis, 0, 0, tiled=True).reshape(x.shape)]
    all_to_all x2 -> x3, starting transfers between devices: 12.5 us -> 16.4 us  [exchange(): return lax.all_to_all(block, axis, 0, 0, tiled=True).reshape(x.shape)]
    ppermute x1, waiting for transfers between devices: 3.85 us -> 0.01 us  [on_device(): extra = lax.ppermute(last, 'dp', onward)]
    unnamed x10 -> x24, local copies, waits for them, and re-layouts: 0.03 us -> 2.98 us
    ppermute x1, waiting for transfers between devices: 6.71 us -> 5.01 us  [on_device(): back = lax.ppermute(extra_gradient, 'dp', backward)]
    pallas_call x9 -> x10, Pallas kernels: 11.2 us -> 11.9 us  [call(): pl.pallas_call(kernel, out_shape=[jax.ShapeDtypeStruct(s, t) for s, t in...]
  transfers between devices with their start and end apart: 4 -> 5, of which waited for: 3 -> 4; matrix products, arithmetic and copies ran while one was open for 0% -> 1% of each run, Pallas kernels for 3% -> 3%
where the time goes in v4:
time: 108 us
  blocking collectives  42.5 us (39%)
  waiting for transfers between devices  26.8 us (25%)
  starting transfers between devices  22.1 us (20%)
  Pallas kernels  11.9 us (11%)
  local copies, waits for them, and re-layouts  2.98 us (3%)
    all_to_all x2, blocking collectives, exchange(): return lax.all_to_all(block, axis, 0, 0, tiled=True).reshape(x.shape)  42.5 us
    all_to_all x3, waiting for transfers between devices, exchange(): return lax.all_to_all(block, axis, 0, 0, tiled=True).reshape(x.shape)  21.8 us
    all_to_all x3, starting transfers between devices, exchange(): return lax.all_to_all(block, axis, 0, 0, tiled=True).reshape(x.shape)  16.4 us
    pallas_call x10, Pallas kernels, call(): pl.pallas_call(kernel, out_shape=[jax.ShapeDtypeStruct(s, t) for s, t in...  11.9 us
    ppermute x1, waiting for transfers between devices, on_device(): back = lax.ppermute(extra_gradient, 'dp', backward)  5.01 us
    ppermute x1, starting transfers between devices, on_device(): extra = lax.ppermute(last, 'dp', onward)  3.51 us
    unnamed x24, local copies, waits for them, and re-layouts  2.98 us
    ppermute x1, starting transfers between devices, on_device(): back = lax.ppermute(extra_gradient, 'dp', backward)  2.26 us
  transfers between devices with their start and end apart: 5, of which 4 were waited for; matrix products, arithmetic and copies ran while one was open for 1% of the time, Pallas kernels for 3%

profile of v4, /device:TPU:1, one launch (start us, length us, event | category | flops | bytes accessed | tf_op | source)
XLA Modules:
  0.0 107.8 jit_solution(8394370355280337841)
XLA Ops:
  0.6 0.0 copy-start.11
  0.6 0.0 copy-start.9
  0.7 2.0 %shard_map.95 = bf16[256,640]{1,0:T(8,128)(2,1)} custom-call(bf16[32,3584]{1,0:T(8,128)(2,1)} %bitcast.28, bf16[32,1024]{1,0:T(8,128)(2,1)} %bitcast.29), custom_call_target="tpu_custom_call" | custom-call | tf_op jit(solution)/shard_map/pallas_call | solution.py:295
  2.6 8.6 %all-to-all-start = ((bf16[32,8,640]{2,1,0:T(8,128)(2,1)}), bf16[32,8,640]{2,1,0:T(8,128)(2,1)S(1)}, u32[]{:S(2)}, u32[]{:S(2)}) async-start(bf16[32,8,640]{2,1,0:T(8,128)(2,1)} %bitcast.27), calls=%async_computation | async-start | bytes 655360 | tf_op jit(solution)/shard_map/all_to_all | solution.py:310
  11.3 1.0 shard_map.94
  12.3 0.0 copy-start.5
  12.3 0.6 copy-done.5
  12.9 0.6 copy-done.7
  13.5 7.3 %all-to-all-done = bf16[32,8,640]{2,1,0:T(8,128)(2,1)S(1)} async-done(((bf16[32,8,640]{2,1,0:T(8,128)(2,1)}), bf16[32,8,640]{2,1,0:T(8,128)(2,1)S(1)}, u32[]{:S(2)}, u32[]{:S(2)}) %all-to-all-start) | async-done | bytes 327712 | tf_op jit(solution)/shard_map/all_to_all | solution.py:310
  20.9 1.6 %shard_map.96 = bf16[512,1152]{1,0:T(8,128)(2,1)} custom-call(s32[8,512]{1,0:T(8,128)S(1)} %get-tuple-element.11.tab_ref, bf16[256,640]{1,0:T(8,128)(2,1)S(1)} %bitcast.25), custom_call_target="tpu_custom_call" | custom-call | tf_op jit(solution)/shard_map/pallas_call | solution.py:295
  22.5 3.9 %all-to-all-start.1 = ((bf16[32,16,1152]{2,1,0:T(8,128)(2,1)}), bf16[32,16,1152]{2,1,0:T(8,128)(2,1)S(1)}, u32[]{:S(2)}, u32[]{:S(2)}) async-start(bf16[32,16,1152]{2,1,0:T(8,128)(2,1)} %bitcast.5), calls=%async_computation.1 | async-start | bytes 2359296 | tf_op jit(solution)/shard_map/all_to_all | solution.py:310
  26.4 0.0 copy-start
  26.4 0.7 pad_maximum_fusion
  27.1 3.5 %collective-permute-start = (bf16[32,4608]{1,0:T(8,128)(2,1)}, bf16[32,4608]{1,0:T(8,128)(2,1)S(1)}, u32[]{:S(2)}, u32[]{:S(2)}) collective-permute-start(bf16[32,4608]{1,0:T(8,128)(2,1)} %pad_maximum_fusion), channel_id=1, source_target_pairs={{0,8},{8,16},{16,24},{24,32},{32,40},{40,48},{48,56},{56,64},{64,7... | collective-permute-start | bytes 884744 | tf_op jit(solution)/shard_map/ppermute | solution.py:318
  30.7 14.1 %all-to-all-done.1 = bf16[32,16,1152]{2,1,0:T(8,128)(2,1)S(1)} async-done(((bf16[32,16,1152]{2,1,0:T(8,128)(2,1)}), bf16[32,16,1152]{2,1,0:T(8,128)(2,1)S(1)}, u32[]{:S(2)}, u32[]{:S(2)}) %all-to-all-start.1) | async-done | bytes 1179680 | tf_op jit(solution)/shard_map/all_to_all | solution.py:310
  44.8 0.7 copy-done.8
  45.5 0.0 collective-permute-done.extra_ref
  45.5 0.0 copy-start.1
  45.5 1.0 copy-done.1
  46.6 1.4 %shard_map.98 = bf16[768,128]{1,0:T(8,128)(2,1)S(1)} custom-call(bf16[512,1152]{1,0:T(8,128)(2,1)S(1)} %bitcast.16, bf16[256,3584]{1,0:T(8,128)(2,1)S(1)} %copy-done, bf16[256,1024]{1,0:T(8,128)(2,1)S(1)} %copy-done.1, bf16[32,4608]{1,0:T(8,128)(2,1)S(1)} %collective-permute-done.extra_ref, s32[8,384]{1,0:T(8,128)S(1)} %shard_map.97.mine_ref), custom_call_target="tpu_custom_call" | custom-call | tf_op jit(solution)/shard_map/pallas_call | solution.py:295
  48.0 17.9 %all_to_all.25 = bf16[8,96,128]{2,1,0:T(8,128)(2,1)S(1)} all-to-all(bf16[8,96,128]{2,1,0:T(8,128)(2,1)S(1)} %bitcast.26), channel_id=1, replica_groups=mesh['dp'=32,'tensor'=8] {'tensor'}, dimensions={0} | all-to-all | bytes 393216 | tf_op jit(solution)/shard_map/all_to_all | solution.py:310
  66.0 1.1 %shard_map.100 = bf16[512,1152]{1,0:T(8,128)(2,1)S(1)} custom-call(bf16[768,128]{1,0:T(8,128)(2,1)S(1)} %bitcast.21, bf16[256,3584]{1,0:T(8,128)(2,1)S(1)} %copy-done, bf16[256,1024]{1,0:T(8,128)(2,1)S(1)} %copy-done.2, bf16[32,4608]{1,0:T(8,128)(2,1)S(1)} %collective-permute-done.extra_ref, s32[8,384]{1,0:T(8,128)S(1)} %shard_map.97.mine_ref), custom_call_target="tpu_custom_call" | custom-call | tf_op jit(solution)/shard_map/pallas_call | solution.py:295
  67.1 24.5 %all_to_all.26 = bf16[32,16,1152]{2,1,0:T(8,128)(2,1)S(1)} all-to-all(bf16[32,16,1152]{2,1,0:T(8,128)(2,1)S(1)} %bitcast.19), channel_id=1, replica_groups=mesh['dp'=32,'tensor'=8] {'dp'}, dimensions={0} | all-to-all | bytes 2359296 | tf_op jit(solution)/shard_map/all_to_all | solution.py:310
  91.6 1.3 %shard_map.101 = bf16[256,640]{1,0:T(8,128)(2,1)} custom-call(s32[8,512]{1,0:T(8,128)S(1)} %copy-done.4, bf16[512,1152]{1,0:T(8,128)(2,1)S(1)} %bitcast.20), custom_call_target="tpu_custom_call" | custom-call | tf_op jit(solution)/shard_map/pallas_call | solution.py:295
  92.8 3.9 %all-to-all-start.4 = ((bf16[32,8,640]{2,1,0:T(8,128)(2,1)}), bf16[32,8,640]{2,1,0:T(8,128)(2,1)S(1)}, u32[]{:S(2)}, u32[]{:S(2)}) async-start(bf16[32,8,640]{2,1,0:T(8,128)(2,1)} %bitcast.11), calls=%async_computation.4 | async-start | bytes 655360 | tf_op jit(solution)/shard_map/all_to_all | solution.py:310
  96.8 0.0 copy-start.6
  96.8 0.5 shard_map.102
  97.3 2.3 %collective-permute-start.1 = (bf16[32,3584]{1,0:T(8,128)(2,1)S(1)}, bf16[32,3584]{1,0:T(8,128)(2,1)S(1)}, u32[]{:S(2)}, u32[]{:S(2)}) collective-permute-start(bf16[32,3584]{1,0:T(8,128)(2,1)S(1)} %shard_map.102), channel_id=1, source_target_pairs={{8,0},{16,8},{24,16},{32,24},{40,32},{48,40},{56,48},{64,56},{72,6... | collective-permute-start | bytes 688136 | tf_op jit(solution)/shard_map/ppermute | solution.py:355
  99.5 1.7 %shard_map.99 = (bf16[256,3584]{1,0:T(8,128)(2,1)}, bf16[32,3584]{1,0:T(8,128)(2,1)S(1)}) custom-call(bf16[768,128]{1,0:T(8,128)(2,1)S(1)} %bitcast.23, bf16[512,1152]{1,0:T(8,128)(2,1)S(1)} %bitcast.18, s32[8,384]{1,0:T(8,128)S(1)} %shard_map.97.mine_ref), custom_call_target="tpu_custom_call" | custom-call | tf_op jit(solution)/shard_map/pallas_call | solution.py:295
  101.2 5.0 %collective-permute-done.1.back_ref = bf16[32,3584]{1,0:T(8,128)(2,1)S(1)} collective-permute-done((bf16[32,3584]{1,0:T(8,128)(2,1)S(1)}, bf16[32,3584]{1,0:T(8,128)(2,1)S(1)}, u32[]{:S(2)}, u32[]{:S(2)}) %collective-permute-start.1) | collective-permute-done | bytes 229408 | tf_op jit(solution)/shard_map/ppermute | solution.py:355
  106.2 0.3 all-to-all-done.4
  106.5 1.3 %shard_map.103 = (bf16[256,3584]{1,0:T(8,128)(2,1)}, f32[32,3584]{1,0:T(8,128)}, f32[32,1024]{1,0:T(8,128)}) custom-call(bf16[256,3584]{1,0:T(8,128)(2,1)} %get-tuple-element.13.head_hbm, f32[32,128]{1,0:T(8,128)S(1)} %copy-done.6, bf16[256,640]{1,0:T(8,128)(2,1)S(1)} %bitcast.24, ...), custom_call_target="tpu_custom_call", output_to_operand_aliasing={{0}: (0, {})} | custom-call | tf_op jit(solution)/shard_map/pallas_call | solution.py:295
  (19 shorter events, 0.0 us)
Async XLA Ops:
  0.6 10.6 %copy-start.11 = (s32[64]{0:T(128)S(1)}, s32[64]{0:T(128)}, u32[]{:S(2)}) copy-start(s32[64]{0:T(128)} %slot_ref.1) | copy-start | bytes 772
  0.6 10.6 %copy-start.9 = (s32[64]{0:T(128)S(1)}, s32[64]{0:T(128)}, u32[]{:S(2)}) copy-start(s32[64]{0:T(128)} %off_ref.1) | copy-start | bytes 772
  0.7 10.6 %copy-start.10 = (s32[64]{0:T(128)S(1)}, s32[64]{0:T(128)}, u32[]{:S(2)}) copy-start(s32[64]{0:T(128)} %cnt_ref.1) | copy-start | bytes 772
  2.6 18.2 %all-to-all-start = ((bf16[32,8,640]{2,1,0:T(8,128)(2,1)}), bf16[32,8,640]{2,1,0:T(8,128)(2,1)S(1)}, u32[]{:S(2)}, u32[]{:S(2)}) async-start(bf16[32,8,640]{2,1,0:T(8,128)(2,1)} %bitcast.27), calls=%async_computation | async-start | bytes 655360 | tf_op jit(solution)/shard_map/all_to_all | solution.py:310
  12.3 0.6 copy-start.5
  12.9 0.6 copy-start.7
  13.5 9.0 %copy-start.3 = (s32[8,512]{1,0:T(8,128)}, s32[8,512]{1,0:T(8,128)S(1)}, u32[]{:S(2)}) copy-start(s32[8,512]{1,0:T(8,128)S(1)} %get-tuple-element.11.tab_ref) | copy-start | bytes 49156
  22.5 3.9 %slice-start = ((bf16[256,3584]{1,0:T(8,128)(2,1)}), bf16[32,3584]{1,0:T(8,128)(2,1)S(1)}, s32[]{:S(2)}) async-start(bf16[256,3584]{1,0:T(8,128)(2,1)} %hid_ref.3), calls=%async_computation.5 | async-start | bytes 458752 | tf_op jit(solution)/shard_map/slice | solution.py:317
  22.5 3.9 %slice-start.1 = ((bf16[256,1024]{1,0:T(8,128)(2,1)}), bf16[32,1024]{1,0:T(8,128)(2,1)S(1)}, s32[]{:S(2)}) async-start(bf16[256,1024]{1,0:T(8,128)(2,1)} %grad_ref.3), calls=%async_computation.6 | async-start | bytes 131072 | tf_op jit(solution)/shard_map/slice | solution.py:317
  22.5 22.3 %all-to-all-start.1 = ((bf16[32,16,1152]{2,1,0:T(8,128)(2,1)}), bf16[32,16,1152]{2,1,0:T(8,128)(2,1)S(1)}, u32[]{:S(2)}, u32[]{:S(2)}) async-start(bf16[32,16,1152]{2,1,0:T(8,128)(2,1)} %bitcast.5), calls=%async_computation.1 | async-start | bytes 2359296 | tf_op jit(solution)/shard_map/all_to_all | solution.py:310
  26.4 19.1 %copy-start = (bf16[256,3584]{1,0:T(8,128)(2,1)S(1)}, bf16[256,3584]{1,0:T(8,128)(2,1)}, u32[]{:S(2)}) copy-start(bf16[256,3584]{1,0:T(8,128)(2,1)} %hid_ref.3) | copy-start | bytes 5505028
  27.1 18.4 %collective-permute-start = (bf16[32,4608]{1,0:T(8,128)(2,1)}, bf16[32,4608]{1,0:T(8,128)(2,1)S(1)}, u32[]{:S(2)}, u32[]{:S(2)}) collective-permute-start(bf16[32,4608]{1,0:T(8,128)(2,1)} %pad_maximum_fusion), channel_id=1, source_target_pairs={{0,8},{8,16},{16,24},{24,32},{32,40},{40,48},{48,56},{56,64},{64,7... | collective-permute-start | bytes 884744 | tf_op jit(solution)/shard_map/ppermute | solution.py:318
  44.8 0.7 copy-start.8
  45.5 1.0 copy-start.1
  46.6 19.4 %copy-start.2 = (bf16[256,1024]{1,0:T(8,128)(2,1)S(1)}, bf16[256,1024]{1,0:T(8,128)(2,1)}, u32[]{:S(2)}) copy-start(bf16[256,1024]{1,0:T(8,128)(2,1)} %grad_ref.3) | copy-start | bytes 1572868
  67.1 24.5 %copy-start.4 = (s32[8,512]{1,0:T(8,128)S(1)}, s32[8,512]{1,0:T(8,128)}, u32[]{:S(2)}) copy-start(s32[8,512]{1,0:T(8,128)} %copy-done.3) | copy-start | bytes 49156
  92.8 13.7 %all-to-all-start.4 = ((bf16[32,8,640]{2,1,0:T(8,128)(2,1)}), bf16[32,8,640]{2,1,0:T(8,128)(2,1)S(1)}, u32[]{:S(2)}, u32[]{:S(2)}) async-start(bf16[32,8,640]{2,1,0:T(8,128)(2,1)} %bitcast.11), calls=%async_computation.4 | async-start | bytes 655360 | tf_op jit(solution)/shard_map/all_to_all | solution.py:310
  96.8 9.7 %copy-start.6 = (f32[32,128]{1,0:T(8,128)S(1)}, f32[32,128]{1,0:T(8,128)}, u32[]{:S(2)}) copy-start(f32[32,128]{1,0:T(8,128)} %copy-done.5) | copy-start | bytes 49156
  97.3 9.0 %collective-permute-start.1 = (bf16[32,3584]{1,0:T(8,128)(2,1)S(1)}, bf16[32,3584]{1,0:T(8,128)(2,1)S(1)}, u32[]{:S(2)}, u32[]{:S(2)}) collective-permute-start(bf16[32,3584]{1,0:T(8,128)(2,1)S(1)} %shard_map.102), channel_id=1, source_target_pairs={{8,0},{16,8},{24,16},{32,24},{40,32},{48,40},{56,48},{64,56},{72,6... | collective-permute-start | bytes 688136 | tf_op jit(solution)/shard_map/ppermute | solution.py:355

commit v5 on v4

--- a/solution.py
+++ b/solution.py
@@ -23,7 +23,7 @@
 LO = 640
 HI = ROW - LO
 EXTRA = 32
-SIG = 96
+SIG = 72
 LIMIT = 16 * 1024 * 1024
 
 
@@ -137,11 +137,11 @@
     return (i & 1) * 8 + (i >> 4) == o
 
 
-def mark_kernel(in_hbm, mine_ref, out_ref):
+def mark_kernel(in_hbm, mine_ref, grad_ref, out_ref):
     out_ref[...] = mine_ref[...]
 
 
-def score_kernel(in_ref, hid_ref, grad_ref, extra_ref, mine_ref, out_ref):
+def score_kernel(grad_ref, in_ref, hid_ref, extra_ref, mine_ref, out_ref):
     own_up = jnp.zeros((128, TOK), F32)
     own_down = jnp.zeros((128, TOK), F32)
     extra_up = jnp.zeros((128, EXTRA), F32)
@@ -151,6 +151,7 @@
         part = quarter(in_ref, q, slice(0, QH))
         own_down += dot(part, hid_ref[:, lanes], 1, 1)
         extra_down += dot(part, extra_ref[:, lanes], 1, 1)
+    for q in range(4):
         lanes = slice(q * QF, (q + 1) * QF)
         part = quarter(in_ref, q, slice(QH, ROW))
         own_up += dot(part, grad_ref[:, lanes], 1, 1)
@@ -171,37 +172,44 @@
         ]
 
     block = jnp.concatenate(folded(own, own_up, own_down), axis=0).astype(BF)
-    tail = jnp.concatenate(folded(extra, extra_up, extra_down), axis=0).astype(BF)
-    tail = jnp.concatenate([tail, jnp.zeros((32, 128 - EXTRA), BF)], axis=1)
-    block = jnp.concatenate([block[:, :128], block[:, 128:], tail], axis=0)
+    tail = jnp.concatenate(folded(extra, extra_up, extra_down), axis=0)
+    tail = jnp.concatenate([tail[i * 8 : i * 8 + 8, :] for i in range(4)], axis=1).astype(BF)
     for z in range(TP):
-        out_ref[z * SIG : (z + 1) * SIG, :] = block
+        out_ref[z * SIG : z * SIG + 32, :] = block[:, :128]
+        out_ref[z * SIG + 32 : z * SIG + 64, :] = block[:, 128:]
+        out_ref[z * SIG + 64 : (z + 1) * SIG, :] = tail
 
 
 def spread_signal(sig_ref, mine_ref, first):
-    parts = []
-    for base in (0, 32, 64):
-        at = base + first
-        total = sig_ref[at : at + RANK, :].astype(F32)
+    def total(at, rows):
+        part = sig_ref[at : at + rows, :].astype(F32)
         for z in range(1, TP):
-            total += sig_ref[z * SIG + at : z * SIG + at + RANK, :].astype(F32)
-        parts.append(total.astype(BF))
+            part += sig_ref[z * SIG + at : z * SIG + at + rows, :].astype(F32)
+        return part
+
+    tail = total(64, 8)
+    at = first * 4
+    tail = jnp.concatenate(
+        [tail[:, at : at + EXTRA], tail[:, at + EXTRA : at + 2 * EXTRA]], axis=0
+    )
+    parts = [total(first, RANK), total(32 + first, RANK)]
     own, extra = members(mine_ref)
     fold = one_hot(rank_rows())
-    rows = dot(fold, jnp.concatenate(parts[:2], axis=1), 0, 0)
-    tail = dot(fold, parts[2], 0, 0)[:, :EXTRA]
+    rows = dot(fold, jnp.concatenate(parts, axis=1).astype(BF), 0, 0)
+    tail = dot(fold, tail.astype(BF), 0, 0)
     return jnp.where(own, rows, 0.0).astype(BF), jnp.where(extra, tail, 0.0).astype(BF)
 
 
-def sum_kernel(sig_ref, hid_ref, grad_ref, extra_ref, mine_ref, out_ref):
+def sum_kernel(grad_ref, sig_ref, hid_ref, extra_ref, mine_ref, out_ref):
     up, up_extra = spread_signal(sig_ref, mine_ref, 0)
-    down, down_extra = spread_signal(sig_ref, mine_ref, RANK)
     for q in range(4):
         lanes = slice(q * QH, (q + 1) * QH)
         sums = dot(up, hid_ref[:, lanes]) + dot(up_extra, extra_ref[:, lanes])
         for rp in range(8):
             at = (rp * 4 + q) * 16
             out_ref[at : at + 16, :QH] = sums[rp * 16 : rp * 16 + 16, :].astype(BF)
+    down, down_extra = spread_signal(sig_ref, mine_ref, RANK)
+    for q in range(4):
         sums = dot(down, grad_ref[:, q * QF : (q + 1) * QF]) + dot(
             down_extra, extra_ref[:, HID + q * QF : HID + (q + 1) * QF]
         )
@@ -345,11 +353,11 @@
     block = ((512, ROW), BF)
     (picked,) = call(pick_kernel, [block], [], tab, pieces)
     local = exchange(picked, "dp", DP)
-    (mine,) = call(mark_kernel, [((8, 384), I32)], [], local, mine, any_in=1)
-    tokens = (hidden, output_gradient, extra, mine)
-    (partial,) = call(score_kernel, [((TP * SIG, 128), BF)], [], local, *tokens)
+    (mine,) = call(mark_kernel, [((8, 384), I32)], [], local, mine, output_gradient, any_in=1)
+    tokens = (hidden, extra, mine)
+    (partial,) = call(score_kernel, [((TP * SIG, 128), BF)], [], output_gradient, local, *tokens)
     signals = exchange(partial, "tensor", TP)
-    (sums,) = call(sum_kernel, [block], [], signals, *tokens)
+    (sums,) = call(sum_kernel, [block], [], output_gradient, signals, *tokens)
     gathered = exchange(sums, "dp", DP)
     (extra_gradient,) = call(extra_kernel, [((EXTRA, HID), BF)], [], signals, local, mine)
     back = lax.ppermute(extra_gradient, "dp", backward)

time: 108 us -> 107 us (level)
  blocking collectives: 42.5 us -> 40.8 us
    all_to_all x2, blocking collectives: 42.5 us -> 40.8 us  [exchange(): return lax.all_to_all(block, axis, 0, 0, tiled=True).reshape(x.shape)]
where the time goes in v5:
time: 107 us; the launch traced here: 106 us
  blocking collectives  40.8 us (38%)
  waiting for transfers between devices  26.8 us (25%)
  starting transfers between devices  22.1 us (21%)
  Pallas kernels  12 us (11%)
  local copies, waits for them, and re-layouts  2.99 us (3%)
    all_to_all x2, blocking collectives, exchange(): return lax.all_to_all(block, axis, 0, 0, tiled=True).reshape(x.shape)  40.8 us
    all_to_all x3, waiting for transfers between devices, exchange(): return lax.all_to_all(block, axis, 0, 0, tiled=True).reshape(x.shape)  21.8 us
    all_to_all x3, starting transfers between devices, exchange(): return lax.all_to_all(block, axis, 0, 0, tiled=True).reshape(x.shape)  16.4 us
    pallas_call x10, Pallas kernels, call(): pl.pallas_call(kernel, out_shape=[jax.ShapeDtypeStruct(s, t) for s, t in...  12 us
    ppermute x1, waiting for transfers between devices, on_device(): back = lax.ppermute(extra_gradient, 'dp', backward)  4.99 us
    ppermute x1, starting transfers between devices, on_device(): extra = lax.ppermute(last, 'dp', onward)  3.51 us
    unnamed x24, local copies, waits for them, and re-layouts  2.98 us
    ppermute x1, starting transfers between devices, on_device(): back = lax.ppermute(extra_gradient, 'dp', backward)  2.26 us
  transfers between devices with their start and end apart: 5, of which 4 were waited for; matrix products, arithmetic and copies ran while one was open for 1% of the time, Pallas kernels for 3%

profile of v5, /device:TPU:1, one launch (start us, length us, event | category | flops | bytes accessed | tf_op | source)
XLA Modules:
  0.0 106.3 jit_solution(3614707700862742443)
XLA Ops:
  0.6 0.0 copy-start.11
  0.6 0.0 copy-start.9
  0.7 0.0 copy-start.10
  0.7 2.0 %shard_map.95 = bf16[256,640]{1,0:T(8,128)(2,1)} custom-call(bf16[32,3584]{1,0:T(8,128)(2,1)} %bitcast.28, bf16[32,1024]{1,0:T(8,128)(2,1)} %bitcast.29), custom_call_target="tpu_custom_call" | custom-call | tf_op jit(solution)/shard_map/pallas_call | solution.py:303
  2.6 8.6 %all-to-all-start = ((bf16[32,8,640]{2,1,0:T(8,128)(2,1)}), bf16[32,8,640]{2,1,0:T(8,128)(2,1)S(1)}, u32[]{:S(2)}, u32[]{:S(2)}) async-start(bf16[32,8,640]{2,1,0:T(8,128)(2,1)} %bitcast.27), calls=%async_computation | async-start | bytes 655360 | tf_op jit(solution)/shard_map/all_to_all | solution.py:318
  11.3 1.0 shard_map.94
  12.3 0.0 copy-start.5
  12.3 0.6 copy-done.5
  12.9 0.6 copy-done.7
  13.5 7.3 %all-to-all-done = bf16[32,8,640]{2,1,0:T(8,128)(2,1)S(1)} async-done(((bf16[32,8,640]{2,1,0:T(8,128)(2,1)}), bf16[32,8,640]{2,1,0:T(8,128)(2,1)S(1)}, u32[]{:S(2)}, u32[]{:S(2)}) %all-to-all-start) | async-done | bytes 327712 | tf_op jit(solution)/shard_map/all_to_all | solution.py:318
  20.9 1.6 %shard_map.96 = bf16[512,1152]{1,0:T(8,128)(2,1)} custom-call(s32[8,512]{1,0:T(8,128)S(1)} %get-tuple-element.11.tab_ref, bf16[256,640]{1,0:T(8,128)(2,1)S(1)} %bitcast.25), custom_call_target="tpu_custom_call" | custom-call | tf_op jit(solution)/shard_map/pallas_call | solution.py:303
  22.5 3.9 %all-to-all-start.1 = ((bf16[32,16,1152]{2,1,0:T(8,128)(2,1)}), bf16[32,16,1152]{2,1,0:T(8,128)(2,1)S(1)}, u32[]{:S(2)}, u32[]{:S(2)}) async-start(bf16[32,16,1152]{2,1,0:T(8,128)(2,1)} %bitcast.5), calls=%async_computation.1 | async-start | bytes 2359296 | tf_op jit(solution)/shard_map/all_to_all | solution.py:318
  26.4 0.0 copy-start
  26.4 0.7 pad_maximum_fusion
  27.1 3.5 %collective-permute-start = (bf16[32,4608]{1,0:T(8,128)(2,1)}, bf16[32,4608]{1,0:T(8,128)(2,1)S(1)}, u32[]{:S(2)}, u32[]{:S(2)}) collective-permute-start(bf16[32,4608]{1,0:T(8,128)(2,1)} %pad_maximum_fusion), channel_id=1, source_target_pairs={{0,8},{8,16},{16,24},{24,32},{32,40},{40,48},{48,56},{56,64},{64,7... | collective-permute-start | bytes 884744 | tf_op jit(solution)/shard_map/ppermute | solution.py:326
  30.7 14.1 %all-to-all-done.1 = bf16[32,16,1152]{2,1,0:T(8,128)(2,1)S(1)} async-done(((bf16[32,16,1152]{2,1,0:T(8,128)(2,1)}), bf16[32,16,1152]{2,1,0:T(8,128)(2,1)S(1)}, u32[]{:S(2)}, u32[]{:S(2)}) %all-to-all-start.1) | async-done | bytes 1179680 | tf_op jit(solution)/shard_map/all_to_all | solution.py:318
  44.8 1.0 copy-done.1
  45.8 0.7 copy-done.8
  46.6 0.0 collective-permute-done.extra_ref
  46.6 1.5 %shard_map.98 = bf16[576,128]{1,0:T(8,128)(2,1)S(1)} custom-call(bf16[256,1024]{1,0:T(8,128)(2,1)S(1)} %copy-done.1, bf16[512,1152]{1,0:T(8,128)(2,1)S(1)} %bitcast.16, bf16[256,3584]{1,0:T(8,128)(2,1)S(1)} %copy-done, bf16[32,4608]{1,0:T(8,128)(2,1)S(1)} %collective-permute-done.extra_ref, s32[8,384]{1,0:T(8,128)S(1)} %shard_map.97.mine_ref), custom_call_target="tpu_custom_call" | custom-call | tf_op jit(solution)/shard_map/pallas_call | solution.py:303
  48.1 16.7 %all_to_all.25 = bf16[8,72,128]{2,1,0:T(8,128)(2,1)S(1)} all-to-all(bf16[8,72,128]{2,1,0:T(8,128)(2,1)S(1)} %bitcast.26), channel_id=1, replica_groups=mesh['dp'=32,'tensor'=8] {'tensor'}, dimensions={0} | all-to-all | bytes 294912 | tf_op jit(solution)/shard_map/all_to_all | solution.py:318
  64.7 1.2 %shard_map.100 = bf16[512,1152]{1,0:T(8,128)(2,1)S(1)} custom-call(bf16[256,1024]{1,0:T(8,128)(2,1)S(1)} %copy-done.2, bf16[576,128]{1,0:T(8,128)(2,1)S(1)} %bitcast.21, bf16[256,3584]{1,0:T(8,128)(2,1)S(1)} %copy-done, bf16[32,4608]{1,0:T(8,128)(2,1)S(1)} %collective-permute-done.extra_ref, s32[8,384]{1,0:T(8,128)S(1)} %shard_map.97.mine_ref), custom_call_target="tpu_custom_call" | custom-call | tf_op jit(solution)/shard_map/pallas_call | solution.py:303
  65.9 24.2 %all_to_all.26 = bf16[32,16,1152]{2,1,0:T(8,128)(2,1)S(1)} all-to-all(bf16[32,16,1152]{2,1,0:T(8,128)(2,1)S(1)} %bitcast.19), channel_id=1, replica_groups=mesh['dp'=32,'tensor'=8] {'dp'}, dimensions={0} | all-to-all | bytes 2359296 | tf_op jit(solution)/shard_map/all_to_all | solution.py:318
  90.1 1.3 %shard_map.101 = bf16[256,640]{1,0:T(8,128)(2,1)} custom-call(s32[8,512]{1,0:T(8,128)S(1)} %copy-done.4, bf16[512,1152]{1,0:T(8,128)(2,1)S(1)} %bitcast.20), custom_call_target="tpu_custom_call" | custom-call | tf_op jit(solution)/shard_map/pallas_call | solution.py:303
  91.4 3.9 %all-to-all-start.4 = ((bf16[32,8,640]{2,1,0:T(8,128)(2,1)}), bf16[32,8,640]{2,1,0:T(8,128)(2,1)S(1)}, u32[]{:S(2)}, u32[]{:S(2)}) async-start(bf16[32,8,640]{2,1,0:T(8,128)(2,1)} %bitcast.11), calls=%async_computation.4 | async-start | bytes 655360 | tf_op jit(solution)/shard_map/all_to_all | solution.py:318
  95.3 0.0 copy-start.6
  95.3 0.5 shard_map.102
  95.8 2.3 %collective-permute-start.1 = (bf16[32,3584]{1,0:T(8,128)(2,1)S(1)}, bf16[32,3584]{1,0:T(8,128)(2,1)S(1)}, u32[]{:S(2)}, u32[]{:S(2)}) collective-permute-start(bf16[32,3584]{1,0:T(8,128)(2,1)S(1)} %shard_map.102), channel_id=1, source_target_pairs={{8,0},{16,8},{24,16},{32,24},{40,32},{48,40},{56,48},{64,56},{72,6... | collective-permute-start | bytes 688136 | tf_op jit(solution)/shard_map/ppermute | solution.py:363
  98.1 1.7 %shard_map.99 = (bf16[256,3584]{1,0:T(8,128)(2,1)}, bf16[32,3584]{1,0:T(8,128)(2,1)S(1)}) custom-call(bf16[576,128]{1,0:T(8,128)(2,1)S(1)} %bitcast.23, bf16[512,1152]{1,0:T(8,128)(2,1)S(1)} %bitcast.18, s32[8,384]{1,0:T(8,128)S(1)} %shard_map.97.mine_ref), custom_call_target="tpu_custom_call" | custom-call | tf_op jit(solution)/shard_map/pallas_call | solution.py:303
  99.8 5.0 %collective-permute-done.1.back_ref = bf16[32,3584]{1,0:T(8,128)(2,1)S(1)} collective-permute-done((bf16[32,3584]{1,0:T(8,128)(2,1)S(1)}, bf16[32,3584]{1,0:T(8,128)(2,1)S(1)}, u32[]{:S(2)}, u32[]{:S(2)}) %collective-permute-start.1) | collective-permute-done | bytes 229408 | tf_op jit(solution)/shard_map/ppermute | solution.py:363
  104.7 0.3 all-to-all-done.4
  105.0 1.3 %shard_map.103 = (bf16[256,3584]{1,0:T(8,128)(2,1)}, f32[32,3584]{1,0:T(8,128)}, f32[32,1024]{1,0:T(8,128)}) custom-call(bf16[256,3584]{1,0:T(8,128)(2,1)} %get-tuple-element.13.head_hbm, f32[32,128]{1,0:T(8,128)S(1)} %copy-done.6, bf16[256,640]{1,0:T(8,128)(2,1)S(1)} %bitcast.24, ...), custom_call_target="tpu_custom_call", output_to_operand_aliasing={{0}: (0, {})} | custom-call | tf_op jit(solution)/shard_map/pallas_call | solution.py:303
  (19 shorter events, 0.0 us)
Async XLA Ops:
  0.6 10.6 %copy-start.11 = (s32[64]{0:T(128)S(1)}, s32[64]{0:T(128)}, u32[]{:S(2)}) copy-start(s32[64]{0:T(128)} %slot_ref.1) | copy-start | bytes 772
  0.6 10.6 %copy-start.9 = (s32[64]{0:T(128)S(1)}, s32[64]{0:T(128)}, u32[]{:S(2)}) copy-start(s32[64]{0:T(128)} %off_ref.1) | copy-start | bytes 772
  0.7 10.6 %copy-start.10 = (s32[64]{0:T(128)S(1)}, s32[64]{0:T(128)}, u32[]{:S(2)}) copy-start(s32[64]{0:T(128)} %cnt_ref.1) | copy-start | bytes 772
  2.6 18.2 %all-to-all-start = ((bf16[32,8,640]{2,1,0:T(8,128)(2,1)}), bf16[32,8,640]{2,1,0:T(8,128)(2,1)S(1)}, u32[]{:S(2)}, u32[]{:S(2)}) async-start(bf16[32,8,640]{2,1,0:T(8,128)(2,1)} %bitcast.27), calls=%async_computation | async-start | bytes 655360 | tf_op jit(solution)/shard_map/all_to_all | solution.py:318
  12.3 0.6 copy-start.5
  12.9 0.6 copy-start.7
  13.5 9.0 %copy-start.3 = (s32[8,512]{1,0:T(8,128)}, s32[8,512]{1,0:T(8,128)S(1)}, u32[]{:S(2)}) copy-start(s32[8,512]{1,0:T(8,128)S(1)} %get-tuple-element.11.tab_ref) | copy-start | bytes 49156
  22.5 3.9 %slice-start = ((bf16[256,3584]{1,0:T(8,128)(2,1)}), bf16[32,3584]{1,0:T(8,128)(2,1)S(1)}, s32[]{:S(2)}) async-start(bf16[256,3584]{1,0:T(8,128)(2,1)} %hid_ref.3), calls=%async_computation.5 | async-start | bytes 458752 | tf_op jit(solution)/shard_map/slice | solution.py:325
  22.5 3.9 %slice-start.1 = ((bf16[256,1024]{1,0:T(8,128)(2,1)}), bf16[32,1024]{1,0:T(8,128)(2,1)S(1)}, s32[]{:S(2)}) async-start(bf16[256,1024]{1,0:T(8,128)(2,1)} %grad_ref.5), calls=%async_computation.6 | async-start | bytes 131072 | tf_op jit(solution)/shard_map/slice | solution.py:325
  22.5 22.3 %all-to-all-start.1 = ((bf16[32,16,1152]{2,1,0:T(8,128)(2,1)}), bf16[32,16,1152]{2,1,0:T(8,128)(2,1)S(1)}, u32[]{:S(2)}, u32[]{:S(2)}) async-start(bf16[32,16,1152]{2,1,0:T(8,128)(2,1)} %bitcast.5), calls=%async_computation.1 | async-start | bytes 2359296 | tf_op jit(solution)/shard_map/all_to_all | solution.py:318
  26.4 20.2 %copy-start = (bf16[256,3584]{1,0:T(8,128)(2,1)S(1)}, bf16[256,3584]{1,0:T(8,128)(2,1)}, u32[]{:S(2)}) copy-start(bf16[256,3584]{1,0:T(8,128)(2,1)} %hid_ref.3) | copy-start | bytes 5505028
  27.1 19.4 %collective-permute-start = (bf16[32,4608]{1,0:T(8,128)(2,1)}, bf16[32,4608]{1,0:T(8,128)(2,1)S(1)}, u32[]{:S(2)}, u32[]{:S(2)}) collective-permute-start(bf16[32,4608]{1,0:T(8,128)(2,1)} %pad_maximum_fusion), channel_id=1, source_target_pairs={{0,8},{8,16},{16,24},{24,32},{32,40},{40,48},{48,56},{56,64},{64,7... | collective-permute-start | bytes 884744 | tf_op jit(solution)/shard_map/ppermute | solution.py:326
  44.8 1.0 copy-start.1
  45.8 0.7 copy-start.8
  46.6 18.2 %copy-start.2 = (bf16[256,1024]{1,0:T(8,128)(2,1)S(1)}, bf16[256,1024]{1,0:T(8,128)(2,1)}, u32[]{:S(2)}) copy-start(bf16[256,1024]{1,0:T(8,128)(2,1)} %grad_ref.5) | copy-start | bytes 1572868
  65.9 24.2 %copy-start.4 = (s32[8,512]{1,0:T(8,128)S(1)}, s32[8,512]{1,0:T(8,128)}, u32[]{:S(2)}) copy-start(s32[8,512]{1,0:T(8,128)} %copy-done.3) | copy-start | bytes 49156
  91.4 13.7 %all-to-all-start.4 = ((bf16[32,8,640]{2,1,0:T(8,128)(2,1)}), bf16[32,8,640]{2,1,0:T(8,128)(2,1)S(1)}, u32[]{:S(2)}, u32[]{:S(2)}) async-start(bf16[32,8,640]{2,1,0:T(8,128)(2,1)} %bitcast.11), calls=%async_computation.4 | async-start | bytes 655360 | tf_op jit(solution)/shard_map/all_to_all | solution.py:318
  95.3 9.7 %copy-start.6 = (f32[32,128]{1,0:T(8,128)S(1)}, f32[32,128]{1,0:T(8,128)}, u32[]{:S(2)}) copy-start(f32[32,128]{1,0:T(8,128)} %copy-done.5) | copy-start | bytes 49156
  95.8 8.9 %collective-permute-start.1 = (bf16[32,3584]{1,0:T(8,128)(2,1)S(1)}, bf16[32,3584]{1,0:T(8,128)(2,1)S(1)}, u32[]{:S(2)}, u32[]{:S(2)}) collective-permute-start(bf16[32,3584]{1,0:T(8,128)(2,1)S(1)} %shard_map.102), channel_id=1, source_target_pairs={{8,0},{16,8},{24,16},{32,24},{40,32},{48,40},{56,48},{64,56},{72,6... | collective-permute-start | bytes 688136 | tf_op jit(solution)/shard_map/ppermute | solution.py:363

commit v6 on v5

--- a/solution.py
+++ b/solution.py
@@ -82,7 +82,21 @@
     return one_hot(j == q * 64 + h * 32 + s * 16 + rp * 2 + r)
 
 
-def cut_kernel(down_hbm, up_hbm, out_ref, down_ref, up_ref, sems):
+def store_parts(value, out_ref, out_hbm, sems, first):
+    copies = []
+    for n, at in enumerate((0, 256, 512)):
+        width = min(256, LO - at)
+        out_ref[:, at : at + width] = value(slice(at, at + width)).astype(BF)
+        lanes = pl.ds(at, width)
+        copies.append(
+            pltpu.make_async_copy(out_ref.at[:, lanes], out_hbm.at[:, lanes], sems.at[first + n])
+        )
+        copies[-1].start()
+    for copy in copies:
+        copy.wait()
+
+
+def cut_kernel(down_hbm, up_hbm, out_hbm, down_ref, up_ref, out_ref, sems):
     copies = [
         pltpu.make_async_copy(down_hbm, down_ref, sems.at[0]),
         pltpu.make_async_copy(up_hbm, up_ref, sems.at[1]),
@@ -105,7 +119,8 @@
                 axis=1,
             )
         )
-    out_ref[...] = dot(order, jnp.concatenate(parts, axis=0)).astype(BF)
+    parts = jnp.concatenate(parts, axis=0)
+    store_parts(lambda lanes: dot(order, parts[:, lanes]), out_ref, out_hbm, sems, 2)
 
 
 def slot_hits(tab_ref, part):
@@ -142,41 +157,39 @@
 
 
 def score_kernel(grad_ref, in_ref, hid_ref, extra_ref, mine_ref, out_ref):
-    own_up = jnp.zeros((128, TOK), F32)
-    own_down = jnp.zeros((128, TOK), F32)
-    extra_up = jnp.zeros((128, EXTRA), F32)
-    extra_down = jnp.zeros((128, EXTRA), F32)
+    up = jnp.zeros((TOK + EXTRA, 128), F32)
+    down = jnp.zeros((TOK + EXTRA, 128), F32)
     for q in range(4):
         lanes = slice(q * QH, (q + 1) * QH)
-        part = quarter(in_ref, q, slice(0, QH))
-        own_down += dot(part, hid_ref[:, lanes], 1, 1)
-        extra_down += dot(part, extra_ref[:, lanes], 1, 1)
-    for q in range(4):
+        tokens = jnp.concatenate([hid_ref[:, lanes], extra_ref[:, lanes]], axis=0)
+        down += dot(tokens, quarter(in_ref, q, slice(0, QH)), 1, 1)
         lanes = slice(q * QF, (q + 1) * QF)
-        part = quarter(in_ref, q, slice(QH, ROW))
-        own_up += dot(part, grad_ref[:, lanes], 1, 1)
-        extra_up += dot(part, extra_ref[:, HID + q * QF : HID + (q + 1) * QF], 1, 1)
-    own, extra = members(mine_ref)
+        behind = slice(HID + q * QF, HID + (q + 1) * QF)
+        tokens = jnp.concatenate([grad_ref[:, lanes], extra_ref[:, behind]], axis=0)
+        up += dot(tokens, quarter(in_ref, q, slice(QH, ROW)), 1, 1)
+    mine = mine_ref[:, : TOK + EXTRA].astype(F32).astype(BF)
+    mine = dot(mine, jnp.full((8, 128), 0.125, BF), 0, 0)
+    member = ((iota((TOK + EXTRA, 128), 1) >> 1) & 7).astype(F32) == mine
     fold = jnp.where(rank_rows(), 1.0, 0.0)
-
-    def folded(member, up, down):
-        return [
+    rows = jnp.concatenate(
+        [
             lax.dot_general(
                 fold,
                 jnp.where(member, part, 0.0),
-                (((1,), (0,)), ((), ())),
+                (((1,), (1,)), ((), ())),
                 preferred_element_type=F32,
                 precision=lax.Precision.HIGHEST,
             )
             for part in (up, down)
-        ]
-
-    block = jnp.concatenate(folded(own, own_up, own_down), axis=0).astype(BF)
-    tail = jnp.concatenate(folded(extra, extra_up, extra_down), axis=0)
+        ],
+        axis=0,
+    )
+    block = rows.astype(BF)
+    tail = rows[:, TOK:]
     tail = jnp.concatenate([tail[i * 8 : i * 8 + 8, :] for i in range(4)], axis=1).astype(BF)
     for z in range(TP):
         out_ref[z * SIG : z * SIG + 32, :] = block[:, :128]
-        out_ref[z * SIG + 32 : z * SIG + 64, :] = block[:, 128:]
+        out_ref[z * SIG + 32 : z * SIG + 64, :] = block[:, 128:TOK]
         out_ref[z * SIG + 64 : (z + 1) * SIG, :] = tail
 
 
@@ -201,18 +214,19 @@
 
 
 def sum_kernel(grad_ref, sig_ref, hid_ref, extra_ref, mine_ref, out_ref):
-    up, up_extra = spread_signal(sig_ref, mine_ref, 0)
+    up = jnp.concatenate(spread_signal(sig_ref, mine_ref, 0), axis=1)
+    down = jnp.concatenate(spread_signal(sig_ref, mine_ref, RANK), axis=1)
     for q in range(4):
         lanes = slice(q * QH, (q + 1) * QH)
-        sums = dot(up, hid_ref[:, lanes]) + dot(up_extra, extra_ref[:, lanes])
+        tokens = jnp.concatenate([hid_ref[:, lanes], extra_ref[:, lanes]], axis=0)
+        sums = dot(up, tokens)
         for rp in range(8):
             at = (rp * 4 + q) * 16
             out_ref[at : at + 16, :QH] = sums[rp * 16 : rp * 16 + 16, :].astype(BF)
-    down, down_extra = spread_signal(sig_ref, mine_ref, RANK)
-    for q in range(4):
-        sums = dot(down, grad_ref[:, q * QF : (q + 1) * QF]) + dot(
-            down_extra, extra_ref[:, HID + q * QF : HID + (q + 1) * QF]
-        )
+        lanes = slice(q * QF, (q + 1) * QF)
+        behind = slice(HID + q * QF, HID + (q + 1) * QF)
+        tokens = jnp.concatenate([grad_ref[:, lanes], extra_ref[:, behind]], axis=0)
+        sums = dot(down, tokens)
         for rp in range(8):
             at = (rp * 4 + q) * 16
             out_ref[at : at + 16, QH:] = sums[rp * 16 : rp * 16 + 16, :].astype(BF)
@@ -247,11 +261,16 @@
         copy.wait()
 
 
-def reduce_kernel(tab_ref, in_ref, out_ref):
-    low = dot(slot_hits(tab_ref, 0), in_ref[:, :LO])
-    high = dot(slot_hits(tab_ref, 1), in_ref[:, LO:])
-    out_ref[:, :HI] = (low[:, :HI] + high).astype(BF)
-    out_ref[:, HI:] = low[:, HI:].astype(BF)
+def reduce_kernel(tab_ref, in_ref, out_hbm, out_ref, sems):
+    hits = [slot_hits(tab_ref, 0), slot_hits(tab_ref, 1)]
+
+    def value(lanes):
+        sums = dot(hits[0], in_ref[:, lanes])
+        if lanes.start < HI:
+            sums += dot(hits[1], in_ref[:, LO + lanes.start : LO + lanes.stop])
+        return sums
+
+    store_parts(value, out_ref, out_hbm, sems, 0)
 
 
 def join_kernel(
@@ -332,11 +351,13 @@
         [
             pltpu.VMEM((32, HID), BF),
             pltpu.VMEM((32, FEA), BF),
-            pltpu.SemaphoreType.DMA((2,)),
+            pltpu.VMEM((256, LO), BF),
+            pltpu.SemaphoreType.DMA((5,)),
         ],
         down,
         up,
         hbm_in=2,
+        hbm_out=1,
         limit=63_400_000,
     )
     pieces = exchange(cut, "dp", DP)
@@ -370,7 +391,14 @@
         mine,
         hbm_out=1,
     )
-    (slot_sums,) = call(reduce_kernel, [((256, LO), BF)], [], tab, gathered)
+    (slot_sums,) = call(
+        reduce_kernel,
+        [((256, LO), BF)],
+        [pltpu.VMEM((256, LO), BF), pltpu.SemaphoreType.DMA((3,))],
+        tab,
+        gathered,
+        hbm_out=1,
+    )
     owned = exchange(slot_sums, "dp", DP)
     hidden_gradient, down_gradient, up_gradient = call(
         join_kernel,

time: 107 us -> 107 us (level)
  no operation moved by 1% of the time
where the time goes in v6:
time: 107 us; the launch traced here: 106 us
  blocking collectives  40.9 us (38%)
  waiting for transfers between devices  26.8 us (25%)
  starting transfers between devices  22.2 us (21%)
  Pallas kernels  11.6 us (11%)
  local copies, waits for them, and re-layouts  2.99 us (3%)
    all_to_all x2, blocking collectives, exchange(): return lax.all_to_all(block, axis, 0, 0, tiled=True).reshape(x.shape)  40.9 us
    all_to_all x3, waiting for transfers between devices, exchange(): return lax.all_to_all(block, axis, 0, 0, tiled=True).reshape(x.shape)  21.8 us
    all_to_all x3, starting transfers between devices, exchange(): return lax.all_to_all(block, axis, 0, 0, tiled=True).reshape(x.shape)  16.4 us
    pallas_call x10, Pallas kernels, call(): pl.pallas_call(kernel, out_shape=[jax.ShapeDtypeStruct(s, t) for s, t in...  11.6 us
    ppermute x1, waiting for transfers between devices, on_device(): back = lax.ppermute(extra_gradient, 'dp', backward)  4.99 us
    ppermute x1, starting transfers between devices, on_device(): extra = lax.ppermute(last, 'dp', onward)  3.51 us
    unnamed x24, local copies, waits for them, and re-layouts  2.98 us
    ppermute x1, starting transfers between devices, on_device(): back = lax.ppermute(extra_gradient, 'dp', backward)  2.26 us
  transfers between devices with their start and end apart: 5, of which 4 were waited for; matrix products, arithmetic and copies ran while one was open for 1% of the time, Pallas kernels for 3%

profile of v6, /device:TPU:1, one launch (start us, length us, event | category | flops | bytes accessed | tf_op | source)
XLA Modules:
  0.0 105.9 jit_solution(15986992306141126450)
XLA Ops:
  0.6 0.0 copy-start.11
  0.6 0.0 copy-start.9
  0.7 0.0 copy-start.10
  0.7 1.9 %shard_map.95 = bf16[256,640]{1,0:T(8,128)(2,1)} custom-call(bf16[32,3584]{1,0:T(8,128)(2,1)} %bitcast.28, bf16[32,1024]{1,0:T(8,128)(2,1)} %bitcast.29), custom_call_target="tpu_custom_call" | custom-call | tf_op jit(solution)/shard_map/pallas_call | solution.py:322
  2.6 8.6 %all-to-all-start = ((bf16[32,8,640]{2,1,0:T(8,128)(2,1)}), bf16[32,8,640]{2,1,0:T(8,128)(2,1)S(1)}, u32[]{:S(2)}, u32[]{:S(2)}) async-start(bf16[32,8,640]{2,1,0:T(8,128)(2,1)} %bitcast.27), calls=%async_computation | async-start | bytes 655360 | tf_op jit(solution)/shard_map/all_to_all | solution.py:337
  11.2 1.0 shard_map.94
  12.3 0.0 copy-start.5
  12.3 0.6 copy-done.5
  12.9 0.6 copy-done.7
  13.5 7.3 %all-to-all-done = bf16[32,8,640]{2,1,0:T(8,128)(2,1)S(1)} async-done(((bf16[32,8,640]{2,1,0:T(8,128)(2,1)}), bf16[32,8,640]{2,1,0:T(8,128)(2,1)S(1)}, u32[]{:S(2)}, u32[]{:S(2)}) %all-to-all-start) | async-done | bytes 327712 | tf_op jit(solution)/shard_map/all_to_all | solution.py:337
  20.8 1.6 %shard_map.96 = bf16[512,1152]{1,0:T(8,128)(2,1)} custom-call(s32[8,512]{1,0:T(8,128)S(1)} %get-tuple-element.11.tab_ref, bf16[256,640]{1,0:T(8,128)(2,1)S(1)} %bitcast.25), custom_call_target="tpu_custom_call" | custom-call | tf_op jit(solution)/shard_map/pallas_call | solution.py:322
  22.5 3.9 %all-to-all-start.1 = ((bf16[32,16,1152]{2,1,0:T(8,128)(2,1)}), bf16[32,16,1152]{2,1,0:T(8,128)(2,1)S(1)}, u32[]{:S(2)}, u32[]{:S(2)}) async-start(bf16[32,16,1152]{2,1,0:T(8,128)(2,1)} %bitcast.5), calls=%async_computation.1 | async-start | bytes 2359296 | tf_op jit(solution)/shard_map/all_to_all | solution.py:337
  26.4 0.0 copy-start
  26.4 0.7 pad_maximum_fusion
  27.1 3.5 %collective-permute-start = (bf16[32,4608]{1,0:T(8,128)(2,1)}, bf16[32,4608]{1,0:T(8,128)(2,1)S(1)}, u32[]{:S(2)}, u32[]{:S(2)}) collective-permute-start(bf16[32,4608]{1,0:T(8,128)(2,1)} %pad_maximum_fusion), channel_id=1, source_target_pairs={{0,8},{8,16},{16,24},{24,32},{32,40},{40,48},{48,56},{56,64},{64,7... | collective-permute-start | bytes 884744 | tf_op jit(solution)/shard_map/ppermute | solution.py:345
  30.6 14.1 %all-to-all-done.1 = bf16[32,16,1152]{2,1,0:T(8,128)(2,1)S(1)} async-done(((bf16[32,16,1152]{2,1,0:T(8,128)(2,1)}), bf16[32,16,1152]{2,1,0:T(8,128)(2,1)S(1)}, u32[]{:S(2)}, u32[]{:S(2)}) %all-to-all-start.1) | async-done | bytes 1179680 | tf_op jit(solution)/shard_map/all_to_all | solution.py:337
  44.8 1.0 copy-done.1
  45.8 0.7 copy-done.8
  46.5 0.0 collective-permute-done.extra_ref
  46.5 1.3 %shard_map.98 = bf16[576,128]{1,0:T(8,128)(2,1)S(1)} custom-call(bf16[256,1024]{1,0:T(8,128)(2,1)S(1)} %copy-done.1, bf16[512,1152]{1,0:T(8,128)(2,1)S(1)} %bitcast.16, bf16[256,3584]{1,0:T(8,128)(2,1)S(1)} %copy-done, bf16[32,4608]{1,0:T(8,128)(2,1)S(1)} %collective-permute-done.extra_ref, s32[8,384]{1,0:T(8,128)S(1)} %shard_map.97.mine_ref), custom_call_target="tpu_custom_call" | custom-call | tf_op jit(solution)/shard_map/pallas_call | solution.py:322
  47.8 16.7 %all_to_all.25 = bf16[8,72,128]{2,1,0:T(8,128)(2,1)S(1)} all-to-all(bf16[8,72,128]{2,1,0:T(8,128)(2,1)S(1)} %bitcast.26), channel_id=1, replica_groups=mesh['dp'=32,'tensor'=8] {'tensor'}, dimensions={0} | all-to-all | bytes 294912 | tf_op jit(solution)/shard_map/all_to_all | solution.py:337
  64.5 1.0 shard_map.100
  65.6 24.2 %all_to_all.26 = bf16[32,16,1152]{2,1,0:T(8,128)(2,1)S(1)} all-to-all(bf16[32,16,1152]{2,1,0:T(8,128)(2,1)S(1)} %bitcast.19), channel_id=1, replica_groups=mesh['dp'=32,'tensor'=8] {'dp'}, dimensions={0} | all-to-all | bytes 2359296 | tf_op jit(solution)/shard_map/all_to_all | solution.py:337
  89.8 1.2 %shard_map.101 = bf16[256,640]{1,0:T(8,128)(2,1)} custom-call(s32[8,512]{1,0:T(8,128)S(1)} %copy-done.4, bf16[512,1152]{1,0:T(8,128)(2,1)S(1)} %bitcast.20), custom_call_target="tpu_custom_call" | custom-call | tf_op jit(solution)/shard_map/pallas_call | solution.py:322
  91.0 3.9 %all-to-all-start.4 = ((bf16[32,8,640]{2,1,0:T(8,128)(2,1)}), bf16[32,8,640]{2,1,0:T(8,128)(2,1)S(1)}, u32[]{:S(2)}, u32[]{:S(2)}) async-start(bf16[32,8,640]{2,1,0:T(8,128)(2,1)} %bitcast.11), calls=%async_computation.4 | async-start | bytes 655360 | tf_op jit(solution)/shard_map/all_to_all | solution.py:337
  94.9 0.0 copy-start.6
  94.9 0.5 shard_map.102
  95.4 2.3 %collective-permute-start.1 = (bf16[32,3584]{1,0:T(8,128)(2,1)S(1)}, bf16[32,3584]{1,0:T(8,128)(2,1)S(1)}, u32[]{:S(2)}, u32[]{:S(2)}) collective-permute-start(bf16[32,3584]{1,0:T(8,128)(2,1)S(1)} %shard_map.102), channel_id=1, source_target_pairs={{8,0},{16,8},{24,16},{32,24},{40,32},{48,40},{56,48},{64,56},{72,6... | collective-permute-start | bytes 688136 | tf_op jit(solution)/shard_map/ppermute | solution.py:384
  97.7 1.7 %shard_map.99 = (bf16[256,3584]{1,0:T(8,128)(2,1)}, bf16[32,3584]{1,0:T(8,128)(2,1)S(1)}) custom-call(bf16[576,128]{1,0:T(8,128)(2,1)S(1)} %bitcast.23, bf16[512,1152]{1,0:T(8,128)(2,1)S(1)} %bitcast.18, s32[8,384]{1,0:T(8,128)S(1)} %shard_map.97.mine_ref), custom_call_target="tpu_custom_call" | custom-call | tf_op jit(solution)/shard_map/pallas_call | solution.py:322
  99.4 5.0 %collective-permute-done.1.back_ref = bf16[32,3584]{1,0:T(8,128)(2,1)S(1)} collective-permute-done((bf16[32,3584]{1,0:T(8,128)(2,1)S(1)}, bf16[32,3584]{1,0:T(8,128)(2,1)S(1)}, u32[]{:S(2)}, u32[]{:S(2)}) %collective-permute-start.1) | collective-permute-done | bytes 229408 | tf_op jit(solution)/shard_map/ppermute | solution.py:384
  104.4 0.3 all-to-all-done.4
  104.7 1.3 %shard_map.103 = (bf16[256,3584]{1,0:T(8,128)(2,1)}, f32[32,3584]{1,0:T(8,128)}, f32[32,1024]{1,0:T(8,128)}) custom-call(bf16[256,3584]{1,0:T(8,128)(2,1)} %get-tuple-element.13.head_hbm, f32[32,128]{1,0:T(8,128)S(1)} %copy-done.6, bf16[256,640]{1,0:T(8,128)(2,1)S(1)} %bitcast.24, ...), custom_call_target="tpu_custom_call", output_to_operand_aliasing={{0}: (0, {})} | custom-call | tf_op jit(solution)/shard_map/pallas_call | solution.py:322
  (19 shorter events, 0.0 us)
Async XLA Ops:
  0.6 10.6 %copy-start.11 = (s32[64]{0:T(128)S(1)}, s32[64]{0:T(128)}, u32[]{:S(2)}) copy-start(s32[64]{0:T(128)} %slot_ref.1) | copy-start | bytes 772
  0.6 10.6 %copy-start.9 = (s32[64]{0:T(128)S(1)}, s32[64]{0:T(128)}, u32[]{:S(2)}) copy-start(s32[64]{0:T(128)} %off_ref.1) | copy-start | bytes 772
  0.7 10.6 %copy-start.10 = (s32[64]{0:T(128)S(1)}, s32[64]{0:T(128)}, u32[]{:S(2)}) copy-start(s32[64]{0:T(128)} %cnt_ref.1) | copy-start | bytes 772
  2.6 18.2 %all-to-all-start = ((bf16[32,8,640]{2,1,0:T(8,128)(2,1)}), bf16[32,8,640]{2,1,0:T(8,128)(2,1)S(1)}, u32[]{:S(2)}, u32[]{:S(2)}) async-start(bf16[32,8,640]{2,1,0:T(8,128)(2,1)} %bitcast.27), calls=%async_computation | async-start | bytes 655360 | tf_op jit(solution)/shard_map/all_to_all | solution.py:337
  12.3 0.6 copy-start.5
  12.9 0.6 copy-start.7
  13.5 9.0 %copy-start.3 = (s32[8,512]{1,0:T(8,128)}, s32[8,512]{1,0:T(8,128)S(1)}, u32[]{:S(2)}) copy-start(s32[8,512]{1,0:T(8,128)S(1)} %get-tuple-element.11.tab_ref) | copy-start | bytes 49156
  22.5 3.9 %slice-start = ((bf16[256,3584]{1,0:T(8,128)(2,1)}), bf16[32,3584]{1,0:T(8,128)(2,1)S(1)}, s32[]{:S(2)}) async-start(bf16[256,3584]{1,0:T(8,128)(2,1)} %hid_ref.3), calls=%async_computation.5 | async-start | bytes 458752 | tf_op jit(solution)/shard_map/slice | solution.py:344
  22.5 3.9 %slice-start.1 = ((bf16[256,1024]{1,0:T(8,128)(2,1)}), bf16[32,1024]{1,0:T(8,128)(2,1)S(1)}, s32[]{:S(2)}) async-start(bf16[256,1024]{1,0:T(8,128)(2,1)} %grad_ref.5), calls=%async_computation.6 | async-start | bytes 131072 | tf_op jit(solution)/shard_map/slice | solution.py:344
  22.5 22.3 %all-to-all-start.1 = ((bf16[32,16,1152]{2,1,0:T(8,128)(2,1)}), bf16[32,16,1152]{2,1,0:T(8,128)(2,1)S(1)}, u32[]{:S(2)}, u32[]{:S(2)}) async-start(bf16[32,16,1152]{2,1,0:T(8,128)(2,1)} %bitcast.5), calls=%async_computation.1 | async-start | bytes 2359296 | tf_op jit(solution)/shard_map/all_to_all | solution.py:337
  26.4 20.2 %copy-start = (bf16[256,3584]{1,0:T(8,128)(2,1)S(1)}, bf16[256,3584]{1,0:T(8,128)(2,1)}, u32[]{:S(2)}) copy-start(bf16[256,3584]{1,0:T(8,128)(2,1)} %hid_ref.3) | copy-start | bytes 5505028
  27.1 19.4 %collective-permute-start = (bf16[32,4608]{1,0:T(8,128)(2,1)}, bf16[32,4608]{1,0:T(8,128)(2,1)S(1)}, u32[]{:S(2)}, u32[]{:S(2)}) collective-permute-start(bf16[32,4608]{1,0:T(8,128)(2,1)} %pad_maximum_fusion), channel_id=1, source_target_pairs={{0,8},{8,16},{16,24},{24,32},{32,40},{40,48},{48,56},{56,64},{64,7... | collective-permute-start | bytes 884744 | tf_op jit(solution)/shard_map/ppermute | solution.py:345
  44.8 1.0 copy-start.1
  45.8 0.7 copy-start.8
  46.5 18.0 %copy-start.2 = (bf16[256,1024]{1,0:T(8,128)(2,1)S(1)}, bf16[256,1024]{1,0:T(8,128)(2,1)}, u32[]{:S(2)}) copy-start(bf16[256,1024]{1,0:T(8,128)(2,1)} %grad_ref.5) | copy-start | bytes 1572868
  65.6 24.2 %copy-start.4 = (s32[8,512]{1,0:T(8,128)S(1)}, s32[8,512]{1,0:T(8,128)}, u32[]{:S(2)}) copy-start(s32[8,512]{1,0:T(8,128)} %copy-done.3) | copy-start | bytes 49156
  91.0 13.7 %all-to-all-start.4 = ((bf16[32,8,640]{2,1,0:T(8,128)(2,1)}), bf16[32,8,640]{2,1,0:T(8,128)(2,1)S(1)}, u32[]{:S(2)}, u32[]{:S(2)}) async-start(bf16[32,8,640]{2,1,0:T(8,128)(2,1)} %bitcast.11), calls=%async_computation.4 | async-start | bytes 655360 | tf_op jit(solution)/shard_map/all_to_all | solution.py:337
  94.9 9.7 %copy-start.6 = (f32[32,128]{1,0:T(8,128)S(1)}, f32[32,128]{1,0:T(8,128)}, u32[]{:S(2)}) copy-start(f32[32,128]{1,0:T(8,128)} %copy-done.5) | copy-start | bytes 49156
  95.4 8.9 %collective-permute-start.1 = (bf16[32,3584]{1,0:T(8,128)(2,1)S(1)}, bf16[32,3584]{1,0:T(8,128)(2,1)S(1)}, u32[]{:S(2)}, u32[]{:S(2)}) collective-permute-start(bf16[32,3584]{1,0:T(8,128)(2,1)S(1)} %shard_map.102), channel_id=1, source_target_pairs={{8,0},{16,8},{24,16},{32,24},{40,32},{48,40},{56,48},{64,56},{72,6... | collective-permute-start | bytes 688136 | tf_op jit(solution)/shard_map/ppermute | solution.py:384

commit v7 on v6

--- a/solution.py
+++ b/solution.py
@@ -39,7 +39,23 @@
     return lax.dot_general(a, b, (((ca,), (cb,)), ((), ())), preferred_element_type=F32)
 
 
-def tables_kernel(dp_ref, off_ref, cnt_ref, slot_ref, tab_ref, mine_ref, scale_ref):
+def travel_order(axis):
+    i = iota((256, 256), 1 - axis)
+    j = iota((256, 256), axis)
+    rp, q, s, r, h = i >> 5, (i >> 3) & 3, (i >> 2) & 1, (i >> 1) & 1, i & 1
+    return one_hot(j == q * 64 + h * 32 + s * 16 + rp * 2 + r)
+
+
+def slot_hits(tab, shape, axis, part):
+    c = iota(shape, axis)
+    i = iota(shape, 1 - axis)
+    hit = ((i >> 2).astype(F32) == tab) & (((i >> 1) & 1) == (c & 1)) & ((i & 1) == part)
+    return one_hot(hit)
+
+
+def tables_kernel(
+    dp_ref, off_ref, cnt_ref, slot_ref, pick_ref, reduce_ref, order_ref, mine_ref, scale_ref
+):
     dp = dp_ref[0]
     i = iota((8, 512), 1)
     first = (i >> 4) * TOK
@@ -68,18 +84,16 @@
 
     init = (jnp.full((8, 512), -1, I32), jnp.zeros((8, 384), I32), jnp.int32(1), jnp.int32(1))
     tab, mine, c0, c1 = lax.fori_loop(0, SLOTS, collect, init, unroll=8)
-    tab_ref[...] = tab
+    column = dot(tab.astype(F32).astype(BF), jnp.full((8, 256), 0.125, BF), 0, 0)
+    row = tab[0:1, :].astype(F32)
+    for part in range(2):
+        pick_ref[part * 512 : (part + 1) * 512, :] = slot_hits(column, (512, 256), 0, part)
+        reduce_ref[part * 256 : (part + 1) * 256, :] = slot_hits(row, (256, 512), 1, part)
+    order_ref[...] = travel_order(0)
     extra = (p < TOK + EXTRA) & (mine == 8)
     mine_ref[...] = jnp.where(own, mine, jnp.where(extra, 0, -1))
     rows = iota((32, 128), 0)
     scale_ref[...] = adapter_factor / jnp.where(rows < 16, c0, c1).astype(F32)
-
-
-def travel_order(first, count):
-    i = iota((256, count), 0)
-    j = iota((256, count), 1) + first
-    rp, q, s, r, h = i >> 5, (i >> 3) & 3, (i >> 2) & 1, (i >> 1) & 1, i & 1
-    return one_hot(j == q * 64 + h * 32 + s * 16 + rp * 2 + r)
 
 
 def store_parts(value, out_ref, out_hbm, sems, first):
@@ -103,7 +117,7 @@
     ]
     for copy in copies:
         copy.start()
-    order = travel_order(0, 256)
+    order = travel_order(1)
     for copy in copies:
         copy.wait()
     parts = []
@@ -123,15 +137,9 @@
     store_parts(lambda lanes: dot(order, parts[:, lanes]), out_ref, out_hbm, sems, 2)
 
 
-def slot_hits(tab_ref, part):
-    i = iota((256, 512), 0)
-    r = iota((256, 512), 1) & 1
-    return one_hot(((i >> 2) == tab_ref[0:1, :]) & (((i >> 1) & 1) == r) & ((i & 1) == part))
-
-
-def pick_kernel(tab_ref, in_ref, out_ref):
-    out_ref[:, :LO] = dot(slot_hits(tab_ref, 0), in_ref[...], 0, 0).astype(BF)
-    out_ref[:, LO:] = dot(slot_hits(tab_ref, 1), in_ref[:, :HI], 0, 0).astype(BF)
+def pick_kernel(hits_ref, in_ref, out_ref):
+    out_ref[:, :LO] = dot(hits_ref[:512, :], in_ref[...]).astype(BF)
+    out_ref[:, LO:] = dot(hits_ref[512:, :], in_ref[:, :HI]).astype(BF)
 
 
 def quarter(ref, q, lanes):
@@ -261,13 +269,11 @@
         copy.wait()
 
 
-def reduce_kernel(tab_ref, in_ref, out_hbm, out_ref, sems):
-    hits = [slot_hits(tab_ref, 0), slot_hits(tab_ref, 1)]
-
+def reduce_kernel(hits_ref, in_ref, out_hbm, out_ref, sems):
     def value(lanes):
-        sums = dot(hits[0], in_ref[:, lanes])
+        sums = dot(hits_ref[:256, :], in_ref[:, lanes])
         if lanes.start < HI:
-            sums += dot(hits[1], in_ref[:, LO + lanes.start : LO + lanes.stop])
+            sums += dot(hits_ref[256:, :], in_ref[:, LO + lanes.start : LO + lanes.stop])
         return sums
 
     store_parts(value, out_ref, out_hbm, sems, 0)
@@ -276,6 +282,7 @@
 def join_kernel(
     head_hbm,
     scale_ref,
+    order_ref,
     in_ref,
     tail_ref,
     back_ref,
@@ -295,11 +302,10 @@
     ]
     copies[0].start()
     scale = scale_ref[:, 0:1]
-    pieces = in_ref[...]
-    for q in range(4):
-        rows = dot(travel_order(q * 64, 64), pieces, 0, 0)
-        low = rows[:32, :] * scale
-        high = rows[32:, :] * scale
+    rows = dot(order_ref[...], in_ref[...])
+    for q in range(4):
+        low = rows[q * 64 : q * 64 + 32, :] * scale
+        high = rows[q * 64 + 32 : q * 64 + 64, :] * scale
         down_ref[:, q * QH : q * QH + LO] = low
         down_ref[:, q * QH + LO : (q + 1) * QH] = high[:, : QH - LO]
         up_ref[:, q * QF : (q + 1) * QF] = high[:, QH - LO : HI]
@@ -361,9 +367,15 @@
         limit=63_400_000,
     )
     pieces = exchange(cut, "dp", DP)
-    tab, mine, scale = call(
+    pick_hits, reduce_hits, order, mine, scale = call(
         tables_kernel,
-        [((8, 512), I32), ((8, 384), I32), ((32, 128), F32)],
+        [
+            ((1024, 256), BF),
+            ((512, 512), BF),
+            ((256, 256), BF),
+            ((8, 384), I32),
+            ((32, 128), F32),
+        ],
         [],
         dp,
         offsets,
@@ -372,7 +384,7 @@
         smem=4,
     )
     block = ((512, ROW), BF)
-    (picked,) = call(pick_kernel, [block], [], tab, pieces)
+    (picked,) = call(pick_kernel, [block], [], pick_hits, pieces)
     local = exchange(picked, "dp", DP)
     (mine,) = call(mark_kernel, [((8, 384), I32)], [], local, mine, output_gradient, any_in=1)
     tokens = (hidden, extra, mine)
@@ -395,7 +407,7 @@
         reduce_kernel,
         [((256, LO), BF)],
         [pltpu.VMEM((256, LO), BF), pltpu.SemaphoreType.DMA((3,))],
-        tab,
+        reduce_hits,
         gathered,
         hbm_out=1,
     )
@@ -411,6 +423,7 @@
         ],
         head,
         scale,
+        order,
         owned,
         tail,
         back,

time: 107 us -> 106 us (level)
  waiting for transfers between devices: 26.8 us -> 24.9 us
  local copies, waits for them, and re-layouts: 2.99 us -> 4.47 us
    all_to_all x3, waiting for transfers between devices: 21.8 us -> 19.9 us  [exchange(): return lax.all_to_all(block, axis, 0, 0, tiled=True).reshape(x.shape)]
    unnamed x24 -> x28, local copies, waits for them, and re-layouts: 2.98 us -> 4.46 us
where the time goes in v7:
time: 106 us
  blocking collectives  41 us (39%)
  waiting for transfers between devices  24.9 us (23%)
  starting transfers between devices  22.1 us (21%)
  Pallas kernels  11.7 us (11%)
  local copies, waits for them, and re-layouts  4.47 us (4%)
    all_to_all x2, blocking collectives, exchange(): return lax.all_to_all(block, axis, 0, 0, tiled=True).reshape(x.shape)  41 us
    all_to_all x3, waiting for transfers between devices, exchange(): return lax.all_to_all(block, axis, 0, 0, tiled=True).reshape(x.shape)  19.9 us
    all_to_all x3, starting transfers between devices, exchange(): return lax.all_to_all(block, axis, 0, 0, tiled=True).reshape(x.shape)  16.4 us
    pallas_call x10, Pallas kernels, call(): pl.pallas_call(kernel, out_shape=[jax.ShapeDtypeStruct(s, t) for s, t in...  11.7 us
    ppermute x1, waiting for transfers between devices, on_device(): back = lax.ppermute(extra_gradient, 'dp', backward)  4.98 us
    unnamed x28, local copies, waits for them, and re-layouts  4.46 us
    ppermute x1, starting transfers between devices, on_device(): extra = lax.ppermute(last, 'dp', onward)  3.51 us
    ppermute x1, starting transfers between devices, on_device(): back = lax.ppermute(extra_gradient, 'dp', backward)  2.26 us
  transfers between devices with their start and end apart: 5, of which 4 were waited for; matrix products, arithmetic and copies ran while one was open for 1% of the time, Pallas kernels for 3%

profile of v7, /device:TPU:1, one launch (start us, length us, event | category | flops | bytes accessed | tf_op | source)
XLA Modules:
  0.0 105.8 jit_solution(17042698550114631871)
XLA Ops:
  0.6 0.0 copy-start.13
  0.6 0.0 copy-start.11
  0.7 1.9 %shard_map.95 = bf16[256,640]{1,0:T(8,128)(2,1)} custom-call(bf16[32,3584]{1,0:T(8,128)(2,1)} %bitcast.28, bf16[32,1024]{1,0:T(8,128)(2,1)} %bitcast.29), custom_call_target="tpu_custom_call" | custom-call | tf_op jit(solution)/shard_map/pallas_call | solution.py:328
  2.6 8.6 %all-to-all-start = ((bf16[32,8,640]{2,1,0:T(8,128)(2,1)}), bf16[32,8,640]{2,1,0:T(8,128)(2,1)S(1)}, u32[]{:S(2)}, u32[]{:S(2)}) async-start(bf16[32,8,640]{2,1,0:T(8,128)(2,1)} %bitcast.27), calls=%async_computation | async-start | bytes 655360 | tf_op jit(solution)/shard_map/all_to_all | solution.py:343
  11.2 1.4 %shard_map.94 = (bf16[1024,256]{1,0:T(8,128)(2,1)S(1)}, bf16[512,512]{1,0:T(8,128)(2,1)S(1)}, bf16[256,256]{1,0:T(8,128)(2,1)S(1)}, s32[8,384]{1,0:T(8,128)S(1)}, f32[32,128]{1,0:T(8,128)S(1)}) custom-call(s32[1]{0:T(128)} %bitcast.dp_ref, s32[64]{0:T(128)S(1)} %copy-done.11, s32[64]{0:T(128)S(1)} %copy-done.12, s32[64]{0:T(128)S(1)} %copy-done.13), custom_call_target="tpu_custom_call" | custom-call | tf_op jit(solution)/shard_map/pallas_call | solution.py:328
  12.7 0.8 copy-done.3
  13.5 0.7 copy-done.5
  14.1 0.6 copy-done.7
  14.7 0.6 copy-done.9
  15.3 5.5 %all-to-all-done = bf16[32,8,640]{2,1,0:T(8,128)(2,1)S(1)} async-done(((bf16[32,8,640]{2,1,0:T(8,128)(2,1)}), bf16[32,8,640]{2,1,0:T(8,128)(2,1)S(1)}, u32[]{:S(2)}, u32[]{:S(2)}) %all-to-all-start) | async-done | bytes 327712 | tf_op jit(solution)/shard_map/all_to_all | solution.py:343
  20.8 1.5 %shard_map.96 = bf16[512,1152]{1,0:T(8,128)(2,1)} custom-call(bf16[1024,256]{1,0:T(8,128)(2,1)S(1)} %get-tuple-element.13.hits_ref, bf16[256,640]{1,0:T(8,128)(2,1)S(1)} %bitcast.24), custom_call_target="tpu_custom_call" | custom-call | tf_op jit(solution)/shard_map/pallas_call | solution.py:328
  22.4 3.9 %all-to-all-start.1 = ((bf16[32,16,1152]{2,1,0:T(8,128)(2,1)}), bf16[32,16,1152]{2,1,0:T(8,128)(2,1)S(1)}, u32[]{:S(2)}, u32[]{:S(2)}) async-start(bf16[32,16,1152]{2,1,0:T(8,128)(2,1)} %bitcast.5), calls=%async_computation.1 | async-start | bytes 2359296 | tf_op jit(solution)/shard_map/all_to_all | solution.py:343
  26.2 0.0 copy-start
  26.3 0.7 pad_maximum_fusion
  27.0 3.5 %collective-permute-start = (bf16[32,4608]{1,0:T(8,128)(2,1)}, bf16[32,4608]{1,0:T(8,128)(2,1)S(1)}, u32[]{:S(2)}, u32[]{:S(2)}) collective-permute-start(bf16[32,4608]{1,0:T(8,128)(2,1)} %pad_maximum_fusion), channel_id=1, source_target_pairs={{0,8},{8,16},{16,24},{24,32},{32,40},{40,48},{48,56},{56,64},{64,7... | collective-permute-start | bytes 884744 | tf_op jit(solution)/shard_map/ppermute | solution.py:351
  30.5 14.1 %all-to-all-done.1 = bf16[32,16,1152]{2,1,0:T(8,128)(2,1)S(1)} async-done(((bf16[32,16,1152]{2,1,0:T(8,128)(2,1)}), bf16[32,16,1152]{2,1,0:T(8,128)(2,1)S(1)}, u32[]{:S(2)}, u32[]{:S(2)}) %all-to-all-start.1) | async-done | bytes 1179680 | tf_op jit(solution)/shard_map/all_to_all | solution.py:343
  44.7 1.0 copy-done.1
  45.7 0.7 copy-done.10
  46.4 0.0 collective-permute-done.extra_ref
  46.4 1.3 %shard_map.98 = bf16[576,128]{1,0:T(8,128)(2,1)S(1)} custom-call(bf16[256,1024]{1,0:T(8,128)(2,1)S(1)} %copy-done.1, bf16[512,1152]{1,0:T(8,128)(2,1)S(1)} %bitcast.16, bf16[256,3584]{1,0:T(8,128)(2,1)S(1)} %copy-done, bf16[32,4608]{1,0:T(8,128)(2,1)S(1)} %collective-permute-done.extra_ref, s32[8,384]{1,0:T(8,128)S(1)} %shard_map.97.mine_ref), custom_call_target="tpu_custom_call" | custom-call | tf_op jit(solution)/shard_map/pallas_call | solution.py:328
  47.7 16.7 %all_to_all.25 = bf16[8,72,128]{2,1,0:T(8,128)(2,1)S(1)} all-to-all(bf16[8,72,128]{2,1,0:T(8,128)(2,1)S(1)} %bitcast.26), channel_id=1, replica_groups=mesh['dp'=32,'tensor'=8] {'tensor'}, dimensions={0} | all-to-all | bytes 294912 | tf_op jit(solution)/shard_map/all_to_all | solution.py:343
  64.4 1.0 shard_map.100
  65.5 24.3 %all_to_all.26 = bf16[32,16,1152]{2,1,0:T(8,128)(2,1)S(1)} all-to-all(bf16[32,16,1152]{2,1,0:T(8,128)(2,1)S(1)} %bitcast.19), channel_id=1, replica_groups=mesh['dp'=32,'tensor'=8] {'dp'}, dimensions={0} | all-to-all | bytes 2359296 | tf_op jit(solution)/shard_map/all_to_all | solution.py:343
  89.8 1.2 %shard_map.101 = bf16[256,640]{1,0:T(8,128)(2,1)} custom-call(bf16[512,512]{1,0:T(8,128)(2,1)S(1)} %copy-done.4, bf16[512,1152]{1,0:T(8,128)(2,1)S(1)} %bitcast.20), custom_call_target="tpu_custom_call" | custom-call | tf_op jit(solution)/shard_map/pallas_call | solution.py:328
  91.0 3.9 %all-to-all-start.4 = ((bf16[32,8,640]{2,1,0:T(8,128)(2,1)}), bf16[32,8,640]{2,1,0:T(8,128)(2,1)S(1)}, u32[]{:S(2)}, u32[]{:S(2)}) async-start(bf16[32,8,640]{2,1,0:T(8,128)(2,1)} %bitcast.11), calls=%async_computation.4 | async-start | bytes 655360 | tf_op jit(solution)/shard_map/all_to_all | solution.py:343
  94.9 0.0 copy-start.6
  94.9 0.5 shard_map.102
  95.4 2.3 %collective-permute-start.1 = (bf16[32,3584]{1,0:T(8,128)(2,1)S(1)}, bf16[32,3584]{1,0:T(8,128)(2,1)S(1)}, u32[]{:S(2)}, u32[]{:S(2)}) collective-permute-start(bf16[32,3584]{1,0:T(8,128)(2,1)S(1)} %shard_map.102), channel_id=1, source_target_pairs={{8,0},{16,8},{24,16},{32,24},{40,32},{48,40},{56,48},{64,56},{72,6... | collective-permute-start | bytes 688136 | tf_op jit(solution)/shard_map/ppermute | solution.py:396
  97.7 1.7 %shard_map.99 = (bf16[256,3584]{1,0:T(8,128)(2,1)}, bf16[32,3584]{1,0:T(8,128)(2,1)S(1)}) custom-call(bf16[576,128]{1,0:T(8,128)(2,1)S(1)} %bitcast.23, bf16[512,1152]{1,0:T(8,128)(2,1)S(1)} %bitcast.18, s32[8,384]{1,0:T(8,128)S(1)} %shard_map.97.mine_ref), custom_call_target="tpu_custom_call" | custom-call | tf_op jit(solution)/shard_map/pallas_call | solution.py:328
  99.4 5.0 %collective-permute-done.1.back_ref = bf16[32,3584]{1,0:T(8,128)(2,1)S(1)} collective-permute-done((bf16[32,3584]{1,0:T(8,128)(2,1)S(1)}, bf16[32,3584]{1,0:T(8,128)(2,1)S(1)}, u32[]{:S(2)}, u32[]{:S(2)}) %collective-permute-start.1) | collective-permute-done | bytes 229408 | tf_op jit(solution)/shard_map/ppermute | solution.py:396
  104.4 0.3 all-to-all-done.4
  104.6 1.2 %shard_map.103 = (bf16[256,3584]{1,0:T(8,128)(2,1)}, f32[32,3584]{1,0:T(8,128)}, f32[32,1024]{1,0:T(8,128)}) custom-call(bf16[256,3584]{1,0:T(8,128)(2,1)} %get-tuple-element.15.head_hbm, f32[32,128]{1,0:T(8,128)S(1)} %copy-done.8, bf16[256,256]{1,0:T(8,128)(2,1)S(1)} %copy-done.6, bf16[256,640]{1,0:T(8,128)(2,1)S(1)} %bitcast.25, ...), custom_call_target="tpu_custom_call", output_to_operand_aliasing={{0}: (0, {})} | custom-call | tf_op jit(solution)/shard_map/pallas_call | solution.py:328
  (23 shorter events, 0.0 us)
Async XLA Ops:
  0.6 10.6 %copy-start.13 = (s32[64]{0:T(128)S(1)}, s32[64]{0:T(128)}, u32[]{:S(2)}) copy-start(s32[64]{0:T(128)} %slot_ref.1) | copy-start | bytes 772
  0.6 10.6 %copy-start.11 = (s32[64]{0:T(128)S(1)}, s32[64]{0:T(128)}, u32[]{:S(2)}) copy-start(s32[64]{0:T(128)} %off_ref.1) | copy-start | bytes 772
  0.7 10.6 %copy-start.12 = (s32[64]{0:T(128)S(1)}, s32[64]{0:T(128)}, u32[]{:S(2)}) copy-start(s32[64]{0:T(128)} %cnt_ref.1) | copy-start | bytes 772
  2.6 18.2 %all-to-all-start = ((bf16[32,8,640]{2,1,0:T(8,128)(2,1)}), bf16[32,8,640]{2,1,0:T(8,128)(2,1)S(1)}, u32[]{:S(2)}, u32[]{:S(2)}) async-start(bf16[32,8,640]{2,1,0:T(8,128)(2,1)} %bitcast.27), calls=%async_computation | async-start | bytes 655360 | tf_op jit(solution)/shard_map/all_to_all | solution.py:343
  12.6 0.8 copy-start.3
  13.5 0.7 copy-start.5
  14.1 0.6 copy-start.7
  14.7 0.6 copy-start.9
  22.4 3.9 %slice-start = ((bf16[256,3584]{1,0:T(8,128)(2,1)}), bf16[32,3584]{1,0:T(8,128)(2,1)S(1)}, s32[]{:S(2)}) async-start(bf16[256,3584]{1,0:T(8,128)(2,1)} %hid_ref.3), calls=%async_computation.5 | async-start | bytes 458752 | tf_op jit(solution)/shard_map/slice | solution.py:350
  22.4 3.9 %slice-start.1 = ((bf16[256,1024]{1,0:T(8,128)(2,1)}), bf16[32,1024]{1,0:T(8,128)(2,1)S(1)}, s32[]{:S(2)}) async-start(bf16[256,1024]{1,0:T(8,128)(2,1)} %grad_ref.5), calls=%async_computation.6 | async-start | bytes 131072 | tf_op jit(solution)/shard_map/slice | solution.py:350
  22.4 22.3 %all-to-all-start.1 = ((bf16[32,16,1152]{2,1,0:T(8,128)(2,1)}), bf16[32,16,1152]{2,1,0:T(8,128)(2,1)S(1)}, u32[]{:S(2)}, u32[]{:S(2)}) async-start(bf16[32,16,1152]{2,1,0:T(8,128)(2,1)} %bitcast.5), calls=%async_computation.1 | async-start | bytes 2359296 | tf_op jit(solution)/shard_map/all_to_all | solution.py:343
  26.2 20.2 %copy-start = (bf16[256,3584]{1,0:T(8,128)(2,1)S(1)}, bf16[256,3584]{1,0:T(8,128)(2,1)}, u32[]{:S(2)}) copy-start(bf16[256,3584]{1,0:T(8,128)(2,1)} %hid_ref.3) | copy-start | bytes 5505028
  27.0 19.4 %collective-permute-start = (bf16[32,4608]{1,0:T(8,128)(2,1)}, bf16[32,4608]{1,0:T(8,128)(2,1)S(1)}, u32[]{:S(2)}, u32[]{:S(2)}) collective-permute-start(bf16[32,4608]{1,0:T(8,128)(2,1)} %pad_maximum_fusion), channel_id=1, source_target_pairs={{0,8},{8,16},{16,24},{24,32},{32,40},{40,48},{48,56},{56,64},{64,7... | collective-permute-start | bytes 884744 | tf_op jit(solution)/shard_map/ppermute | solution.py:351
  44.7 1.0 copy-start.1
  45.7 0.7 copy-start.10
  46.4 18.0 %copy-start.2 = (bf16[256,1024]{1,0:T(8,128)(2,1)S(1)}, bf16[256,1024]{1,0:T(8,128)(2,1)}, u32[]{:S(2)}) copy-start(bf16[256,1024]{1,0:T(8,128)(2,1)} %grad_ref.5) | copy-start | bytes 1572868
  65.5 24.3 %copy-start.4 = (bf16[512,512]{1,0:T(8,128)(2,1)S(1)}, bf16[512,512]{1,0:T(8,128)(2,1)}, u32[]{:S(2)}) copy-start(bf16[512,512]{1,0:T(8,128)(2,1)} %copy-done.3) | copy-start | bytes 1572868
  91.0 13.7 %all-to-all-start.4 = ((bf16[32,8,640]{2,1,0:T(8,128)(2,1)}), bf16[32,8,640]{2,1,0:T(8,128)(2,1)S(1)}, u32[]{:S(2)}, u32[]{:S(2)}) async-start(bf16[32,8,640]{2,1,0:T(8,128)(2,1)} %bitcast.11), calls=%async_computation.4 | async-start | bytes 655360 | tf_op jit(solution)/shard_map/all_to_all | solution.py:343
  94.9 9.7 %copy-start.6 = (bf16[256,256]{1,0:T(8,128)(2,1)S(1)}, bf16[256,256]{1,0:T(8,128)(2,1)}, u32[]{:S(2)}) copy-start(bf16[256,256]{1,0:T(8,128)(2,1)} %copy-done.5) | copy-start | bytes 393220
  94.9 9.7 %copy-start.8 = (f32[32,128]{1,0:T(8,128)S(1)}, f32[32,128]{1,0:T(8,128)}, u32[]{:S(2)}) copy-start(f32[32,128]{1,0:T(8,128)} %copy-done.7) | copy-start | bytes 49156
  95.4 8.9 %collective-permute-start.1 = (bf16[32,3584]{1,0:T(8,128)(2,1)S(1)}, bf16[32,3584]{1,0:T(8,128)(2,1)S(1)}, u32[]{:S(2)}, u32[]{:S(2)}) collective-permute-start(bf16[32,3584]{1,0:T(8,128)(2,1)S(1)} %shard_map.102), channel_id=1, source_target_pairs={{8,0},{16,8},{24,16},{32,24},{40,32},{48,40},{56,48},{64,56},{72,6... | collective-permute-start | bytes 688136 | tf_op jit(solution)/shard_map/ppermute | solution.py:396

commit v8 on v7

--- a/solution.py
+++ b/solution.py
@@ -369,13 +369,7 @@
     pieces = exchange(cut, "dp", DP)
     pick_hits, reduce_hits, order, mine, scale = call(
         tables_kernel,
-        [
-            ((1024, 256), BF),
-            ((512, 512), BF),
-            ((256, 256), BF),
-            ((8, 384), I32),
-            ((32, 128), F32),
-        ],
+        [((1024, 256), BF), ((512, 512), BF), ((256, 256), BF), ((8, 384), I32), ((32, 128), F32)],
         [],
         dp,
         offsets,

time: 106 us -> 106 us (level)
  no operation moved by 1% of the time
where the time goes in v8:
time: 106 us
  blocking collectives  41 us (39%)
  waiting for transfers between devices  24.9 us (23%)
  starting transfers between devices  22.1 us (21%)
  Pallas kernels  11.7 us (11%)
  local copies, waits for them, and re-layouts  4.47 us (4%)
    all_to_all x2, blocking collectives, exchange(): return lax.all_to_all(block, axis, 0, 0, tiled=True).reshape(x.shape)  41 us
    all_to_all x3, waiting for transfers between devices, exchange(): return lax.all_to_all(block, axis, 0, 0, tiled=True).reshape(x.shape)  19.9 us
    all_to_all x3, starting transfers between devices, exchange(): return lax.all_to_all(block, axis, 0, 0, tiled=True).reshape(x.shape)  16.4 us
    pallas_call x10, Pallas kernels, call(): pl.pallas_call(kernel, out_shape=[jax.ShapeDtypeStruct(s, t) for s, t in...  11.7 us
    ppermute x1, waiting for transfers between devices, on_device(): back = lax.ppermute(extra_gradient, 'dp', backward)  4.98 us
    unnamed x28, local copies, waits for them, and re-layouts  4.46 us
    ppermute x1, starting transfers between devices, on_device(): extra = lax.ppermute(last, 'dp', onward)  3.51 us
    ppermute x1, starting transfers between devices, on_device(): back = lax.ppermute(extra_gradient, 'dp', backward)  2.26 us
  transfers between devices with their start and end apart: 5, of which 4 were waited for; matrix products, arithmetic and copies ran while one was open for 1% of the time, Pallas kernels for 3%

profile of v8, /device:TPU:1, one launch (start us, length us, event | category | flops | bytes accessed | tf_op | source)
XLA Modules:
  0.0 105.8 jit_solution(17042698550114631871)
XLA Ops:
  0.6 0.0 copy-start.13
  0.6 0.0 copy-start.11
  0.7 1.9 %shard_map.95 = bf16[256,640]{1,0:T(8,128)(2,1)} custom-call(bf16[32,3584]{1,0:T(8,128)(2,1)} %bitcast.28, bf16[32,1024]{1,0:T(8,128)(2,1)} %bitcast.29), custom_call_target="tpu_custom_call" | custom-call | tf_op jit(solution)/shard_map/pallas_call | solution.py:328
  2.6 8.6 %all-to-all-start = ((bf16[32,8,640]{2,1,0:T(8,128)(2,1)}), bf16[32,8,640]{2,1,0:T(8,128)(2,1)S(1)}, u32[]{:S(2)}, u32[]{:S(2)}) async-start(bf16[32,8,640]{2,1,0:T(8,128)(2,1)} %bitcast.27), calls=%async_computation | async-start | bytes 655360 | tf_op jit(solution)/shard_map/all_to_all | solution.py:343
  11.2 1.4 %shard_map.94 = (bf16[1024,256]{1,0:T(8,128)(2,1)S(1)}, bf16[512,512]{1,0:T(8,128)(2,1)S(1)}, bf16[256,256]{1,0:T(8,128)(2,1)S(1)}, s32[8,384]{1,0:T(8,128)S(1)}, f32[32,128]{1,0:T(8,128)S(1)}) custom-call(s32[1]{0:T(128)} %bitcast.dp_ref, s32[64]{0:T(128)S(1)} %copy-done.11, s32[64]{0:T(128)S(1)} %copy-done.12, s32[64]{0:T(128)S(1)} %copy-done.13), custom_call_target="tpu_custom_call" | custom-call | tf_op jit(solution)/shard_map/pallas_call | solution.py:328
  12.7 0.8 copy-done.3
  13.5 0.7 copy-done.5
  14.1 0.6 copy-done.7
  14.7 0.6 copy-done.9
  15.3 5.5 %all-to-all-done = bf16[32,8,640]{2,1,0:T(8,128)(2,1)S(1)} async-done(((bf16[32,8,640]{2,1,0:T(8,128)(2,1)}), bf16[32,8,640]{2,1,0:T(8,128)(2,1)S(1)}, u32[]{:S(2)}, u32[]{:S(2)}) %all-to-all-start) | async-done | bytes 327712 | tf_op jit(solution)/shard_map/all_to_all | solution.py:343
  20.8 1.5 %shard_map.96 = bf16[512,1152]{1,0:T(8,128)(2,1)} custom-call(bf16[1024,256]{1,0:T(8,128)(2,1)S(1)} %get-tuple-element.13.hits_ref, bf16[256,640]{1,0:T(8,128)(2,1)S(1)} %bitcast.24), custom_call_target="tpu_custom_call" | custom-call | tf_op jit(solution)/shard_map/pallas_call | solution.py:328
  22.4 3.9 %all-to-all-start.1 = ((bf16[32,16,1152]{2,1,0:T(8,128)(2,1)}), bf16[32,16,1152]{2,1,0:T(8,128)(2,1)S(1)}, u32[]{:S(2)}, u32[]{:S(2)}) async-start(bf16[32,16,1152]{2,1,0:T(8,128)(2,1)} %bitcast.5), calls=%async_computation.1 | async-start | bytes 2359296 | tf_op jit(solution)/shard_map/all_to_all | solution.py:343
  26.2 0.0 copy-start
  26.3 0.7 pad_maximum_fusion
  27.0 3.5 %collective-permute-start = (bf16[32,4608]{1,0:T(8,128)(2,1)}, bf16[32,4608]{1,0:T(8,128)(2,1)S(1)}, u32[]{:S(2)}, u32[]{:S(2)}) collective-permute-start(bf16[32,4608]{1,0:T(8,128)(2,1)} %pad_maximum_fusion), channel_id=1, source_target_pairs={{0,8},{8,16},{16,24},{24,32},{32,40},{40,48},{48,56},{56,64},{64,7... | collective-permute-start | bytes 884744 | tf_op jit(solution)/shard_map/ppermute | solution.py:351
  30.5 14.1 %all-to-all-done.1 = bf16[32,16,1152]{2,1,0:T(8,128)(2,1)S(1)} async-done(((bf16[32,16,1152]{2,1,0:T(8,128)(2,1)}), bf16[32,16,1152]{2,1,0:T(8,128)(2,1)S(1)}, u32[]{:S(2)}, u32[]{:S(2)}) %all-to-all-start.1) | async-done | bytes 1179680 | tf_op jit(solution)/shard_map/all_to_all | solution.py:343
  44.7 1.0 copy-done.1
  45.7 0.7 copy-done.10
  46.4 0.0 collective-permute-done.extra_ref
  46.4 1.3 %shard_map.98 = bf16[576,128]{1,0:T(8,128)(2,1)S(1)} custom-call(bf16[256,1024]{1,0:T(8,128)(2,1)S(1)} %copy-done.1, bf16[512,1152]{1,0:T(8,128)(2,1)S(1)} %bitcast.16, bf16[256,3584]{1,0:T(8,128)(2,1)S(1)} %copy-done, bf16[32,4608]{1,0:T(8,128)(2,1)S(1)} %collective-permute-done.extra_ref, s32[8,384]{1,0:T(8,128)S(1)} %shard_map.97.mine_ref), custom_call_target="tpu_custom_call" | custom-call | tf_op jit(solution)/shard_map/pallas_call | solution.py:328
  47.7 16.7 %all_to_all.25 = bf16[8,72,128]{2,1,0:T(8,128)(2,1)S(1)} all-to-all(bf16[8,72,128]{2,1,0:T(8,128)(2,1)S(1)} %bitcast.26), channel_id=1, replica_groups=mesh['dp'=32,'tensor'=8] {'tensor'}, dimensions={0} | all-to-all | bytes 294912 | tf_op jit(solution)/shard_map/all_to_all | solution.py:343
  64.4 1.0 shard_map.100
  65.5 24.3 %all_to_all.26 = bf16[32,16,1152]{2,1,0:T(8,128)(2,1)S(1)} all-to-all(bf16[32,16,1152]{2,1,0:T(8,128)(2,1)S(1)} %bitcast.19), channel_id=1, replica_groups=mesh['dp'=32,'tensor'=8] {'dp'}, dimensions={0} | all-to-all | bytes 2359296 | tf_op jit(solution)/shard_map/all_to_all | solution.py:343
  89.8 1.2 %shard_map.101 = bf16[256,640]{1,0:T(8,128)(2,1)} custom-call(bf16[512,512]{1,0:T(8,128)(2,1)S(1)} %copy-done.4, bf16[512,1152]{1,0:T(8,128)(2,1)S(1)} %bitcast.20), custom_call_target="tpu_custom_call" | custom-call | tf_op jit(solution)/shard_map/pallas_call | solution.py:328
  91.0 3.9 %all-to-all-start.4 = ((bf16[32,8,640]{2,1,0:T(8,128)(2,1)}), bf16[32,8,640]{2,1,0:T(8,128)(2,1)S(1)}, u32[]{:S(2)}, u32[]{:S(2)}) async-start(bf16[32,8,640]{2,1,0:T(8,128)(2,1)} %bitcast.11), calls=%async_computation.4 | async-start | bytes 655360 | tf_op jit(solution)/shard_map/all_to_all | solution.py:343
  94.9 0.0 copy-start.6
  94.9 0.5 shard_map.102
  95.4 2.3 %collective-permute-start.1 = (bf16[32,3584]{1,0:T(8,128)(2,1)S(1)}, bf16[32,3584]{1,0:T(8,128)(2,1)S(1)}, u32[]{:S(2)}, u32[]{:S(2)}) collective-permute-start(bf16[32,3584]{1,0:T(8,128)(2,1)S(1)} %shard_map.102), channel_id=1, source_target_pairs={{8,0},{16,8},{24,16},{32,24},{40,32},{48,40},{56,48},{64,56},{72,6... | collective-permute-start | bytes 688136 | tf_op jit(solution)/shard_map/ppermute | solution.py:390
  97.7 1.7 %shard_map.99 = (bf16[256,3584]{1,0:T(8,128)(2,1)}, bf16[32,3584]{1,0:T(8,128)(2,1)S(1)}) custom-call(bf16[576,128]{1,0:T(8,128)(2,1)S(1)} %bitcast.23, bf16[512,1152]{1,0:T(8,128)(2,1)S(1)} %bitcast.18, s32[8,384]{1,0:T(8,128)S(1)} %shard_map.97.mine_ref), custom_call_target="tpu_custom_call" | custom-call | tf_op jit(solution)/shard_map/pallas_call | solution.py:328
  99.4 5.0 %collective-permute-done.1.back_ref = bf16[32,3584]{1,0:T(8,128)(2,1)S(1)} collective-permute-done((bf16[32,3584]{1,0:T(8,128)(2,1)S(1)}, bf16[32,3584]{1,0:T(8,128)(2,1)S(1)}, u32[]{:S(2)}, u32[]{:S(2)}) %collective-permute-start.1) | collective-permute-done | bytes 229408 | tf_op jit(solution)/shard_map/ppermute | solution.py:390
  104.4 0.3 all-to-all-done.4
  104.6 1.2 %shard_map.103 = (bf16[256,3584]{1,0:T(8,128)(2,1)}, f32[32,3584]{1,0:T(8,128)}, f32[32,1024]{1,0:T(8,128)}) custom-call(bf16[256,3584]{1,0:T(8,128)(2,1)} %get-tuple-element.15.head_hbm, f32[32,128]{1,0:T(8,128)S(1)} %copy-done.8, bf16[256,256]{1,0:T(8,128)(2,1)S(1)} %copy-done.6, bf16[256,640]{1,0:T(8,128)(2,1)S(1)} %bitcast.25, ...), custom_call_target="tpu_custom_call", output_to_operand_aliasing={{0}: (0, {})} | custom-call | tf_op jit(solution)/shard_map/pallas_call | solution.py:328
  (23 shorter events, 0.0 us)
Async XLA Ops:
  0.6 10.6 %copy-start.13 = (s32[64]{0:T(128)S(1)}, s32[64]{0:T(128)}, u32[]{:S(2)}) copy-start(s32[64]{0:T(128)} %slot_ref.1) | copy-start | bytes 772
  0.6 10.6 %copy-start.11 = (s32[64]{0:T(128)S(1)}, s32[64]{0:T(128)}, u32[]{:S(2)}) copy-start(s32[64]{0:T(128)} %off_ref.1) | copy-start | bytes 772
  0.7 10.6 %copy-start.12 = (s32[64]{0:T(128)S(1)}, s32[64]{0:T(128)}, u32[]{:S(2)}) copy-start(s32[64]{0:T(128)} %cnt_ref.1) | copy-start | bytes 772
  2.6 18.2 %all-to-all-start = ((bf16[32,8,640]{2,1,0:T(8,128)(2,1)}), bf16[32,8,640]{2,1,0:T(8,128)(2,1)S(1)}, u32[]{:S(2)}, u32[]{:S(2)}) async-start(bf16[32,8,640]{2,1,0:T(8,128)(2,1)} %bitcast.27), calls=%async_computation | async-start | bytes 655360 | tf_op jit(solution)/shard_map/all_to_all | solution.py:343
  12.6 0.8 copy-start.3
  13.5 0.7 copy-start.5
  14.1 0.6 copy-start.7
  14.7 0.6 copy-start.9
  22.4 3.9 %slice-start = ((bf16[256,3584]{1,0:T(8,128)(2,1)}), bf16[32,3584]{1,0:T(8,128)(2,1)S(1)}, s32[]{:S(2)}) async-start(bf16[256,3584]{1,0:T(8,128)(2,1)} %hid_ref.3), calls=%async_computation.5 | async-start | bytes 458752 | tf_op jit(solution)/shard_map/slice | solution.py:350
  22.4 3.9 %slice-start.1 = ((bf16[256,1024]{1,0:T(8,128)(2,1)}), bf16[32,1024]{1,0:T(8,128)(2,1)S(1)}, s32[]{:S(2)}) async-start(bf16[256,1024]{1,0:T(8,128)(2,1)} %grad_ref.5), calls=%async_computation.6 | async-start | bytes 131072 | tf_op jit(solution)/shard_map/slice | solution.py:350
  22.4 22.3 %all-to-all-start.1 = ((bf16[32,16,1152]{2,1,0:T(8,128)(2,1)}), bf16[32,16,1152]{2,1,0:T(8,128)(2,1)S(1)}, u32[]{:S(2)}, u32[]{:S(2)}) async-start(bf16[32,16,1152]{2,1,0:T(8,128)(2,1)} %bitcast.5), calls=%async_computation.1 | async-start | bytes 2359296 | tf_op jit(solution)/shard_map/all_to_all | solution.py:343
  26.2 20.2 %copy-start = (bf16[256,3584]{1,0:T(8,128)(2,1)S(1)}, bf16[256,3584]{1,0:T(8,128)(2,1)}, u32[]{:S(2)}) copy-start(bf16[256,3584]{1,0:T(8,128)(2,1)} %hid_ref.3) | copy-start | bytes 5505028
  27.0 19.4 %collective-permute-start = (bf16[32,4608]{1,0:T(8,128)(2,1)}, bf16[32,4608]{1,0:T(8,128)(2,1)S(1)}, u32[]{:S(2)}, u32[]{:S(2)}) collective-permute-start(bf16[32,4608]{1,0:T(8,128)(2,1)} %pad_maximum_fusion), channel_id=1, source_target_pairs={{0,8},{8,16},{16,24},{24,32},{32,40},{40,48},{48,56},{56,64},{64,7... | collective-permute-start | bytes 884744 | tf_op jit(solution)/shard_map/ppermute | solution.py:351
  44.7 1.0 copy-start.1
  45.7 0.7 copy-start.10
  46.4 18.0 %copy-start.2 = (bf16[256,1024]{1,0:T(8,128)(2,1)S(1)}, bf16[256,1024]{1,0:T(8,128)(2,1)}, u32[]{:S(2)}) copy-start(bf16[256,1024]{1,0:T(8,128)(2,1)} %grad_ref.5) | copy-start | bytes 1572868
  65.5 24.3 %copy-start.4 = (bf16[512,512]{1,0:T(8,128)(2,1)S(1)}, bf16[512,512]{1,0:T(8,128)(2,1)}, u32[]{:S(2)}) copy-start(bf16[512,512]{1,0:T(8,128)(2,1)} %copy-done.3) | copy-start | bytes 1572868
  91.0 13.7 %all-to-all-start.4 = ((bf16[32,8,640]{2,1,0:T(8,128)(2,1)}), bf16[32,8,640]{2,1,0:T(8,128)(2,1)S(1)}, u32[]{:S(2)}, u32[]{:S(2)}) async-start(bf16[32,8,640]{2,1,0:T(8,128)(2,1)} %bitcast.11), calls=%async_computation.4 | async-start | bytes 655360 | tf_op jit(solution)/shard_map/all_to_all | solution.py:343
  94.9 9.7 %copy-start.6 = (bf16[256,256]{1,0:T(8,128)(2,1)S(1)}, bf16[256,256]{1,0:T(8,128)(2,1)}, u32[]{:S(2)}) copy-start(bf16[256,256]{1,0:T(8,128)(2,1)} %copy-done.5) | copy-start | bytes 393220
  94.9 9.7 %copy-start.8 = (f32[32,128]{1,0:T(8,128)S(1)}, f32[32,128]{1,0:T(8,128)}, u32[]{:S(2)}) copy-start(f32[32,128]{1,0:T(8,128)} %copy-done.7) | copy-start | bytes 49156
  95.4 8.9 %collective-permute-start.1 = (bf16[32,3584]{1,0:T(8,128)(2,1)S(1)}, bf16[32,3584]{1,0:T(8,128)(2,1)S(1)}, u32[]{:S(2)}, u32[]{:S(2)}) collective-permute-start(bf16[32,3584]{1,0:T(8,128)(2,1)S(1)} %shard_map.102), channel_id=1, source_target_pairs={{8,0},{16,8},{24,16},{32,24},{40,32},{48,40},{56,48},{64,56},{72,6... | collective-permute-start | bytes 688136 | tf_op jit(solution)/shard_map/ppermute | solution.py:390

commit v9 on v7

--- a/solution.py
+++ b/solution.py
@@ -178,20 +178,9 @@
     mine = mine_ref[:, : TOK + EXTRA].astype(F32).astype(BF)
     mine = dot(mine, jnp.full((8, 128), 0.125, BF), 0, 0)
     member = ((iota((TOK + EXTRA, 128), 1) >> 1) & 7).astype(F32) == mine
-    fold = jnp.where(rank_rows(), 1.0, 0.0)
-    rows = jnp.concatenate(
-        [
-            lax.dot_general(
-                fold,
-                jnp.where(member, part, 0.0),
-                (((1,), (1,)), ((), ())),
-                preferred_element_type=F32,
-                precision=lax.Precision.HIGHEST,
-            )
-            for part in (up, down)
-        ],
-        axis=0,
-    )
+    fold = one_hot(rank_rows())
+    rows = [dot(fold, jnp.where(member, part, 0.0).astype(BF), 1, 1) for part in (up, down)]
+    rows = jnp.concatenate(rows, axis=0)
     block = rows.astype(BF)
     tail = rows[:, TOK:]
     tail = jnp.concatenate([tail[i * 8 : i * 8 + 8, :] for i in range(4)], axis=1).astype(BF)
@@ -222,22 +211,25 @@
 
 
 def sum_kernel(grad_ref, sig_ref, hid_ref, extra_ref, mine_ref, out_ref):
-    up = jnp.concatenate(spread_signal(sig_ref, mine_ref, 0), axis=1)
-    down = jnp.concatenate(spread_signal(sig_ref, mine_ref, RANK), axis=1)
-    for q in range(4):
-        lanes = slice(q * QH, (q + 1) * QH)
-        tokens = jnp.concatenate([hid_ref[:, lanes], extra_ref[:, lanes]], axis=0)
-        sums = dot(up, tokens)
-        for rp in range(8):
-            at = (rp * 4 + q) * 16
-            out_ref[at : at + 16, :QH] = sums[rp * 16 : rp * 16 + 16, :].astype(BF)
-        lanes = slice(q * QF, (q + 1) * QF)
-        behind = slice(HID + q * QF, HID + (q + 1) * QF)
-        tokens = jnp.concatenate([grad_ref[:, lanes], extra_ref[:, behind]], axis=0)
-        sums = dot(down, tokens)
-        for rp in range(8):
-            at = (rp * 4 + q) * 16
-            out_ref[at : at + 16, QH:] = sums[rp * 16 : rp * 16 + 16, :].astype(BF)
+    for first, tokens_ref, lead, tiles, at_lane in (
+        (0, hid_ref, 0, QH // 128, 0),
+        (RANK, grad_ref, HID, QF // 128, QH),
+    ):
+        signal = jnp.concatenate(spread_signal(sig_ref, mine_ref, first), axis=1)
+        for n in range(tokens_ref.shape[1] // 256):
+            lanes = slice(n * 256, (n + 1) * 256)
+            behind = slice(lead + n * 256, lead + (n + 1) * 256)
+            tokens = jnp.concatenate([tokens_ref[:, lanes], extra_ref[:, behind]], axis=0)
+            sums = dot(signal, tokens)
+            for half in range(2):
+                q, tile = divmod(2 * n + half, tiles)
+                part = sums[:, half * 128 : (half + 1) * 128]
+                lane = at_lane + tile * 128
+                for rp in range(8):
+                    at = (rp * 4 + q) * 16
+                    out_ref[at : at + 16, lane : lane + 128] = part[
+                        rp * 16 : rp * 16 + 16, :
+                    ].astype(BF)
 
 
 def extra_kernel(sig_ref, in_ref, mine_ref, out_ref):

time: 106 us -> 106 us (level)
  no operation moved by 1% of the time
where the time goes in v9:
time: 106 us
  blocking collectives  41 us (39%)
  waiting for transfers between devices  24.9 us (23%)
  starting transfers between devices  22.1 us (21%)
  Pallas kernels  11.5 us (11%)
  local copies, waits for them, and re-layouts  4.47 us (4%)
    all_to_all x2, blocking collectives, exchange(): return lax.all_to_all(block, axis, 0, 0, tiled=True).reshape(x.shape)  41 us
    all_to_all x3, waiting for transfers between devices, exchange(): return lax.all_to_all(block, axis, 0, 0, tiled=True).reshape(x.shape)  19.9 us
    all_to_all x3, starting transfers between devices, exchange(): return lax.all_to_all(block, axis, 0, 0, tiled=True).reshape(x.shape)  16.4 us
    pallas_call x10, Pallas kernels, call(): pl.pallas_call(kernel, out_shape=[jax.ShapeDtypeStruct(s, t) for s, t in...  11.5 us
    ppermute x1, waiting for transfers between devices, on_device(): back = lax.ppermute(extra_gradient, 'dp', backward)  4.98 us
    unnamed x28, local copies, waits for them, and re-layouts  4.46 us
    ppermute x1, starting transfers between devices, on_device(): extra = lax.ppermute(last, 'dp', onward)  3.51 us
    ppermute x1, starting transfers between devices, on_device(): back = lax.ppermute(extra_gradient, 'dp', backward)  2.26 us
  transfers between devices with their start and end apart: 5, of which 4 were waited for; matrix products, arithmetic and copies ran while one was open for 1% of the time, Pallas kernels for 3%

profile of v9, /device:TPU:1, one launch (start us, length us, event | category | flops | bytes accessed | tf_op | source)
XLA Modules:
  0.0 105.6 jit_solution(10758065881667065108)
XLA Ops:
  0.6 0.0 copy-start.13
  0.6 0.0 copy-start.11
  0.7 1.9 %shard_map.95 = bf16[256,640]{1,0:T(8,128)(2,1)} custom-call(bf16[32,3584]{1,0:T(8,128)(2,1)} %bitcast.28, bf16[32,1024]{1,0:T(8,128)(2,1)} %bitcast.29), custom_call_target="tpu_custom_call" | custom-call | tf_op jit(solution)/shard_map/pallas_call | solution.py:320
  2.6 8.6 %all-to-all-start = ((bf16[32,8,640]{2,1,0:T(8,128)(2,1)}), bf16[32,8,640]{2,1,0:T(8,128)(2,1)S(1)}, u32[]{:S(2)}, u32[]{:S(2)}) async-start(bf16[32,8,640]{2,1,0:T(8,128)(2,1)} %bitcast.27), calls=%async_computation | async-start | bytes 655360 | tf_op jit(solution)/shard_map/all_to_all | solution.py:335
  11.2 1.4 %shard_map.94 = (bf16[1024,256]{1,0:T(8,128)(2,1)S(1)}, bf16[512,512]{1,0:T(8,128)(2,1)S(1)}, bf16[256,256]{1,0:T(8,128)(2,1)S(1)}, s32[8,384]{1,0:T(8,128)S(1)}, f32[32,128]{1,0:T(8,128)S(1)}) custom-call(s32[1]{0:T(128)} %bitcast.dp_ref, s32[64]{0:T(128)S(1)} %copy-done.11, s32[64]{0:T(128)S(1)} %copy-done.12, s32[64]{0:T(128)S(1)} %copy-done.13), custom_call_target="tpu_custom_call" | custom-call | tf_op jit(solution)/shard_map/pallas_call | solution.py:320
  12.7 0.8 copy-done.3
  13.5 0.7 copy-done.5
  14.1 0.6 copy-done.7
  14.7 0.6 copy-done.9
  15.3 5.5 %all-to-all-done = bf16[32,8,640]{2,1,0:T(8,128)(2,1)S(1)} async-done(((bf16[32,8,640]{2,1,0:T(8,128)(2,1)}), bf16[32,8,640]{2,1,0:T(8,128)(2,1)S(1)}, u32[]{:S(2)}, u32[]{:S(2)}) %all-to-all-start) | async-done | bytes 327712 | tf_op jit(solution)/shard_map/all_to_all | solution.py:335
  20.8 1.5 %shard_map.96 = bf16[512,1152]{1,0:T(8,128)(2,1)} custom-call(bf16[1024,256]{1,0:T(8,128)(2,1)S(1)} %get-tuple-element.13.hits_ref, bf16[256,640]{1,0:T(8,128)(2,1)S(1)} %bitcast.24), custom_call_target="tpu_custom_call" | custom-call | tf_op jit(solution)/shard_map/pallas_call | solution.py:320
  22.4 3.9 %all-to-all-start.1 = ((bf16[32,16,1152]{2,1,0:T(8,128)(2,1)}), bf16[32,16,1152]{2,1,0:T(8,128)(2,1)S(1)}, u32[]{:S(2)}, u32[]{:S(2)}) async-start(bf16[32,16,1152]{2,1,0:T(8,128)(2,1)} %bitcast.5), calls=%async_computation.1 | async-start | bytes 2359296 | tf_op jit(solution)/shard_map/all_to_all | solution.py:335
  26.2 0.0 copy-start
  26.3 0.7 pad_maximum_fusion
  27.0 3.5 %collective-permute-start = (bf16[32,4608]{1,0:T(8,128)(2,1)}, bf16[32,4608]{1,0:T(8,128)(2,1)S(1)}, u32[]{:S(2)}, u32[]{:S(2)}) collective-permute-start(bf16[32,4608]{1,0:T(8,128)(2,1)} %pad_maximum_fusion), channel_id=1, source_target_pairs={{0,8},{8,16},{16,24},{24,32},{32,40},{40,48},{48,56},{56,64},{64,7... | collective-permute-start | bytes 884744 | tf_op jit(solution)/shard_map/ppermute | solution.py:343
  30.5 14.1 %all-to-all-done.1 = bf16[32,16,1152]{2,1,0:T(8,128)(2,1)S(1)} async-done(((bf16[32,16,1152]{2,1,0:T(8,128)(2,1)}), bf16[32,16,1152]{2,1,0:T(8,128)(2,1)S(1)}, u32[]{:S(2)}, u32[]{:S(2)}) %all-to-all-start.1) | async-done | bytes 1179680 | tf_op jit(solution)/shard_map/all_to_all | solution.py:335
  44.7 1.0 copy-done.1
  45.7 0.7 copy-done.10
  46.4 0.0 collective-permute-done.extra_ref
  46.4 1.1 %shard_map.98 = bf16[576,128]{1,0:T(8,128)(2,1)S(1)} custom-call(bf16[256,1024]{1,0:T(8,128)(2,1)S(1)} %copy-done.1, bf16[512,1152]{1,0:T(8,128)(2,1)S(1)} %bitcast.16, bf16[256,3584]{1,0:T(8,128)(2,1)S(1)} %copy-done, bf16[32,4608]{1,0:T(8,128)(2,1)S(1)} %collective-permute-done.extra_ref, s32[8,384]{1,0:T(8,128)S(1)} %shard_map.97.mine_ref), custom_call_target="tpu_custom_call" | custom-call | tf_op jit(solution)/shard_map/pallas_call | solution.py:320
  47.5 16.7 %all_to_all.25 = bf16[8,72,128]{2,1,0:T(8,128)(2,1)S(1)} all-to-all(bf16[8,72,128]{2,1,0:T(8,128)(2,1)S(1)} %bitcast.26), channel_id=1, replica_groups=mesh['dp'=32,'tensor'=8] {'tensor'}, dimensions={0} | all-to-all | bytes 294912 | tf_op jit(solution)/shard_map/all_to_all | solution.py:335
  64.2 1.1 %shard_map.100 = bf16[512,1152]{1,0:T(8,128)(2,1)S(1)} custom-call(bf16[256,1024]{1,0:T(8,128)(2,1)S(1)} %copy-done.2, bf16[576,128]{1,0:T(8,128)(2,1)S(1)} %bitcast.21, bf16[256,3584]{1,0:T(8,128)(2,1)S(1)} %copy-done, bf16[32,4608]{1,0:T(8,128)(2,1)S(1)} %collective-permute-done.extra_ref, s32[8,384]{1,0:T(8,128)S(1)} %shard_map.97.mine_ref), custom_call_target="tpu_custom_call" | custom-call | tf_op jit(solution)/shard_map/pallas_call | solution.py:320
  65.3 24.3 %all_to_all.26 = bf16[32,16,1152]{2,1,0:T(8,128)(2,1)S(1)} all-to-all(bf16[32,16,1152]{2,1,0:T(8,128)(2,1)S(1)} %bitcast.19), channel_id=1, replica_groups=mesh['dp'=32,'tensor'=8] {'dp'}, dimensions={0} | all-to-all | bytes 2359296 | tf_op jit(solution)/shard_map/all_to_all | solution.py:335
  89.6 1.2 %shard_map.101 = bf16[256,640]{1,0:T(8,128)(2,1)} custom-call(bf16[512,512]{1,0:T(8,128)(2,1)S(1)} %copy-done.4, bf16[512,1152]{1,0:T(8,128)(2,1)S(1)} %bitcast.20), custom_call_target="tpu_custom_call" | custom-call | tf_op jit(solution)/shard_map/pallas_call | solution.py:320
  90.8 3.9 %all-to-all-start.4 = ((bf16[32,8,640]{2,1,0:T(8,128)(2,1)}), bf16[32,8,640]{2,1,0:T(8,128)(2,1)S(1)}, u32[]{:S(2)}, u32[]{:S(2)}) async-start(bf16[32,8,640]{2,1,0:T(8,128)(2,1)} %bitcast.11), calls=%async_computation.4 | async-start | bytes 655360 | tf_op jit(solution)/shard_map/all_to_all | solution.py:335
  94.7 0.0 copy-start.6
  94.7 0.5 shard_map.102
  95.2 2.3 %collective-permute-start.1 = (bf16[32,3584]{1,0:T(8,128)(2,1)S(1)}, bf16[32,3584]{1,0:T(8,128)(2,1)S(1)}, u32[]{:S(2)}, u32[]{:S(2)}) collective-permute-start(bf16[32,3584]{1,0:T(8,128)(2,1)S(1)} %shard_map.102), channel_id=1, source_target_pairs={{8,0},{16,8},{24,16},{32,24},{40,32},{48,40},{56,48},{64,56},{72,6... | collective-permute-start | bytes 688136 | tf_op jit(solution)/shard_map/ppermute | solution.py:388
  97.5 1.7 %shard_map.99 = (bf16[256,3584]{1,0:T(8,128)(2,1)}, bf16[32,3584]{1,0:T(8,128)(2,1)S(1)}) custom-call(bf16[576,128]{1,0:T(8,128)(2,1)S(1)} %bitcast.23, bf16[512,1152]{1,0:T(8,128)(2,1)S(1)} %bitcast.18, s32[8,384]{1,0:T(8,128)S(1)} %shard_map.97.mine_ref), custom_call_target="tpu_custom_call" | custom-call | tf_op jit(solution)/shard_map/pallas_call | solution.py:320
  99.2 5.0 %collective-permute-done.1.back_ref = bf16[32,3584]{1,0:T(8,128)(2,1)S(1)} collective-permute-done((bf16[32,3584]{1,0:T(8,128)(2,1)S(1)}, bf16[32,3584]{1,0:T(8,128)(2,1)S(1)}, u32[]{:S(2)}, u32[]{:S(2)}) %collective-permute-start.1) | collective-permute-done | bytes 229408 | tf_op jit(solution)/shard_map/ppermute | solution.py:388
  104.1 0.3 all-to-all-done.4
  104.4 1.2 %shard_map.103 = (bf16[256,3584]{1,0:T(8,128)(2,1)}, f32[32,3584]{1,0:T(8,128)}, f32[32,1024]{1,0:T(8,128)}) custom-call(bf16[256,3584]{1,0:T(8,128)(2,1)} %get-tuple-element.15.head_hbm, f32[32,128]{1,0:T(8,128)S(1)} %copy-done.8, bf16[256,256]{1,0:T(8,128)(2,1)S(1)} %copy-done.6, bf16[256,640]{1,0:T(8,128)(2,1)S(1)} %bitcast.25, ...), custom_call_target="tpu_custom_call", output_to_operand_aliasing={{0}: (0, {})} | custom-call | tf_op jit(solution)/shard_map/pallas_call | solution.py:320
  (23 shorter events, 0.0 us)
Async XLA Ops:
  0.6 10.6 %copy-start.13 = (s32[64]{0:T(128)S(1)}, s32[64]{0:T(128)}, u32[]{:S(2)}) copy-start(s32[64]{0:T(128)} %slot_ref.1) | copy-start | bytes 772
  0.6 10.6 %copy-start.11 = (s32[64]{0:T(128)S(1)}, s32[64]{0:T(128)}, u32[]{:S(2)}) copy-start(s32[64]{0:T(128)} %off_ref.1) | copy-start | bytes 772
  0.7 10.6 %copy-start.12 = (s32[64]{0:T(128)S(1)}, s32[64]{0:T(128)}, u32[]{:S(2)}) copy-start(s32[64]{0:T(128)} %cnt_ref.1) | copy-start | bytes 772
  2.6 18.2 %all-to-all-start = ((bf16[32,8,640]{2,1,0:T(8,128)(2,1)}), bf16[32,8,640]{2,1,0:T(8,128)(2,1)S(1)}, u32[]{:S(2)}, u32[]{:S(2)}) async-start(bf16[32,8,640]{2,1,0:T(8,128)(2,1)} %bitcast.27), calls=%async_computation | async-start | bytes 655360 | tf_op jit(solution)/shard_map/all_to_all | solution.py:335
  12.6 0.8 copy-start.3
  13.5 0.7 copy-start.5
  14.1 0.6 copy-start.7
  14.7 0.6 copy-start.9
  22.4 3.9 %slice-start = ((bf16[256,3584]{1,0:T(8,128)(2,1)}), bf16[32,3584]{1,0:T(8,128)(2,1)S(1)}, s32[]{:S(2)}) async-start(bf16[256,3584]{1,0:T(8,128)(2,1)} %hid_ref.3), calls=%async_computation.5 | async-start | bytes 458752 | tf_op jit(solution)/shard_map/slice | solution.py:342
  22.4 3.9 %slice-start.1 = ((bf16[256,1024]{1,0:T(8,128)(2,1)}), bf16[32,1024]{1,0:T(8,128)(2,1)S(1)}, s32[]{:S(2)}) async-start(bf16[256,1024]{1,0:T(8,128)(2,1)} %grad_ref.5), calls=%async_computation.6 | async-start | bytes 131072 | tf_op jit(solution)/shard_map/slice | solution.py:342
  22.4 22.3 %all-to-all-start.1 = ((bf16[32,16,1152]{2,1,0:T(8,128)(2,1)}), bf16[32,16,1152]{2,1,0:T(8,128)(2,1)S(1)}, u32[]{:S(2)}, u32[]{:S(2)}) async-start(bf16[32,16,1152]{2,1,0:T(8,128)(2,1)} %bitcast.5), calls=%async_computation.1 | async-start | bytes 2359296 | tf_op jit(solution)/shard_map/all_to_all | solution.py:335
  26.2 20.2 %copy-start = (bf16[256,3584]{1,0:T(8,128)(2,1)S(1)}, bf16[256,3584]{1,0:T(8,128)(2,1)}, u32[]{:S(2)}) copy-start(bf16[256,3584]{1,0:T(8,128)(2,1)} %hid_ref.3) | copy-start | bytes 5505028
  27.0 19.4 %collective-permute-start = (bf16[32,4608]{1,0:T(8,128)(2,1)}, bf16[32,4608]{1,0:T(8,128)(2,1)S(1)}, u32[]{:S(2)}, u32[]{:S(2)}) collective-permute-start(bf16[32,4608]{1,0:T(8,128)(2,1)} %pad_maximum_fusion), channel_id=1, source_target_pairs={{0,8},{8,16},{16,24},{24,32},{32,40},{40,48},{48,56},{56,64},{64,7... | collective-permute-start | bytes 884744 | tf_op jit(solution)/shard_map/ppermute | solution.py:343
  44.7 1.0 copy-start.1
  45.7 0.7 copy-start.10
  46.4 17.8 %copy-start.2 = (bf16[256,1024]{1,0:T(8,128)(2,1)S(1)}, bf16[256,1024]{1,0:T(8,128)(2,1)}, u32[]{:S(2)}) copy-start(bf16[256,1024]{1,0:T(8,128)(2,1)} %grad_ref.5) | copy-start | bytes 1572868
  65.3 24.3 %copy-start.4 = (bf16[512,512]{1,0:T(8,128)(2,1)S(1)}, bf16[512,512]{1,0:T(8,128)(2,1)}, u32[]{:S(2)}) copy-start(bf16[512,512]{1,0:T(8,128)(2,1)} %copy-done.3) | copy-start | bytes 1572868
  90.8 13.7 %all-to-all-start.4 = ((bf16[32,8,640]{2,1,0:T(8,128)(2,1)}), bf16[32,8,640]{2,1,0:T(8,128)(2,1)S(1)}, u32[]{:S(2)}, u32[]{:S(2)}) async-start(bf16[32,8,640]{2,1,0:T(8,128)(2,1)} %bitcast.11), calls=%async_computation.4 | async-start | bytes 655360 | tf_op jit(solution)/shard_map/all_to_all | solution.py:335
  94.7 9.7 %copy-start.6 = (bf16[256,256]{1,0:T(8,128)(2,1)S(1)}, bf16[256,256]{1,0:T(8,128)(2,1)}, u32[]{:S(2)}) copy-start(bf16[256,256]{1,0:T(8,128)(2,1)} %copy-done.5) | copy-start | bytes 393220
  94.7 9.7 %copy-start.8 = (f32[32,128]{1,0:T(8,128)S(1)}, f32[32,128]{1,0:T(8,128)}, u32[]{:S(2)}) copy-start(f32[32,128]{1,0:T(8,128)} %copy-done.7) | copy-start | bytes 49156
  95.2 8.9 %collective-permute-start.1 = (bf16[32,3584]{1,0:T(8,128)(2,1)S(1)}, bf16[32,3584]{1,0:T(8,128)(2,1)S(1)}, u32[]{:S(2)}, u32[]{:S(2)}) collective-permute-start(bf16[32,3584]{1,0:T(8,128)(2,1)S(1)} %shard_map.102), channel_id=1, source_target_pairs={{8,0},{16,8},{24,16},{32,24},{40,32},{48,40},{56,48},{64,56},{72,6... | collective-permute-start | bytes 688136 | tf_op jit(solution)/shard_map/ppermute | solution.py:388

commit v10 on v7

--- a/solution.py
+++ b/solution.py
@@ -178,20 +178,9 @@
     mine = mine_ref[:, : TOK + EXTRA].astype(F32).astype(BF)
     mine = dot(mine, jnp.full((8, 128), 0.125, BF), 0, 0)
     member = ((iota((TOK + EXTRA, 128), 1) >> 1) & 7).astype(F32) == mine
-    fold = jnp.where(rank_rows(), 1.0, 0.0)
-    rows = jnp.concatenate(
-        [
-            lax.dot_general(
-                fold,
-                jnp.where(member, part, 0.0),
-                (((1,), (1,)), ((), ())),
-                preferred_element_type=F32,
-                precision=lax.Precision.HIGHEST,
-            )
-            for part in (up, down)
-        ],
-        axis=0,
-    )
+    fold = one_hot(rank_rows())
+    rows = [dot(fold, jnp.where(member, part, 0.0).astype(BF), 1, 1) for part in (up, down)]
+    rows = jnp.concatenate(rows, axis=0)
     block = rows.astype(BF)
     tail = rows[:, TOK:]
     tail = jnp.concatenate([tail[i * 8 : i * 8 + 8, :] for i in range(4)], axis=1).astype(BF)
@@ -221,23 +210,30 @@
     return jnp.where(own, rows, 0.0).astype(BF), jnp.where(extra, tail, 0.0).astype(BF)
 
 
-def sum_kernel(grad_ref, sig_ref, hid_ref, extra_ref, mine_ref, out_ref):
+def sum_kernel(grad_ref, sig_ref, hid_ref, extra_ref, mine_ref, out_hbm, out_ref, sems):
     up = jnp.concatenate(spread_signal(sig_ref, mine_ref, 0), axis=1)
     down = jnp.concatenate(spread_signal(sig_ref, mine_ref, RANK), axis=1)
+    copies = []
     for q in range(4):
         lanes = slice(q * QH, (q + 1) * QH)
         tokens = jnp.concatenate([hid_ref[:, lanes], extra_ref[:, lanes]], axis=0)
         sums = dot(up, tokens)
+        rows = slice(q * 16, q * 16 + 16)
         for rp in range(8):
-            at = (rp * 4 + q) * 16
-            out_ref[at : at + 16, :QH] = sums[rp * 16 : rp * 16 + 16, :].astype(BF)
+            out_ref[rp, rows, :QH] = sums[rp * 16 : rp * 16 + 16, :].astype(BF)
         lanes = slice(q * QF, (q + 1) * QF)
         behind = slice(HID + q * QF, HID + (q + 1) * QF)
         tokens = jnp.concatenate([grad_ref[:, lanes], extra_ref[:, behind]], axis=0)
         sums = dot(down, tokens)
         for rp in range(8):
-            at = (rp * 4 + q) * 16
-            out_ref[at : at + 16, QH:] = sums[rp * 16 : rp * 16 + 16, :].astype(BF)
+            out_ref[rp, rows, QH:] = sums[rp * 16 : rp * 16 + 16, :].astype(BF)
+        rows = pl.ds(q * 16, 16)
+        copies.append(
+            pltpu.make_async_copy(out_ref.at[:, rows, :], out_hbm.at[:, rows, :], sems.at[q])
+        )
+        copies[-1].start()
+    for copy in copies:
+        copy.wait()
 
 
 def extra_kernel(sig_ref, in_ref, mine_ref, out_ref):
@@ -269,14 +265,11 @@
         copy.wait()
 
 
-def reduce_kernel(hits_ref, in_ref, out_hbm, out_ref, sems):
-    def value(lanes):
-        sums = dot(hits_ref[:256, :], in_ref[:, lanes])
-        if lanes.start < HI:
-            sums += dot(hits_ref[256:, :], in_ref[:, LO + lanes.start : LO + lanes.stop])
-        return sums
-
-    store_parts(value, out_ref, out_hbm, sems, 0)
+def reduce_kernel(after_hbm, hits_ref, in_ref, out_ref):
+    low = dot(hits_ref[:256, :], in_ref[:, :LO])
+    high = dot(hits_ref[256:, :], in_ref[:, LO:])
+    out_ref[:, :HI] = (low[:, :HI] + high).astype(BF)
+    out_ref[:, HI:] = low[:, HI:].astype(BF)
 
 
 def join_kernel(
@@ -390,7 +383,16 @@
     tokens = (hidden, extra, mine)
     (partial,) = call(score_kernel, [((TP * SIG, 128), BF)], [], output_gradient, local, *tokens)
     signals = exchange(partial, "tensor", TP)
-    (sums,) = call(sum_kernel, [block], [], output_gradient, signals, *tokens)
+    (sums,) = call(
+        sum_kernel,
+        [((8, 64, ROW), BF)],
+        [pltpu.VMEM((8, 64, ROW), BF), pltpu.SemaphoreType.DMA((4,))],
+        output_gradient,
+        signals,
+        *tokens,
+        hbm_out=1,
+    )
+    sums = sums.reshape(512, ROW)
     gathered = exchange(sums, "dp", DP)
     (extra_gradient,) = call(extra_kernel, [((EXTRA, HID), BF)], [], signals, local, mine)
     back = lax.ppermute(extra_gradient, "dp", backward)
@@ -403,14 +405,7 @@
         mine,
         hbm_out=1,
     )
-    (slot_sums,) = call(
-        reduce_kernel,
-        [((256, LO), BF)],
-        [pltpu.VMEM((256, LO), BF), pltpu.SemaphoreType.DMA((3,))],
-        reduce_hits,
-        gathered,
-        hbm_out=1,
-    )
+    (slot_sums,) = call(reduce_kernel, [((256, LO), BF)], [], back, reduce_hits, gathered, any_in=1)
     owned = exchange(slot_sums, "dp", DP)
     hidden_gradient, down_gradient, up_gradient = call(
         join_kernel,

time: 106 us -> 110 us (1.038)
  blocking collectives: 41 us -> 16.7 us
  waiting for transfers between devices: 24.9 us -> 43.3 us
  starting transfers between devices: 22.1 us -> 29.4 us
  local copies, waits for them, and re-layouts: 4.47 us -> 6.4 us
    all_to_all x2 -> x1, blocking collectives: 41 us -> 16.7 us  [exchange(): return lax.all_to_all(block, axis, 0, 0, tiled=True).reshape(x.shape)]
    ppermute x1, waiting for transfers between devices: 4.98 us -> 14.9 us  [on_device(): back = lax.ppermute(extra_gradient, 'dp', backward)]
    all_to_all x3 -> x4, waiting for transfers between devices: 19.9 us -> 28.5 us  [exchange(): return lax.all_to_all(block, axis, 0, 0, tiled=True).reshape(x.shape)]
    all_to_all x3 -> x4, starting transfers between devices: 16.4 us -> 23.8 us  [exchange(): return lax.all_to_all(block, axis, 0, 0, tiled=True).reshape(x.shape)]
    unnamed x28 -> x34, local copies, waits for them, and re-layouts: 4.46 us -> 6.39 us
  transfers between devices with their start and end apart: 5 -> 6, of which waited for: 4 -> 5; matrix products, arithmetic and copies ran while one was open for 1% -> 1% of each run, Pallas kernels for 3% -> 3%
where the time goes in v10:
time: 110 us
  waiting for transfers between devices  43.3 us (39%)
  starting transfers between devices  29.4 us (27%)
  blocking collectives  16.7 us (15%)
  Pallas kernels  12.2 us (11%)
  local copies, waits for them, and re-layouts  6.4 us (6%)
    all_to_all x4, waiting for transfers between devices, exchange(): return lax.all_to_all(block, axis, 0, 0, tiled=True).reshape(x.shape)  28.5 us
    all_to_all x4, starting transfers between devices, exchange(): return lax.all_to_all(block, axis, 0, 0, tiled=True).reshape(x.shape)  23.8 us
    all_to_all x1, blocking collectives, exchange(): return lax.all_to_all(block, axis, 0, 0, tiled=True).reshape(x.shape)  16.7 us
    ppermute x1, waiting for transfers between devices, on_device(): back = lax.ppermute(extra_gradient, 'dp', backward)  14.9 us
    pallas_call x10, Pallas kernels, call(): pl.pallas_call(kernel, out_shape=[jax.ShapeDtypeStruct(s, t) for s, t in...  12.2 us
    unnamed x34, local copies, waits for them, and re-layouts  6.39 us
    ppermute x1, starting transfers between devices, on_device(): extra = lax.ppermute(last, 'dp', onward)  3.51 us
  transfers between devices with their start and end apart: 6, of which 5 were waited for; matrix products, arithmetic and copies ran while one was open for 1% of the time, Pallas kernels for 3%

profile of v10, /device:TPU:1, one launch (start us, length us, event | category | flops | bytes accessed | tf_op | source)
XLA Modules:
  0.0 109.6 jit_solution(1672238366263645179)
XLA Ops:
  0.7 1.9 %shard_map.95 = bf16[256,640]{1,0:T(8,128)(2,1)} custom-call(bf16[32,3584]{1,0:T(8,128)(2,1)} %bitcast.28, bf16[32,1024]{1,0:T(8,128)(2,1)} %bitcast.29), custom_call_target="tpu_custom_call" | custom-call | tf_op jit(solution)/shard_map/pallas_call | solution.py:321
  2.6 8.6 %all-to-all-start = ((bf16[32,8,640]{2,1,0:T(8,128)(2,1)}), bf16[32,8,640]{2,1,0:T(8,128)(2,1)S(1)}, u32[]{:S(2)}, u32[]{:S(2)}) async-start(bf16[32,8,640]{2,1,0:T(8,128)(2,1)} %bitcast.27), calls=%async_computation | async-start | bytes 655360 | tf_op jit(solution)/shard_map/all_to_all | solution.py:336
  11.2 1.4 %shard_map.94 = (bf16[1024,256]{1,0:T(8,128)(2,1)S(1)}, bf16[512,512]{1,0:T(8,128)(2,1)S(1)}, bf16[256,256]{1,0:T(8,128)(2,1)S(1)}, s32[8,384]{1,0:T(8,128)S(1)}, f32[32,128]{1,0:T(8,128)S(1)}) custom-call(s32[1]{0:T(128)} %bitcast.dp_ref, s32[64]{0:T(128)S(1)} %copy-done.14, s32[64]{0:T(128)S(1)} %copy-done.15, s32[64]{0:T(128)S(1)} %copy-done.16), custom_call_target="tpu_custom_call" | custom-call | tf_op jit(solution)/shard_map/pallas_call | solution.py:321
  12.7 0.8 copy-done.6
  13.4 0.7 copy-done.8
  14.1 0.6 copy-done.10
  14.7 0.6 copy-done.12
  15.3 5.5 %all-to-all-done = bf16[32,8,640]{2,1,0:T(8,128)(2,1)S(1)} async-done(((bf16[32,8,640]{2,1,0:T(8,128)(2,1)}), bf16[32,8,640]{2,1,0:T(8,128)(2,1)S(1)}, u32[]{:S(2)}, u32[]{:S(2)}) %all-to-all-start) | async-done | bytes 327712 | tf_op jit(solution)/shard_map/all_to_all | solution.py:336
  20.8 1.5 %shard_map.96 = bf16[512,1152]{1,0:T(8,128)(2,1)} custom-call(bf16[1024,256]{1,0:T(8,128)(2,1)S(1)} %get-tuple-element.13.hits_ref, bf16[256,640]{1,0:T(8,128)(2,1)S(1)} %bitcast.24), custom_call_target="tpu_custom_call" | custom-call | tf_op jit(solution)/shard_map/pallas_call | solution.py:321
  22.4 3.9 %all-to-all-start.1 = ((bf16[32,16,1152]{2,1,0:T(8,128)(2,1)}), bf16[32,16,1152]{2,1,0:T(8,128)(2,1)S(1)}, u32[]{:S(2)}, u32[]{:S(2)}) async-start(bf16[32,16,1152]{2,1,0:T(8,128)(2,1)} %bitcast.5), calls=%async_computation.1 | async-start | bytes 2359296 | tf_op jit(solution)/shard_map/all_to_all | solution.py:336
  26.2 0.0 copy-start
  26.3 0.7 pad_maximum_fusion
  27.0 3.5 %collective-permute-start = (bf16[32,4608]{1,0:T(8,128)(2,1)}, bf16[32,4608]{1,0:T(8,128)(2,1)S(1)}, u32[]{:S(2)}, u32[]{:S(2)}) collective-permute-start(bf16[32,4608]{1,0:T(8,128)(2,1)} %pad_maximum_fusion), channel_id=1, source_target_pairs={{0,8},{8,16},{16,24},{24,32},{32,40},{40,48},{48,56},{56,64},{64,7... | collective-permute-start | bytes 884744 | tf_op jit(solution)/shard_map/ppermute | solution.py:344
  30.5 14.1 %all-to-all-done.1 = bf16[32,16,1152]{2,1,0:T(8,128)(2,1)S(1)} async-done(((bf16[32,16,1152]{2,1,0:T(8,128)(2,1)}), bf16[32,16,1152]{2,1,0:T(8,128)(2,1)S(1)}, u32[]{:S(2)}, u32[]{:S(2)}) %all-to-all-start.1) | async-done | bytes 1179680 | tf_op jit(solution)/shard_map/all_to_all | solution.py:336
  44.7 1.0 copy-done.1
  45.7 0.7 copy-done.13
  46.4 0.0 copy-start.4
  46.4 1.1 shard_map.98
  47.5 16.7 %all_to_all.25 = bf16[8,72,128]{2,1,0:T(8,128)(2,1)S(1)} all-to-all(bf16[8,72,128]{2,1,0:T(8,128)(2,1)S(1)} %bitcast.26), channel_id=1, replica_groups=mesh['dp'=32,'tensor'=8] {'tensor'}, dimensions={0} | all-to-all | bytes 294912 | tf_op jit(solution)/shard_map/all_to_all | solution.py:336
  64.2 1.0 copy-done.5
  65.2 1.7 %shard_map.101 = bf16[8,64,1152]{2,1,0:T(8,128)(2,1)S(1)} custom-call(bf16[256,1024]{1,0:T(8,128)(2,1)S(1)} %copy-done.2, bf16[576,128]{1,0:T(8,128)(2,1)S(1)} %bitcast.21, bf16[256,3584]{1,0:T(8,128)(2,1)S(1)} %copy-done, bf16[32,4608]{1,0:T(8,128)(2,1)S(1)} %copy-done.5, s32[8,384]{1,0:T(8,128)S(1)} %shard_map.97.mine_ref), custom_call_target="tpu_custom_call" | custom-call | tf_op jit(solution)/shard_map/pallas_call | solution.py:321
  66.8 1.0 copy-done.3
  67.9 5.5 %all-to-all-start.3 = ((bf16[32,16,1152]{2,1,0:T(8,128)(2,1)}), bf16[32,16,1152]{2,1,0:T(8,128)(2,1)S(1)}, u32[]{:S(2)}, u32[]{:S(2)}) async-start(bf16[32,16,1152]{2,1,0:T(8,128)(2,1)} %bitcast.19), calls=%async_computation.3 | async-start | bytes 2359296 | tf_op jit(solution)/shard_map/all_to_all | solution.py:336
  73.3 0.5 shard_map.100
  73.8 2.1 %collective-permute-start.1 = (bf16[32,3584]{1,0:T(8,128)(2,1)S(1)}, bf16[32,3584]{1,0:T(8,128)(2,1)S(1)}, u32[]{:S(2)}, u32[]{:S(2)}) collective-permute-start(bf16[32,3584]{1,0:T(8,128)(2,1)S(1)} %shard_map.100), channel_id=1, source_target_pairs={{8,0},{16,8},{24,16},{32,24},{40,32},{48,40},{56,48},{64,56},{72,6... | collective-permute-start | bytes 688136 | tf_op jit(solution)/shard_map/ppermute | solution.py:398
  76.0 14.9 %collective-permute-done.1.after_hbm.back_ref = bf16[32,3584]{1,0:T(8,128)(2,1)S(1)} collective-permute-done((bf16[32,3584]{1,0:T(8,128)(2,1)S(1)}, bf16[32,3584]{1,0:T(8,128)(2,1)S(1)}, u32[]{:S(2)}, u32[]{:S(2)}) %collective-permute-start.1) | collective-permute-done | bytes 229408 | tf_op jit(solution)/shard_map/ppermute | solution.py:398
  90.8 0.8 all-to-all-done.3
  91.7 1.2 %shard_map.102 = bf16[256,640]{1,0:T(8,128)(2,1)} custom-call(bf16[32,3584]{1,0:T(8,128)(2,1)S(1)} %collective-permute-done.1.after_hbm.back_ref, bf16[512,512]{1,0:T(8,128)(2,1)S(1)} %copy-done.7, bf16[512,1152]{1,0:T(8,128)(2,1)S(1)} %bitcast.20), custom_call_target="tpu_custom_call" | custom-call | tf_op jit(solution)/shard_map/pallas_call | solution.py:321
  92.9 5.9 %all-to-all-start.4 = ((bf16[32,8,640]{2,1,0:T(8,128)(2,1)}), bf16[32,8,640]{2,1,0:T(8,128)(2,1)S(1)}, u32[]{:S(2)}, u32[]{:S(2)}) async-start(bf16[32,8,640]{2,1,0:T(8,128)(2,1)} %bitcast.11), calls=%async_computation.4 | async-start | bytes 655360 | tf_op jit(solution)/shard_map/all_to_all | solution.py:336
  98.8 1.7 %shard_map.99 = (bf16[256,3584]{1,0:T(8,128)(2,1)}, bf16[32,3584]{1,0:T(8,128)(2,1)S(1)}) custom-call(bf16[576,128]{1,0:T(8,128)(2,1)S(1)} %bitcast.23, bf16[512,1152]{1,0:T(8,128)(2,1)S(1)} %bitcast.18, s32[8,384]{1,0:T(8,128)S(1)} %shard_map.97.mine_ref), custom_call_target="tpu_custom_call" | custom-call | tf_op jit(solution)/shard_map/pallas_call | solution.py:321
  100.5 7.9 %all-to-all-done.4 = bf16[32,8,640]{2,1,0:T(8,128)(2,1)S(1)} async-done(((bf16[32,8,640]{2,1,0:T(8,128)(2,1)}), bf16[32,8,640]{2,1,0:T(8,128)(2,1)S(1)}, u32[]{:S(2)}, u32[]{:S(2)}) %all-to-all-start.4) | async-done | bytes 327712 | tf_op jit(solution)/shard_map/all_to_all | solution.py:336
  108.4 1.2 %shard_map.103 = (bf16[256,3584]{1,0:T(8,128)(2,1)}, f32[32,3584]{1,0:T(8,128)}, f32[32,1024]{1,0:T(8,128)}) custom-call(bf16[256,3584]{1,0:T(8,128)(2,1)} %get-tuple-element.15.head_hbm, f32[32,128]{1,0:T(8,128)S(1)} %copy-done.11, bf16[256,256]{1,0:T(8,128)(2,1)S(1)} %copy-done.9, bf16[256,640]{1,0:T(8,128)(2,1)S(1)} %bitcast.25, ...), custom_call_target="tpu_custom_call", output_to_operand_aliasing={{0}: (0, {})} | custom-call | tf_op jit(solution)/shard_map/pallas_call | solution.py:321
  (30 shorter events, 0.1 us)
Async XLA Ops:
  0.6 10.6 %copy-start.16 = (s32[64]{0:T(128)S(1)}, s32[64]{0:T(128)}, u32[]{:S(2)}) copy-start(s32[64]{0:T(128)} %slot_ref.1) | copy-start | bytes 772
  0.6 10.6 %copy-start.14 = (s32[64]{0:T(128)S(1)}, s32[64]{0:T(128)}, u32[]{:S(2)}) copy-start(s32[64]{0:T(128)} %off_ref.1) | copy-start | bytes 772
  0.7 10.6 %copy-start.15 = (s32[64]{0:T(128)S(1)}, s32[64]{0:T(128)}, u32[]{:S(2)}) copy-start(s32[64]{0:T(128)} %cnt_ref.1) | copy-start | bytes 772
  2.6 18.2 %all-to-all-start = ((bf16[32,8,640]{2,1,0:T(8,128)(2,1)}), bf16[32,8,640]{2,1,0:T(8,128)(2,1)S(1)}, u32[]{:S(2)}, u32[]{:S(2)}) async-start(bf16[32,8,640]{2,1,0:T(8,128)(2,1)} %bitcast.27), calls=%async_computation | async-start | bytes 655360 | tf_op jit(solution)/shard_map/all_to_all | solution.py:336
  12.6 0.8 copy-start.6
  13.4 0.7 copy-start.8
  14.1 0.6 copy-start.10
  14.7 0.6 copy-start.12
  22.4 3.9 %slice-start = ((bf16[256,3584]{1,0:T(8,128)(2,1)}), bf16[32,3584]{1,0:T(8,128)(2,1)S(1)}, s32[]{:S(2)}) async-start(bf16[256,3584]{1,0:T(8,128)(2,1)} %hid_ref.3), calls=%async_computation.5 | async-start | bytes 458752 | tf_op jit(solution)/shard_map/slice | solution.py:343
  22.4 3.9 %slice-start.1 = ((bf16[256,1024]{1,0:T(8,128)(2,1)}), bf16[32,1024]{1,0:T(8,128)(2,1)S(1)}, s32[]{:S(2)}) async-start(bf16[256,1024]{1,0:T(8,128)(2,1)} %grad_ref.5), calls=%async_computation.6 | async-start | bytes 131072 | tf_op jit(solution)/shard_map/slice | solution.py:343
  22.4 22.3 %all-to-all-start.1 = ((bf16[32,16,1152]{2,1,0:T(8,128)(2,1)}), bf16[32,16,1152]{2,1,0:T(8,128)(2,1)S(1)}, u32[]{:S(2)}, u32[]{:S(2)}) async-start(bf16[32,16,1152]{2,1,0:T(8,128)(2,1)} %bitcast.5), calls=%async_computation.1 | async-start | bytes 2359296 | tf_op jit(solution)/shard_map/all_to_all | solution.py:336
  26.2 20.2 %copy-start = (bf16[256,3584]{1,0:T(8,128)(2,1)S(1)}, bf16[256,3584]{1,0:T(8,128)(2,1)}, u32[]{:S(2)}) copy-start(bf16[256,3584]{1,0:T(8,128)(2,1)} %hid_ref.3) | copy-start | bytes 5505028
  27.0 19.4 %collective-permute-start = (bf16[32,4608]{1,0:T(8,128)(2,1)}, bf16[32,4608]{1,0:T(8,128)(2,1)S(1)}, u32[]{:S(2)}, u32[]{:S(2)}) collective-permute-start(bf16[32,4608]{1,0:T(8,128)(2,1)} %pad_maximum_fusion), channel_id=1, source_target_pairs={{0,8},{8,16},{16,24},{24,32},{32,40},{40,48},{48,56},{56,64},{64,7... | collective-permute-start | bytes 884744 | tf_op jit(solution)/shard_map/ppermute | solution.py:344
  44.7 1.0 copy-start.1
  45.7 0.7 copy-start.13
  46.4 17.8 %copy-start.2 = (bf16[256,1024]{1,0:T(8,128)(2,1)S(1)}, bf16[256,1024]{1,0:T(8,128)(2,1)}, u32[]{:S(2)}) copy-start(bf16[256,1024]{1,0:T(8,128)(2,1)} %grad_ref.5) | copy-start | bytes 1572868
  46.4 1.1 copy-start.4
  64.2 1.0 copy-start.5
  66.8 1.0 copy-start.3
  67.9 23.8 %all-to-all-start.3 = ((bf16[32,16,1152]{2,1,0:T(8,128)(2,1)}), bf16[32,16,1152]{2,1,0:T(8,128)(2,1)S(1)}, u32[]{:S(2)}, u32[]{:S(2)}) async-start(bf16[32,16,1152]{2,1,0:T(8,128)(2,1)} %bitcast.19), calls=%async_computation.3 | async-start | bytes 2359296 | tf_op jit(solution)/shard_map/all_to_all | solution.py:336
  73.3 18.4 %copy-start.7 = (bf16[512,512]{1,0:T(8,128)(2,1)S(1)}, bf16[512,512]{1,0:T(8,128)(2,1)}, u32[]{:S(2)}) copy-start(bf16[512,512]{1,0:T(8,128)(2,1)} %copy-done.6) | copy-start | bytes 1572868
  73.8 17.0 %collective-permute-start.1 = (bf16[32,3584]{1,0:T(8,128)(2,1)S(1)}, bf16[32,3584]{1,0:T(8,128)(2,1)S(1)}, u32[]{:S(2)}, u32[]{:S(2)}) collective-permute-start(bf16[32,3584]{1,0:T(8,128)(2,1)S(1)} %shard_map.100), channel_id=1, source_target_pairs={{8,0},{16,8},{24,16},{32,24},{40,32},{48,40},{56,48},{64,56},{72,6... | collective-permute-start | bytes 688136 | tf_op jit(solution)/shard_map/ppermute | solution.py:398
  92.9 15.5 %copy-start.9 = (bf16[256,256]{1,0:T(8,128)(2,1)S(1)}, bf16[256,256]{1,0:T(8,128)(2,1)}, u32[]{:S(2)}) copy-start(bf16[256,256]{1,0:T(8,128)(2,1)} %copy-done.8) | copy-start | bytes 393220
  92.9 15.5 %copy-start.11 = (f32[32,128]{1,0:T(8,128)S(1)}, f32[32,128]{1,0:T(8,128)}, u32[]{:S(2)}) copy-start(f32[32,128]{1,0:T(8,128)} %copy-done.10) | copy-start | bytes 49156
  92.9 15.5 %all-to-all-start.4 = ((bf16[32,8,640]{2,1,0:T(8,128)(2,1)}), bf16[32,8,640]{2,1,0:T(8,128)(2,1)S(1)}, u32[]{:S(2)}, u32[]{:S(2)}) async-start(bf16[32,8,640]{2,1,0:T(8,128)(2,1)} %bitcast.11), calls=%async_computation.4 | async-start | bytes 655360 | tf_op jit(solution)/shard_map/all_to_all | solution.py:336

commit v11 on v7

--- a/solution.py
+++ b/solution.py
@@ -134,7 +134,16 @@
             )
         )
     parts = jnp.concatenate(parts, axis=0)
-    store_parts(lambda lanes: dot(order, parts[:, lanes]), out_ref, out_hbm, sems, 2)
+    for half in range(2):
+        rows = slice(half * 128, half * 128 + 128)
+        out_ref[rows, :] = dot(order[rows, :], parts).astype(BF)
+        rows = pl.ds(half * 128, 128)
+        copies.append(
+            pltpu.make_async_copy(out_ref.at[rows, :], out_hbm.at[rows, :], sems.at[2 + half])
+        )
+        copies[-1].start()
+    for copy in copies[2:]:
+        copy.wait()
 
 
 def pick_kernel(hits_ref, in_ref, out_ref):
@@ -165,33 +174,17 @@
 
 
 def score_kernel(grad_ref, in_ref, hid_ref, extra_ref, mine_ref, out_ref):
-    up = jnp.zeros((TOK + EXTRA, 128), F32)
-    down = jnp.zeros((TOK + EXTRA, 128), F32)
-    for q in range(4):
-        lanes = slice(q * QH, (q + 1) * QH)
-        tokens = jnp.concatenate([hid_ref[:, lanes], extra_ref[:, lanes]], axis=0)
-        down += dot(tokens, quarter(in_ref, q, slice(0, QH)), 1, 1)
-        lanes = slice(q * QF, (q + 1) * QF)
-        behind = slice(HID + q * QF, HID + (q + 1) * QF)
-        tokens = jnp.concatenate([grad_ref[:, lanes], extra_ref[:, behind]], axis=0)
-        up += dot(tokens, quarter(in_ref, q, slice(QH, ROW)), 1, 1)
+    quarters = [quarter(in_ref, q, slice(0, ROW)) for q in range(4)]
+    tokens = jnp.concatenate([hid_ref[...], extra_ref[:, :HID]], axis=0)
+    down = dot(tokens, jnp.concatenate([m[:, :QH] for m in quarters], axis=1), 1, 1)
+    tokens = jnp.concatenate([grad_ref[...], extra_ref[:, HID:]], axis=0)
+    up = dot(tokens, jnp.concatenate([m[:, QH:] for m in quarters], axis=1), 1, 1)
     mine = mine_ref[:, : TOK + EXTRA].astype(F32).astype(BF)
     mine = dot(mine, jnp.full((8, 128), 0.125, BF), 0, 0)
     member = ((iota((TOK + EXTRA, 128), 1) >> 1) & 7).astype(F32) == mine
-    fold = jnp.where(rank_rows(), 1.0, 0.0)
-    rows = jnp.concatenate(
-        [
-            lax.dot_general(
-                fold,
-                jnp.where(member, part, 0.0),
-                (((1,), (1,)), ((), ())),
-                preferred_element_type=F32,
-                precision=lax.Precision.HIGHEST,
-            )
-            for part in (up, down)
-        ],
-        axis=0,
-    )
+    fold = one_hot(rank_rows())
+    rows = [dot(fold, jnp.where(member, part, 0.0).astype(BF), 1, 1) for part in (up, down)]
+    rows = jnp.concatenate(rows, axis=0)
     block = rows.astype(BF)
     tail = rows[:, TOK:]
     tail = jnp.concatenate([tail[i * 8 : i * 8 + 8, :] for i in range(4)], axis=1).astype(BF)
@@ -294,7 +287,7 @@
     rows_ref,
     sems,
 ):
-    rows_ref[...] = (tail_ref[...].astype(F32) + back_ref[...].astype(F32)).astype(BF)
+    rows_ref[...] = tail_ref[...] + back_ref[...]
     copies = [
         pltpu.make_async_copy(
             rows_ref, hidden_hbm.at[pl.ds(TOK - EXTRA, EXTRA), :], sems.at[8]

time: 106 us -> 106 us (level)
  no operation moved by 1% of the time
where the time goes in v11:
time: 106 us
  blocking collectives  41 us (39%)
  waiting for transfers between devices  24.9 us (23%)
  starting transfers between devices  22.1 us (21%)
  Pallas kernels  11.4 us (11%)
  local copies, waits for them, and re-layouts  4.47 us (4%)
    all_to_all x2, blocking collectives, exchange(): return lax.all_to_all(block, axis, 0, 0, tiled=True).reshape(x.shape)  41 us
    all_to_all x3, waiting for transfers between devices, exchange(): return lax.all_to_all(block, axis, 0, 0, tiled=True).reshape(x.shape)  19.9 us
    all_to_all x3, starting transfers between devices, exchange(): return lax.all_to_all(block, axis, 0, 0, tiled=True).reshape(x.shape)  16.4 us
    pallas_call x10, Pallas kernels, call(): pl.pallas_call(kernel, out_shape=[jax.ShapeDtypeStruct(s, t) for s, t in...  11.4 us
    ppermute x1, waiting for transfers between devices, on_device(): back = lax.ppermute(extra_gradient, 'dp', backward)  4.98 us
    unnamed x28, local copies, waits for them, and re-layouts  4.46 us
    ppermute x1, starting transfers between devices, on_device(): extra = lax.ppermute(last, 'dp', onward)  3.51 us
    ppermute x1, starting transfers between devices, on_device(): back = lax.ppermute(extra_gradient, 'dp', backward)  2.26 us
  transfers between devices with their start and end apart: 5, of which 4 were waited for; matrix products, arithmetic and copies ran while one was open for 1% of the time, Pallas kernels for 3%

profile of v11, /device:TPU:1, one launch (start us, length us, event | category | flops | bytes accessed | tf_op | source)
XLA Modules:
  0.0 105.5 jit_solution(17921664013141735680)
XLA Ops:
  0.6 0.0 copy-start.13
  0.6 0.0 copy-start.11
  0.7 2.0 %shard_map.95 = bf16[256,640]{1,0:T(8,128)(2,1)} custom-call(bf16[32,3584]{1,0:T(8,128)(2,1)} %bitcast.28, bf16[32,1024]{1,0:T(8,128)(2,1)} %bitcast.29), custom_call_target="tpu_custom_call" | custom-call | tf_op jit(solution)/shard_map/pallas_call | solution.py:321
  2.6 8.6 %all-to-all-start = ((bf16[32,8,640]{2,1,0:T(8,128)(2,1)}), bf16[32,8,640]{2,1,0:T(8,128)(2,1)S(1)}, u32[]{:S(2)}, u32[]{:S(2)}) async-start(bf16[32,8,640]{2,1,0:T(8,128)(2,1)} %bitcast.27), calls=%async_computation | async-start | bytes 655360 | tf_op jit(solution)/shard_map/all_to_all | solution.py:336
  11.3 1.4 %shard_map.94 = (bf16[1024,256]{1,0:T(8,128)(2,1)S(1)}, bf16[512,512]{1,0:T(8,128)(2,1)S(1)}, bf16[256,256]{1,0:T(8,128)(2,1)S(1)}, s32[8,384]{1,0:T(8,128)S(1)}, f32[32,128]{1,0:T(8,128)S(1)}) custom-call(s32[1]{0:T(128)} %bitcast.dp_ref, s32[64]{0:T(128)S(1)} %copy-done.11, s32[64]{0:T(128)S(1)} %copy-done.12, s32[64]{0:T(128)S(1)} %copy-done.13), custom_call_target="tpu_custom_call" | custom-call | tf_op jit(solution)/shard_map/pallas_call | solution.py:321
  12.7 0.8 copy-done.3
  13.5 0.7 copy-done.5
  14.1 0.6 copy-done.7
  14.8 0.6 copy-done.9
  15.4 5.5 %all-to-all-done = bf16[32,8,640]{2,1,0:T(8,128)(2,1)S(1)} async-done(((bf16[32,8,640]{2,1,0:T(8,128)(2,1)}), bf16[32,8,640]{2,1,0:T(8,128)(2,1)S(1)}, u32[]{:S(2)}, u32[]{:S(2)}) %all-to-all-start) | async-done | bytes 327712 | tf_op jit(solution)/shard_map/all_to_all | solution.py:336
  20.9 1.5 %shard_map.96 = bf16[512,1152]{1,0:T(8,128)(2,1)} custom-call(bf16[1024,256]{1,0:T(8,128)(2,1)S(1)} %get-tuple-element.13.hits_ref, bf16[256,640]{1,0:T(8,128)(2,1)S(1)} %bitcast.24), custom_call_target="tpu_custom_call" | custom-call | tf_op jit(solution)/shard_map/pallas_call | solution.py:321
  22.4 3.9 %all-to-all-start.1 = ((bf16[32,16,1152]{2,1,0:T(8,128)(2,1)}), bf16[32,16,1152]{2,1,0:T(8,128)(2,1)S(1)}, u32[]{:S(2)}, u32[]{:S(2)}) async-start(bf16[32,16,1152]{2,1,0:T(8,128)(2,1)} %bitcast.5), calls=%async_computation.1 | async-start | bytes 2359296 | tf_op jit(solution)/shard_map/all_to_all | solution.py:336
  26.3 0.0 copy-start
  26.3 0.7 pad_maximum_fusion
  27.0 3.5 %collective-permute-start = (bf16[32,4608]{1,0:T(8,128)(2,1)}, bf16[32,4608]{1,0:T(8,128)(2,1)S(1)}, u32[]{:S(2)}, u32[]{:S(2)}) collective-permute-start(bf16[32,4608]{1,0:T(8,128)(2,1)} %pad_maximum_fusion), channel_id=1, source_target_pairs={{0,8},{8,16},{16,24},{24,32},{32,40},{40,48},{48,56},{56,64},{64,7... | collective-permute-start | bytes 884744 | tf_op jit(solution)/shard_map/ppermute | solution.py:344
  30.5 14.1 %all-to-all-done.1 = bf16[32,16,1152]{2,1,0:T(8,128)(2,1)S(1)} async-done(((bf16[32,16,1152]{2,1,0:T(8,128)(2,1)}), bf16[32,16,1152]{2,1,0:T(8,128)(2,1)S(1)}, u32[]{:S(2)}, u32[]{:S(2)}) %all-to-all-start.1) | async-done | bytes 1179680 | tf_op jit(solution)/shard_map/all_to_all | solution.py:336
  44.7 1.0 copy-done.1
  45.7 0.7 copy-done.10
  46.4 0.0 collective-permute-done.extra_ref
  46.4 1.1 %shard_map.98 = bf16[576,128]{1,0:T(8,128)(2,1)S(1)} custom-call(bf16[256,1024]{1,0:T(8,128)(2,1)S(1)} %copy-done.1, bf16[512,1152]{1,0:T(8,128)(2,1)S(1)} %bitcast.16, bf16[256,3584]{1,0:T(8,128)(2,1)S(1)} %copy-done, bf16[32,4608]{1,0:T(8,128)(2,1)S(1)} %collective-permute-done.extra_ref, s32[8,384]{1,0:T(8,128)S(1)} %shard_map.97.mine_ref), custom_call_target="tpu_custom_call" | custom-call | tf_op jit(solution)/shard_map/pallas_call | solution.py:321
  47.5 16.7 %all_to_all.25 = bf16[8,72,128]{2,1,0:T(8,128)(2,1)S(1)} all-to-all(bf16[8,72,128]{2,1,0:T(8,128)(2,1)S(1)} %bitcast.26), channel_id=1, replica_groups=mesh['dp'=32,'tensor'=8] {'tensor'}, dimensions={0} | all-to-all | bytes 294912 | tf_op jit(solution)/shard_map/all_to_all | solution.py:336
  64.2 1.0 shard_map.100
  65.2 24.3 %all_to_all.26 = bf16[32,16,1152]{2,1,0:T(8,128)(2,1)S(1)} all-to-all(bf16[32,16,1152]{2,1,0:T(8,128)(2,1)S(1)} %bitcast.19), channel_id=1, replica_groups=mesh['dp'=32,'tensor'=8] {'dp'}, dimensions={0} | all-to-all | bytes 2359296 | tf_op jit(solution)/shard_map/all_to_all | solution.py:336
  89.5 1.2 %shard_map.101 = bf16[256,640]{1,0:T(8,128)(2,1)} custom-call(bf16[512,512]{1,0:T(8,128)(2,1)S(1)} %copy-done.4, bf16[512,1152]{1,0:T(8,128)(2,1)S(1)} %bitcast.20), custom_call_target="tpu_custom_call" | custom-call | tf_op jit(solution)/shard_map/pallas_call | solution.py:321
  90.7 3.9 %all-to-all-start.4 = ((bf16[32,8,640]{2,1,0:T(8,128)(2,1)}), bf16[32,8,640]{2,1,0:T(8,128)(2,1)S(1)}, u32[]{:S(2)}, u32[]{:S(2)}) async-start(bf16[32,8,640]{2,1,0:T(8,128)(2,1)} %bitcast.11), calls=%async_computation.4 | async-start | bytes 655360 | tf_op jit(solution)/shard_map/all_to_all | solution.py:336
  94.7 0.0 copy-start.6
  94.7 0.5 shard_map.102
  95.2 2.3 %collective-permute-start.1 = (bf16[32,3584]{1,0:T(8,128)(2,1)S(1)}, bf16[32,3584]{1,0:T(8,128)(2,1)S(1)}, u32[]{:S(2)}, u32[]{:S(2)}) collective-permute-start(bf16[32,3584]{1,0:T(8,128)(2,1)S(1)} %shard_map.102), channel_id=1, source_target_pairs={{8,0},{16,8},{24,16},{32,24},{40,32},{48,40},{56,48},{64,56},{72,6... | collective-permute-start | bytes 688136 | tf_op jit(solution)/shard_map/ppermute | solution.py:389
  97.5 1.7 %shard_map.99 = (bf16[256,3584]{1,0:T(8,128)(2,1)}, bf16[32,3584]{1,0:T(8,128)(2,1)S(1)}) custom-call(bf16[576,128]{1,0:T(8,128)(2,1)S(1)} %bitcast.23, bf16[512,1152]{1,0:T(8,128)(2,1)S(1)} %bitcast.18, s32[8,384]{1,0:T(8,128)S(1)} %shard_map.97.mine_ref), custom_call_target="tpu_custom_call" | custom-call | tf_op jit(solution)/shard_map/pallas_call | solution.py:321
  99.1 5.0 %collective-permute-done.1.back_ref = bf16[32,3584]{1,0:T(8,128)(2,1)S(1)} collective-permute-done((bf16[32,3584]{1,0:T(8,128)(2,1)S(1)}, bf16[32,3584]{1,0:T(8,128)(2,1)S(1)}, u32[]{:S(2)}, u32[]{:S(2)}) %collective-permute-start.1) | collective-permute-done | bytes 229408 | tf_op jit(solution)/shard_map/ppermute | solution.py:389
  104.1 0.3 all-to-all-done.4
  104.4 1.1 %shard_map.103 = (bf16[256,3584]{1,0:T(8,128)(2,1)}, f32[32,3584]{1,0:T(8,128)}, f32[32,1024]{1,0:T(8,128)}) custom-call(bf16[256,3584]{1,0:T(8,128)(2,1)} %get-tuple-element.15.head_hbm, f32[32,128]{1,0:T(8,128)S(1)} %copy-done.8, bf16[256,256]{1,0:T(8,128)(2,1)S(1)} %copy-done.6, bf16[256,640]{1,0:T(8,128)(2,1)S(1)} %bitcast.25, ...), custom_call_target="tpu_custom_call", output_to_operand_aliasing={{0}: (0, {})} | custom-call | tf_op jit(solution)/shard_map/pallas_call | solution.py:321
  (23 shorter events, 0.0 us)
Async XLA Ops:
  0.6 10.6 %copy-start.13 = (s32[64]{0:T(128)S(1)}, s32[64]{0:T(128)}, u32[]{:S(2)}) copy-start(s32[64]{0:T(128)} %slot_ref.1) | copy-start | bytes 772
  0.6 10.6 %copy-start.11 = (s32[64]{0:T(128)S(1)}, s32[64]{0:T(128)}, u32[]{:S(2)}) copy-start(s32[64]{0:T(128)} %off_ref.1) | copy-start | bytes 772
  0.7 10.6 %copy-start.12 = (s32[64]{0:T(128)S(1)}, s32[64]{0:T(128)}, u32[]{:S(2)}) copy-start(s32[64]{0:T(128)} %cnt_ref.1) | copy-start | bytes 772
  2.6 18.2 %all-to-all-start = ((bf16[32,8,640]{2,1,0:T(8,128)(2,1)}), bf16[32,8,640]{2,1,0:T(8,128)(2,1)S(1)}, u32[]{:S(2)}, u32[]{:S(2)}) async-start(bf16[32,8,640]{2,1,0:T(8,128)(2,1)} %bitcast.27), calls=%async_computation | async-start | bytes 655360 | tf_op jit(solution)/shard_map/all_to_all | solution.py:336
  12.7 0.8 copy-start.3
  13.5 0.7 copy-start.5
  14.1 0.6 copy-start.7
  14.7 0.6 copy-start.9
  22.4 3.9 %slice-start = ((bf16[256,3584]{1,0:T(8,128)(2,1)}), bf16[32,3584]{1,0:T(8,128)(2,1)S(1)}, s32[]{:S(2)}) async-start(bf16[256,3584]{1,0:T(8,128)(2,1)} %hid_ref.3), calls=%async_computation.5 | async-start | bytes 458752 | tf_op jit(solution)/shard_map/slice | solution.py:343
  22.4 3.9 %slice-start.1 = ((bf16[256,1024]{1,0:T(8,128)(2,1)}), bf16[32,1024]{1,0:T(8,128)(2,1)S(1)}, s32[]{:S(2)}) async-start(bf16[256,1024]{1,0:T(8,128)(2,1)} %grad_ref.5), calls=%async_computation.6 | async-start | bytes 131072 | tf_op jit(solution)/shard_map/slice | solution.py:343
  22.4 22.3 %all-to-all-start.1 = ((bf16[32,16,1152]{2,1,0:T(8,128)(2,1)}), bf16[32,16,1152]{2,1,0:T(8,128)(2,1)S(1)}, u32[]{:S(2)}, u32[]{:S(2)}) async-start(bf16[32,16,1152]{2,1,0:T(8,128)(2,1)} %bitcast.5), calls=%async_computation.1 | async-start | bytes 2359296 | tf_op jit(solution)/shard_map/all_to_all | solution.py:336
  26.3 20.2 %copy-start = (bf16[256,3584]{1,0:T(8,128)(2,1)S(1)}, bf16[256,3584]{1,0:T(8,128)(2,1)}, u32[]{:S(2)}) copy-start(bf16[256,3584]{1,0:T(8,128)(2,1)} %hid_ref.3) | copy-start | bytes 5505028
  27.0 19.4 %collective-permute-start = (bf16[32,4608]{1,0:T(8,128)(2,1)}, bf16[32,4608]{1,0:T(8,128)(2,1)S(1)}, u32[]{:S(2)}, u32[]{:S(2)}) collective-permute-start(bf16[32,4608]{1,0:T(8,128)(2,1)} %pad_maximum_fusion), channel_id=1, source_target_pairs={{0,8},{8,16},{16,24},{24,32},{32,40},{40,48},{48,56},{56,64},{64,7... | collective-permute-start | bytes 884744 | tf_op jit(solution)/shard_map/ppermute | solution.py:344
  44.7 1.0 copy-start.1
  45.7 0.7 copy-start.10
  46.4 17.8 %copy-start.2 = (bf16[256,1024]{1,0:T(8,128)(2,1)S(1)}, bf16[256,1024]{1,0:T(8,128)(2,1)}, u32[]{:S(2)}) copy-start(bf16[256,1024]{1,0:T(8,128)(2,1)} %grad_ref.5) | copy-start | bytes 1572868
  65.2 24.3 %copy-start.4 = (bf16[512,512]{1,0:T(8,128)(2,1)S(1)}, bf16[512,512]{1,0:T(8,128)(2,1)}, u32[]{:S(2)}) copy-start(bf16[512,512]{1,0:T(8,128)(2,1)} %copy-done.3) | copy-start | bytes 1572868
  90.7 13.7 %all-to-all-start.4 = ((bf16[32,8,640]{2,1,0:T(8,128)(2,1)}), bf16[32,8,640]{2,1,0:T(8,128)(2,1)S(1)}, u32[]{:S(2)}, u32[]{:S(2)}) async-start(bf16[32,8,640]{2,1,0:T(8,128)(2,1)} %bitcast.11), calls=%async_computation.4 | async-start | bytes 655360 | tf_op jit(solution)/shard_map/all_to_all | solution.py:336
  94.7 9.7 %copy-start.6 = (bf16[256,256]{1,0:T(8,128)(2,1)S(1)}, bf16[256,256]{1,0:T(8,128)(2,1)}, u32[]{:S(2)}) copy-start(bf16[256,256]{1,0:T(8,128)(2,1)} %copy-done.5) | copy-start | bytes 393220
  94.7 9.7 %copy-start.8 = (f32[32,128]{1,0:T(8,128)S(1)}, f32[32,128]{1,0:T(8,128)}, u32[]{:S(2)}) copy-start(f32[32,128]{1,0:T(8,128)} %copy-done.7) | copy-start | bytes 49156
  95.2 8.9 %collective-permute-start.1 = (bf16[32,3584]{1,0:T(8,128)(2,1)S(1)}, bf16[32,3584]{1,0:T(8,128)(2,1)S(1)}, u32[]{:S(2)}, u32[]{:S(2)}) collective-permute-start(bf16[32,3584]{1,0:T(8,128)(2,1)S(1)} %shard_map.102), channel_id=1, source_target_pairs={{8,0},{16,8},{24,16},{32,24},{40,32},{48,40},{56,48},{64,56},{72,6... | collective-permute-start | bytes 688136 | tf_op jit(solution)/shard_map/ppermute | solution.py:389

commit v12 on v7

--- a/solution.py
+++ b/solution.py
@@ -178,20 +178,9 @@
     mine = mine_ref[:, : TOK + EXTRA].astype(F32).astype(BF)
     mine = dot(mine, jnp.full((8, 128), 0.125, BF), 0, 0)
     member = ((iota((TOK + EXTRA, 128), 1) >> 1) & 7).astype(F32) == mine
-    fold = jnp.where(rank_rows(), 1.0, 0.0)
-    rows = jnp.concatenate(
-        [
-            lax.dot_general(
-                fold,
-                jnp.where(member, part, 0.0),
-                (((1,), (1,)), ((), ())),
-                preferred_element_type=F32,
-                precision=lax.Precision.HIGHEST,
-            )
-            for part in (up, down)
-        ],
-        axis=0,
-    )
+    fold = one_hot(rank_rows())
+    rows = [dot(fold, jnp.where(member, part, 0.0).astype(BF), 1, 1) for part in (up, down)]
+    rows = jnp.concatenate(rows, axis=0)
     block = rows.astype(BF)
     tail = rows[:, TOK:]
     tail = jnp.concatenate([tail[i * 8 : i * 8 + 8, :] for i in range(4)], axis=1).astype(BF)
@@ -294,7 +283,7 @@
     rows_ref,
     sems,
 ):
-    rows_ref[...] = (tail_ref[...].astype(F32) + back_ref[...].astype(F32)).astype(BF)
+    rows_ref[...] = tail_ref[...] + back_ref[...]
     copies = [
         pltpu.make_async_copy(
             rows_ref, hidden_hbm.at[pl.ds(TOK - EXTRA, EXTRA), :], sems.at[8]

time: 106 us -> 106 us (level)
  no operation moved by 1% of the time
where the time goes in v12:
time: 106 us
  blocking collectives  41 us (39%)
  waiting for transfers between devices  24.9 us (23%)
  starting transfers between devices  22.1 us (21%)
  Pallas kernels  11.4 us (11%)
  local copies, waits for them, and re-layouts  4.47 us (4%)
    all_to_all x2, blocking collectives, exchange(): return lax.all_to_all(block, axis, 0, 0, tiled=True).reshape(x.shape)  41 us
    all_to_all x3, waiting for transfers between devices, exchange(): return lax.all_to_all(block, axis, 0, 0, tiled=True).reshape(x.shape)  19.9 us
    all_to_all x3, starting transfers between devices, exchange(): return lax.all_to_all(block, axis, 0, 0, tiled=True).reshape(x.shape)  16.4 us
    pallas_call x10, Pallas kernels, call(): pl.pallas_call(kernel, out_shape=[jax.ShapeDtypeStruct(s, t) for s, t in...  11.4 us
    ppermute x1, waiting for transfers between devices, on_device(): back = lax.ppermute(extra_gradient, 'dp', backward)  4.98 us
    unnamed x28, local copies, waits for them, and re-layouts  4.46 us
    ppermute x1, starting transfers between devices, on_device(): extra = lax.ppermute(last, 'dp', onward)  3.51 us
    ppermute x1, starting transfers between devices, on_device(): back = lax.ppermute(extra_gradient, 'dp', backward)  2.26 us
  transfers between devices with their start and end apart: 5, of which 4 were waited for; matrix products, arithmetic and copies ran while one was open for 1% of the time, Pallas kernels for 3%

profile of v12, /device:TPU:1, one launch (start us, length us, event | category | flops | bytes accessed | tf_op | source)
XLA Modules:
  0.0 105.5 jit_solution(512525227045103321)
XLA Ops:
  0.6 0.0 copy-start.13
  0.6 0.0 copy-start.11
  0.7 1.9 %shard_map.95 = bf16[256,640]{1,0:T(8,128)(2,1)} custom-call(bf16[32,3584]{1,0:T(8,128)(2,1)} %bitcast.28, bf16[32,1024]{1,0:T(8,128)(2,1)} %bitcast.29), custom_call_target="tpu_custom_call" | custom-call | tf_op jit(solution)/shard_map/pallas_call | solution.py:317
  2.6 8.6 %all-to-all-start = ((bf16[32,8,640]{2,1,0:T(8,128)(2,1)}), bf16[32,8,640]{2,1,0:T(8,128)(2,1)S(1)}, u32[]{:S(2)}, u32[]{:S(2)}) async-start(bf16[32,8,640]{2,1,0:T(8,128)(2,1)} %bitcast.27), calls=%async_computation | async-start | bytes 655360 | tf_op jit(solution)/shard_map/all_to_all | solution.py:332
  11.2 1.4 %shard_map.94 = (bf16[1024,256]{1,0:T(8,128)(2,1)S(1)}, bf16[512,512]{1,0:T(8,128)(2,1)S(1)}, bf16[256,256]{1,0:T(8,128)(2,1)S(1)}, s32[8,384]{1,0:T(8,128)S(1)}, f32[32,128]{1,0:T(8,128)S(1)}) custom-call(s32[1]{0:T(128)} %bitcast.dp_ref, s32[64]{0:T(128)S(1)} %copy-done.11, s32[64]{0:T(128)S(1)} %copy-done.12, s32[64]{0:T(128)S(1)} %copy-done.13), custom_call_target="tpu_custom_call" | custom-call | tf_op jit(solution)/shard_map/pallas_call | solution.py:317
  12.7 0.8 copy-done.3
  13.5 0.7 copy-done.5
  14.1 0.6 copy-done.7
  14.7 0.6 copy-done.9
  15.3 5.5 %all-to-all-done = bf16[32,8,640]{2,1,0:T(8,128)(2,1)S(1)} async-done(((bf16[32,8,640]{2,1,0:T(8,128)(2,1)}), bf16[32,8,640]{2,1,0:T(8,128)(2,1)S(1)}, u32[]{:S(2)}, u32[]{:S(2)}) %all-to-all-start) | async-done | bytes 327712 | tf_op jit(solution)/shard_map/all_to_all | solution.py:332
  20.8 1.5 %shard_map.96 = bf16[512,1152]{1,0:T(8,128)(2,1)} custom-call(bf16[1024,256]{1,0:T(8,128)(2,1)S(1)} %get-tuple-element.13.hits_ref, bf16[256,640]{1,0:T(8,128)(2,1)S(1)} %bitcast.24), custom_call_target="tpu_custom_call" | custom-call | tf_op jit(solution)/shard_map/pallas_call | solution.py:317
  22.4 3.9 %all-to-all-start.1 = ((bf16[32,16,1152]{2,1,0:T(8,128)(2,1)}), bf16[32,16,1152]{2,1,0:T(8,128)(2,1)S(1)}, u32[]{:S(2)}, u32[]{:S(2)}) async-start(bf16[32,16,1152]{2,1,0:T(8,128)(2,1)} %bitcast.5), calls=%async_computation.1 | async-start | bytes 2359296 | tf_op jit(solution)/shard_map/all_to_all | solution.py:332
  26.2 0.0 copy-start
  26.3 0.7 pad_maximum_fusion
  27.0 3.5 %collective-permute-start = (bf16[32,4608]{1,0:T(8,128)(2,1)}, bf16[32,4608]{1,0:T(8,128)(2,1)S(1)}, u32[]{:S(2)}, u32[]{:S(2)}) collective-permute-start(bf16[32,4608]{1,0:T(8,128)(2,1)} %pad_maximum_fusion), channel_id=1, source_target_pairs={{0,8},{8,16},{16,24},{24,32},{32,40},{40,48},{48,56},{56,64},{64,7... | collective-permute-start | bytes 884744 | tf_op jit(solution)/shard_map/ppermute | solution.py:340
  30.5 14.1 %all-to-all-done.1 = bf16[32,16,1152]{2,1,0:T(8,128)(2,1)S(1)} async-done(((bf16[32,16,1152]{2,1,0:T(8,128)(2,1)}), bf16[32,16,1152]{2,1,0:T(8,128)(2,1)S(1)}, u32[]{:S(2)}, u32[]{:S(2)}) %all-to-all-start.1) | async-done | bytes 1179680 | tf_op jit(solution)/shard_map/all_to_all | solution.py:332
  44.7 1.0 copy-done.1
  45.7 0.7 copy-done.10
  46.4 0.0 collective-permute-done.extra_ref
  46.4 1.1 %shard_map.98 = bf16[576,128]{1,0:T(8,128)(2,1)S(1)} custom-call(bf16[256,1024]{1,0:T(8,128)(2,1)S(1)} %copy-done.1, bf16[512,1152]{1,0:T(8,128)(2,1)S(1)} %bitcast.16, bf16[256,3584]{1,0:T(8,128)(2,1)S(1)} %copy-done, bf16[32,4608]{1,0:T(8,128)(2,1)S(1)} %collective-permute-done.extra_ref, s32[8,384]{1,0:T(8,128)S(1)} %shard_map.97.mine_ref), custom_call_target="tpu_custom_call" | custom-call | tf_op jit(solution)/shard_map/pallas_call | solution.py:317
  47.5 16.7 %all_to_all.25 = bf16[8,72,128]{2,1,0:T(8,128)(2,1)S(1)} all-to-all(bf16[8,72,128]{2,1,0:T(8,128)(2,1)S(1)} %bitcast.26), channel_id=1, replica_groups=mesh['dp'=32,'tensor'=8] {'tensor'}, dimensions={0} | all-to-all | bytes 294912 | tf_op jit(solution)/shard_map/all_to_all | solution.py:332
  64.2 1.0 shard_map.100
  65.2 24.3 %all_to_all.26 = bf16[32,16,1152]{2,1,0:T(8,128)(2,1)S(1)} all-to-all(bf16[32,16,1152]{2,1,0:T(8,128)(2,1)S(1)} %bitcast.19), channel_id=1, replica_groups=mesh['dp'=32,'tensor'=8] {'dp'}, dimensions={0} | all-to-all | bytes 2359296 | tf_op jit(solution)/shard_map/all_to_all | solution.py:332
  89.5 1.2 %shard_map.101 = bf16[256,640]{1,0:T(8,128)(2,1)} custom-call(bf16[512,512]{1,0:T(8,128)(2,1)S(1)} %copy-done.4, bf16[512,1152]{1,0:T(8,128)(2,1)S(1)} %bitcast.20), custom_call_target="tpu_custom_call" | custom-call | tf_op jit(solution)/shard_map/pallas_call | solution.py:317
  90.7 3.9 %all-to-all-start.4 = ((bf16[32,8,640]{2,1,0:T(8,128)(2,1)}), bf16[32,8,640]{2,1,0:T(8,128)(2,1)S(1)}, u32[]{:S(2)}, u32[]{:S(2)}) async-start(bf16[32,8,640]{2,1,0:T(8,128)(2,1)} %bitcast.11), calls=%async_computation.4 | async-start | bytes 655360 | tf_op jit(solution)/shard_map/all_to_all | solution.py:332
  94.7 0.0 copy-start.6
  94.7 0.5 shard_map.102
  95.2 2.3 %collective-permute-start.1 = (bf16[32,3584]{1,0:T(8,128)(2,1)S(1)}, bf16[32,3584]{1,0:T(8,128)(2,1)S(1)}, u32[]{:S(2)}, u32[]{:S(2)}) collective-permute-start(bf16[32,3584]{1,0:T(8,128)(2,1)S(1)} %shard_map.102), channel_id=1, source_target_pairs={{8,0},{16,8},{24,16},{32,24},{40,32},{48,40},{56,48},{64,56},{72,6... | collective-permute-start | bytes 688136 | tf_op jit(solution)/shard_map/ppermute | solution.py:385
  97.4 1.7 %shard_map.99 = (bf16[256,3584]{1,0:T(8,128)(2,1)}, bf16[32,3584]{1,0:T(8,128)(2,1)S(1)}) custom-call(bf16[576,128]{1,0:T(8,128)(2,1)S(1)} %bitcast.23, bf16[512,1152]{1,0:T(8,128)(2,1)S(1)} %bitcast.18, s32[8,384]{1,0:T(8,128)S(1)} %shard_map.97.mine_ref), custom_call_target="tpu_custom_call" | custom-call | tf_op jit(solution)/shard_map/pallas_call | solution.py:317
  99.1 5.0 %collective-permute-done.1.back_ref = bf16[32,3584]{1,0:T(8,128)(2,1)S(1)} collective-permute-done((bf16[32,3584]{1,0:T(8,128)(2,1)S(1)}, bf16[32,3584]{1,0:T(8,128)(2,1)S(1)}, u32[]{:S(2)}, u32[]{:S(2)}) %collective-permute-start.1) | collective-permute-done | bytes 229408 | tf_op jit(solution)/shard_map/ppermute | solution.py:385
  104.1 0.3 all-to-all-done.4
  104.4 1.1 %shard_map.103 = (bf16[256,3584]{1,0:T(8,128)(2,1)}, f32[32,3584]{1,0:T(8,128)}, f32[32,1024]{1,0:T(8,128)}) custom-call(bf16[256,3584]{1,0:T(8,128)(2,1)} %get-tuple-element.15.head_hbm, f32[32,128]{1,0:T(8,128)S(1)} %copy-done.8, bf16[256,256]{1,0:T(8,128)(2,1)S(1)} %copy-done.6, bf16[256,640]{1,0:T(8,128)(2,1)S(1)} %bitcast.25, ...), custom_call_target="tpu_custom_call", output_to_operand_aliasing={{0}: (0, {})} | custom-call | tf_op jit(solution)/shard_map/pallas_call | solution.py:317
  (23 shorter events, 0.0 us)
Async XLA Ops:
  0.6 10.6 %copy-start.13 = (s32[64]{0:T(128)S(1)}, s32[64]{0:T(128)}, u32[]{:S(2)}) copy-start(s32[64]{0:T(128)} %slot_ref.1) | copy-start | bytes 772
  0.6 10.6 %copy-start.11 = (s32[64]{0:T(128)S(1)}, s32[64]{0:T(128)}, u32[]{:S(2)}) copy-start(s32[64]{0:T(128)} %off_ref.1) | copy-start | bytes 772
  0.7 10.6 %copy-start.12 = (s32[64]{0:T(128)S(1)}, s32[64]{0:T(128)}, u32[]{:S(2)}) copy-start(s32[64]{0:T(128)} %cnt_ref.1) | copy-start | bytes 772
  2.6 18.2 %all-to-all-start = ((bf16[32,8,640]{2,1,0:T(8,128)(2,1)}), bf16[32,8,640]{2,1,0:T(8,128)(2,1)S(1)}, u32[]{:S(2)}, u32[]{:S(2)}) async-start(bf16[32,8,640]{2,1,0:T(8,128)(2,1)} %bitcast.27), calls=%async_computation | async-start | bytes 655360 | tf_op jit(solution)/shard_map/all_to_all | solution.py:332
  12.6 0.8 copy-start.3
  13.5 0.7 copy-start.5
  14.1 0.6 copy-start.7
  14.7 0.6 copy-start.9
  22.4 3.9 %slice-start = ((bf16[256,3584]{1,0:T(8,128)(2,1)}), bf16[32,3584]{1,0:T(8,128)(2,1)S(1)}, s32[]{:S(2)}) async-start(bf16[256,3584]{1,0:T(8,128)(2,1)} %hid_ref.3), calls=%async_computation.5 | async-start | bytes 458752 | tf_op jit(solution)/shard_map/slice | solution.py:339
  22.4 3.9 %slice-start.1 = ((bf16[256,1024]{1,0:T(8,128)(2,1)}), bf16[32,1024]{1,0:T(8,128)(2,1)S(1)}, s32[]{:S(2)}) async-start(bf16[256,1024]{1,0:T(8,128)(2,1)} %grad_ref.5), calls=%async_computation.6 | async-start | bytes 131072 | tf_op jit(solution)/shard_map/slice | solution.py:339
  22.4 22.3 %all-to-all-start.1 = ((bf16[32,16,1152]{2,1,0:T(8,128)(2,1)}), bf16[32,16,1152]{2,1,0:T(8,128)(2,1)S(1)}, u32[]{:S(2)}, u32[]{:S(2)}) async-start(bf16[32,16,1152]{2,1,0:T(8,128)(2,1)} %bitcast.5), calls=%async_computation.1 | async-start | bytes 2359296 | tf_op jit(solution)/shard_map/all_to_all | solution.py:332
  26.2 20.2 %copy-start = (bf16[256,3584]{1,0:T(8,128)(2,1)S(1)}, bf16[256,3584]{1,0:T(8,128)(2,1)}, u32[]{:S(2)}) copy-start(bf16[256,3584]{1,0:T(8,128)(2,1)} %hid_ref.3) | copy-start | bytes 5505028
  27.0 19.4 %collective-permute-start = (bf16[32,4608]{1,0:T(8,128)(2,1)}, bf16[32,4608]{1,0:T(8,128)(2,1)S(1)}, u32[]{:S(2)}, u32[]{:S(2)}) collective-permute-start(bf16[32,4608]{1,0:T(8,128)(2,1)} %pad_maximum_fusion), channel_id=1, source_target_pairs={{0,8},{8,16},{16,24},{24,32},{32,40},{40,48},{48,56},{56,64},{64,7... | collective-permute-start | bytes 884744 | tf_op jit(solution)/shard_map/ppermute | solution.py:340
  44.7 1.0 copy-start.1
  45.7 0.7 copy-start.10
  46.4 17.8 %copy-start.2 = (bf16[256,1024]{1,0:T(8,128)(2,1)S(1)}, bf16[256,1024]{1,0:T(8,128)(2,1)}, u32[]{:S(2)}) copy-start(bf16[256,1024]{1,0:T(8,128)(2,1)} %grad_ref.5) | copy-start | bytes 1572868
  65.2 24.3 %copy-start.4 = (bf16[512,512]{1,0:T(8,128)(2,1)S(1)}, bf16[512,512]{1,0:T(8,128)(2,1)}, u32[]{:S(2)}) copy-start(bf16[512,512]{1,0:T(8,128)(2,1)} %copy-done.3) | copy-start | bytes 1572868
  90.7 13.7 %all-to-all-start.4 = ((bf16[32,8,640]{2,1,0:T(8,128)(2,1)}), bf16[32,8,640]{2,1,0:T(8,128)(2,1)S(1)}, u32[]{:S(2)}, u32[]{:S(2)}) async-start(bf16[32,8,640]{2,1,0:T(8,128)(2,1)} %bitcast.11), calls=%async_computation.4 | async-start | bytes 655360 | tf_op jit(solution)/shard_map/all_to_all | solution.py:332
  94.7 9.7 %copy-start.6 = (bf16[256,256]{1,0:T(8,128)(2,1)S(1)}, bf16[256,256]{1,0:T(8,128)(2,1)}, u32[]{:S(2)}) copy-start(bf16[256,256]{1,0:T(8,128)(2,1)} %copy-done.5) | copy-start | bytes 393220
  94.7 9.7 %copy-start.8 = (f32[32,128]{1,0:T(8,128)S(1)}, f32[32,128]{1,0:T(8,128)}, u32[]{:S(2)}) copy-start(f32[32,128]{1,0:T(8,128)} %copy-done.7) | copy-start | bytes 49156
  95.2 8.9 %collective-permute-start.1 = (bf16[32,3584]{1,0:T(8,128)(2,1)S(1)}, bf16[32,3584]{1,0:T(8,128)(2,1)S(1)}, u32[]{:S(2)}, u32[]{:S(2)}) collective-permute-start(bf16[32,3584]{1,0:T(8,128)(2,1)S(1)} %shard_map.102), channel_id=1, source_target_pairs={{8,0},{16,8},{24,16},{32,24},{40,32},{48,40},{56,48},{64,56},{72,6... | collective-permute-start | bytes 688136 | tf_op jit(solution)/shard_map/ppermute | solution.py:385
